TPU v7x, 128 devices: a whole 4x4x4 slice. The times are simulated.
128 devices in a mesh: dp: 4 (over x), seq: 32 (over z, y, core).
Axes of the slice: x: 4, y: 4, z: 4, core: 2. Of those that a mesh axis runs over, the one named last changes fastest.
Arguments:
- conv_input: bfloat16 [16384, 5376], P(('dp', 'seq')), may hold values from -6 to 6
- doc_start: int32 [16384], P(('dp', 'seq')), may hold values 0 or 1
- conv_weight: float32 [4, 5376], replicated, may hold values from -3 to 3
- conv_bias: float32 [5376], replicated, may hold values from -0.5 to 0.5
- dt_raw: float32 [16384, 80], P(('dp', 'seq')), may hold values from -3 to 3
- dt_bias: float32 [80], replicated, may hold values from -5.5 to -4.2
- a_log: float32 [80], replicated, may hold values from -9 to 2, as said below
- skip_gain: float32 [80], replicated, may hold values from 0.5 to 1.5
- cotangent: bfloat16 [16384, 5120], P(('dp', 'seq')), may hold values from -6 to 6
Outputs:
- ssm_output: bfloat16 [16384, 5120], P(('dp', 'seq'))
- grad_input: bfloat16 [16384, 5376], P(('dp', 'seq'))
- grad_conv_weight: float32 [4, 5376], replicated
- grad_conv_bias: float32 [5376], replicated
- grad_dt_bias: float32 [80], replicated
- grad_a_log: float32 [80], replicated
- grad_skip_gain: float32 [80], replicated
Inputs may be any that keep to these rules, and one draw needn't show every extreme that they name: `doc_start`: 1 marks the first token of a document; documents may cross shard boundaries. One value per head; exp(a_log) lies between 25 / 4096 and 4.2, so that the per-token decay rates exp(a_log) * steps_dt run from under 1 / 4096 to about 1.1.
All inputs are finite; a program needn't handle non-finite values.
Results may differ from a plain program's by a relative error of at most 0.00115.
Values may be sent and summed in bfloat16 or wider, within the bound.
A program may use at most 320 MiB of HBM per device.

v0:
```python
import jax
import jax.numpy as jnp
from jax import lax
from jax.sharding import PartitionSpec as P

HEADS = 80
HEAD_DIM = 64
STATE = 128
CONV = 4
BLOCK = 64
INNER = 5120


exact_mode = lax.Precision.HIGHEST


def from_behind(array, axis, by):
    size = lax.axis_size(axis)
    pairs = [(i, i + by) for i in range(size) if 0 <= i + by < size]
    return lax.ppermute(array, axis, pairs)


def prefix(array, axis, combine, identity, reverse):
    size, place = (lax.axis_size(axis), lax.axis_index(axis))
    everything = jax.tree.map(lambda part: lax.all_gather(part, axis), array)
    start = jax.tree.map(
        lambda part, zero: jnp.broadcast_to(jnp.asarray(zero, part.dtype), part.shape),
        array,
        identity,
    )

    def step(k, before):
        at = size - 1 - k if reverse else k
        reached = at > place if reverse else at < place
        new = combine(before, jax.tree.map(lambda part: part[at], everything))
        return jax.tree.map(lambda a, b: jnp.where(reached, a, b), new, before)

    return lax.fori_loop(0, size, step, start)


def prepare_inputs(
    tail_rows, conv_input, doc_start, conv_weight, conv_bias, dt_raw, dt_bias, a_log
):
    row_count = conv_input.shape[0]
    extended = jnp.concatenate([tail_rows, conv_input], axis=0)
    resets = doc_start.astype(jnp.float32)
    segment = jnp.cumsum(resets)
    padded = jnp.concatenate([jnp.zeros((CONV - 1,), jnp.float32), segment])
    convolved = conv_bias[None, :] + conv_weight[CONV - 1][None, :] * extended[CONV - 1 :]
    for offset in range(1, CONV):
        first_row = CONV - 1 - offset
        tap_valid = (padded[first_row : first_row + row_count] == segment).astype(jnp.float32)
        convolved = (
            convolved
            + conv_weight[first_row][None, :]
            * extended[first_row : first_row + row_count]
            * tap_valid[:, None]
        )
    activated = jax.nn.silu(convolved)
    values_x = activated[:, :INNER].reshape(row_count, HEADS, HEAD_DIM)
    keys_b = activated[:, INNER : INNER + STATE]
    reads_c = activated[:, INNER + STATE :]
    steps_dt = jax.nn.softplus(dt_raw + dt_bias[None, :])
    log_decay = -jnp.exp(a_log)[None, :] * steps_dt
    return (values_x, keys_b, reads_c, steps_dt, log_decay)


def scan_block(carry, block_data):
    carry_state, skip_gain = carry
    values_x, keys_b, reads_c, steps_dt, log_decay, resets = block_data
    length = values_x.shape[0]
    segment = jnp.cumsum(resets)
    running = jnp.cumsum(log_decay, axis=0)
    positions = jnp.arange(length)
    causal = (positions[:, None] >= positions[None, :]) & (segment[:, None] == segment[None, :])
    spread_log = running.T[:, :, None] - running.T[:, None, :]
    within = jnp.where(causal[None], jnp.exp(jnp.where(causal[None], spread_log, 0.0)), 0.0)
    scores = jnp.dot(reads_c, keys_b.T, precision=exact_mode)
    weights = within * scores[None] * steps_dt.T[:, None, :]
    output = jnp.einsum("hts,shp->thp", weights, values_x, precision=exact_mode)
    untouched = (segment == 0).astype(running.dtype)
    entry_weight = jnp.exp(running) * untouched[:, None]
    output = (
        output
        + jnp.einsum("tn,hpn->thp", reads_c, carry_state, precision=exact_mode)
        * entry_weight[:, :, None]
    )
    output = output + skip_gain[None, :, None] * values_x
    last_segment = (segment == segment[length - 1]).astype(running.dtype)
    leave_weight = (
        jnp.exp(running[length - 1][None, :] - running) * last_segment[:, None] * steps_dt
    )
    through = jnp.exp(running[length - 1]) * untouched[length - 1]
    added = jnp.einsum(
        "shp,sn->hpn", leave_weight[:, :, None] * values_x, keys_b, precision=exact_mode
    )
    carry_state = carry_state * through[:, None, None] + added
    return ((carry_state, skip_gain), output)


def chain_blocks(values_x, keys_b, reads_c, steps_dt, log_decay, resets, skip_gain, start_state):
    row_count = values_x.shape[0]
    block_count = row_count // BLOCK
    pieces = tuple(
        (
            member.reshape((block_count, BLOCK) + member.shape[1:])
            for member in (values_x, keys_b, reads_c, steps_dt, log_decay, resets)
        )
    )
    stepper = jax.checkpoint(scan_block)
    (final_state, _), outputs = lax.scan(stepper, (start_state, skip_gain), pieces)
    return (outputs.reshape(row_count, INNER), final_state)


def join_states(earlier, later):
    return (earlier[0] * later[0], later[0][:, None, None] * earlier[1] + later[1])


def on_device(
    conv_input, doc_start, conv_weight, conv_bias, dt_raw, dt_bias, a_log, skip_gain, cotangent
):
    row_count = conv_input.shape[0]
    resets = doc_start.astype(jnp.float32)
    after = jnp.concatenate([1.0 - resets[row_count - CONV + 2 :], jnp.ones((1,), jnp.float32)])
    keep_rows = jnp.flip(jnp.cumprod(jnp.flip(after)))
    tail_out = conv_input[row_count - CONV + 1 :] * keep_rows[:, None].astype(jnp.bfloat16)
    tail_in = from_behind(tail_out, "seq", 1)

    def prepare_local(tail_rows, rows_value, weight_value, bias_value, dtb_value, alog_value):
        return prepare_inputs(
            tail_rows,
            rows_value,
            doc_start,
            weight_value,
            bias_value,
            dt_raw,
            dtb_value,
            alog_value,
        )

    prepared, pull_prep = jax.vjp(
        prepare_local,
        tail_in.astype(jnp.float32),
        conv_input.astype(jnp.float32),
        conv_weight,
        conv_bias,
        dt_bias,
        a_log,
    )
    values_x, keys_b, reads_c, steps_dt, log_decay = prepared
    zero_state = jnp.zeros((HEADS, HEAD_DIM, STATE), jnp.float32)

    def local_chain(x_value, b_value, c_value, dt_value, decay_value, gain_value):
        return chain_blocks(
            x_value, b_value, c_value, dt_value, decay_value, resets, gain_value, zero_state
        )

    (local_out, local_state), pull_chain = jax.vjp(
        local_chain, values_x, keys_b, reads_c, steps_dt, log_decay, skip_gain
    )

    def entering(decay_value):
        running = jnp.cumsum(decay_value, axis=0)
        untouched = (jnp.cumsum(resets) == 0).astype(running.dtype)
        return (
            jnp.exp(running) * untouched[:, None],
            jnp.exp(running[row_count - 1]) * untouched[row_count - 1],
        )

    entry_weight, through = entering(log_decay)
    upstream = cotangent.astype(jnp.float32)
    upstream_heads = upstream.reshape(row_count, HEADS, HEAD_DIM)
    adjoint_local = jnp.einsum(
        "thp,tn->hpn", upstream_heads * entry_weight[:, :, None], reads_c, precision=exact_mode
    )
    identity = (jnp.ones((HEADS,), jnp.float32), jnp.zeros((HEADS, HEAD_DIM, STATE), jnp.float32))
    incoming = prefix((through, local_state), "seq", join_states, identity, False)[1]
    adjoint_end = prefix((through, adjoint_local), "seq", join_states, identity, True)[1]

    def carried(c_value, decay_value):
        weight_in, through_in = entering(decay_value)
        added = (
            jnp.einsum("tn,hpn->thp", c_value, incoming, precision=exact_mode)
            * weight_in[:, :, None]
        )
        return (added.reshape(row_count, INNER), through_in[:, None, None] * incoming)

    (carried_out, _), pull_carried = jax.vjp(carried, reads_c, log_decay)
    output = (local_out + carried_out).astype(jnp.bfloat16)
    grad_x, grad_b, grad_c, grad_dt, grad_decay, grad_gain = pull_chain((upstream, adjoint_end))
    grad_c_extra, grad_decay_extra = pull_carried((upstream, adjoint_end))
    grad_tail, grad_rows, grad_weight, grad_bias, grad_dtb, grad_alog = pull_prep(
        (grad_x, grad_b, grad_c + grad_c_extra, grad_dt, grad_decay + grad_decay_extra)
    )
    returned = from_behind(grad_tail, "seq", -1)
    grad_rows = jnp.concatenate(
        [
            grad_rows[: row_count - CONV + 1],
            grad_rows[row_count - CONV + 1 :] + returned * keep_rows[:, None],
        ],
        axis=0,
    )
    summed = lax.psum((grad_weight, grad_bias, grad_dtb, grad_alog, grad_gain), ("dp", "seq"))
    scale = float(lax.axis_size("dp") * lax.axis_size("seq") * row_count) ** (-0.5)
    return (
        output,
        grad_rows.astype(jnp.bfloat16),
        summed[0] * scale,
        summed[1] * scale,
        summed[2] * scale,
        summed[3] * scale,
        summed[4] * scale,
    )


def solution(mesh):
    return jax.shard_map(
        on_device,
        mesh=mesh,
        in_specs=(
            P(("dp", "seq"), None),
            P(("dp", "seq")),
            P(),
            P(),
            P(("dp", "seq"), None),
            P(),
            P(),
            P(),
            P(("dp", "seq"), None),
        ),
        out_specs=(P(("dp", "seq"), None), P(("dp", "seq"), None), P(), P(), P(), P(), P()),
        check_vma=False,
    )
```

profile of v0, /device:TPU:1, one launch (start us, length us, event | category | flops | bytes accessed | tf_op | source)
XLA Modules:
  0.0 1133.3 jit_solution(11397604116379961711)
XLA Ops:
  9.4 4.6 collective-permute-start
  21.4 7.5 fusion.100
  31.3 5.1 reshape.509
  36.5 69.3 %while.76 = (s32[]{:T(128)}, f32[80,64,128]{2,1,0:T(8,128)S(1)}, f32[2,64,80,64]{3,2,1,0:T(8,128)}, f32[2,80,64,128]{3,2,1,0:T(8,128)}, f32[2,80]{1,0:T(2,128)S(...) while((s32[]{:T(128)}, f32[80,64,128]{2,1,0:T(8,128)S(1)}, ...), condition=%wide.region_5.6_spmd.clone, body=%wide.region_2.5_spmd.clone.sunk | while | flops 1271495936 | bytes 43904780 | solution.py:111
  50.0 5.3 multiply_add_fusion.7
  55.8 8.7 fusion.194
  84.6 5.3 multiply_add_fusion.7
  90.4 8.7 fusion.194
  114.3 21.7 %all-gather.2 = f32[32,1,80]{2,1,0:T(1,128)S(1)} all-gather(f32[1,1,80]{2,1,0:T(1,128)S(1)} %multiply_bitcast_fusion), channel_id=1, replica_groups=mesh['dp'=4,'seq'=32] {'seq'}, dimensions={0}, use_global_device_ids=true | all-gather | bytes 10560 | tf_op jit(solution)/shard_map/all_gather | solution.py:25
  136.0 218.2 %all-gather.6.cloned.1.call-done = f32[2560,64,128]{2,1,0:T(8,128)} async-done(((f32[80,64,128]{2,1,0:T(8,128)}), f32[2560,64,128]{2,1,0:T(8,128)}) %all-gather.6.cloned.1.call-update) | async-done | bytes 83886096 | tf_op jit(solution)/shard_map/all_gather | solution.py:25
  354.3 77.1 %while.77 = (s32[]{:T(128)}, f32[80,64,128]{2,1,0:T(8,128)S(1)}, s32[]{:T(128)}, f32[32,80]{1,0:T(8,128)S(1)}, f32[32,80,64,128]{3,2,1,0:T(8,128)}, /*index=5*/s32[]{:T(128)}, s32[]{:T(128)}) while((s32[]{:T(128)}, f32[80,64,128]{2,1,0:T(8,128)S(1)}, s32[]{:T(128)}, f32[32,80]{1,0:T(8,128)S(1)}, f32[32,80,64,128]{3,2,1,0:T(8,128)}, ...), condition=%wide.region_8.9_spmd.clone, body=%wide.region_7.8_spmd.clone.sunk | while | flops 2621444 | bytes 7865393 | solution.py:38
  431.3 8.7 multiply_reduce_fusion.10
  441.5 5.1 fusion.101
  446.7 6.0 reshape.542
  452.7 8.1 copy.125
  460.8 6.5 copy.124
  467.3 5.4 reshape.512
  472.7 4.2 copy.118
  484.9 205.6 %all-gather.8.cloned.1.call-done = f32[2560,64,128]{2,1,0:T(8,128)} async-done(((f32[80,64,128]{2,1,0:T(8,128)}), f32[2560,64,128]{2,1,0:T(8,128)}) %all-gather.8.cloned.1.call-update) | async-done | bytes 83886096 | tf_op jit(solution)/shard_map/all_gather | solution.py:25
  690.5 77.1 %while.78 = (s32[]{:T(128)}, f32[80,64,128]{2,1,0:T(8,128)S(1)}, s32[]{:T(128)}, f32[32,80]{1,0:T(8,128)S(1)}, f32[32,80,64,128]{3,2,1,0:T(8,128)}, /*index=5*/s32[]{:T(128)}, s32[]{:T(128)}, s32[]{:T(128)}, s32[]{:T(128)}) while((s32[]{:T(128)}, f32[80,64,128]{2,1,0:T(8,128)S(1)}, s32[]{:T(128)}, f32[32,80]{1,0:T(8,128)S(1)}, ...), condition=%wide.region_10.11_spmd.clone, body=%wide.region_9.10_spmd.clone.sunk | while | flops 2621448 | bytes 7865455 | solution.py:38
  772.6 176.0 %while.79 = (s32[]{:T(128)}, f32[80,64,128]{2,1,0:T(8,128)}, f32[80]{0:T(128)S(1)}, f32[2,64,80,64]{2,1,3,0:T(8,128)}, f32[2,64,128]{2,1,0:T(8,128)S(1)}, /*inde...) while((s32[]{:T(128)}, f32[80,64,128]{2,1,0:T(8,128)}, ...), condition=%wide.region_24.25_spmd.clone, body=%wide.region_11.24_spmd.clone.sunk | while | flops 3052656640 | bytes 114250048 | solution.py:111
  784.3 4.6 copy.230
  788.9 8.2 fusion.220
  797.3 9.1 multiply_reduce_fusion.17
  811.5 9.6 multiply_reduce_fusion.16
  821.3 4.1 fusion.223
  825.3 4.5 copy.225
  830.5 6.4 multiply_add_fusion.8
  836.9 6.5 fusion.219
  843.4 4.1 copy.229
  847.5 4.5 bitcast_dynamic-update-slice_fusion.7
  852.3 3.9 fusion.225
  868.3 4.7 copy.230
  873.0 8.2 fusion.220
  881.4 9.1 multiply_reduce_fusion.17
  895.6 9.6 multiply_reduce_fusion.16
  905.4 4.1 fusion.223
  909.5 4.7 copy.225
  914.8 6.4 multiply_add_fusion.8
  921.2 6.5 fusion.219
  931.6 4.5 bitcast_dynamic-update-slice_fusion.7
  936.3 3.9 fusion.225
  948.6 6.1 copy.127
  954.8 5.5 reshape.518
  960.3 7.3 fusion.110
  967.7 5.5 multiply_reduce_fusion.9
  986.6 66.0 %all-reduce.15 = (f32[5376]{0:T(1024)S(1)}, f32[80]{0:T(128)S(1)}, f32[80]{0:T(128)S(1)}, f32[80]{0:T(128)S(1)}) all-reduce(f32[5376]{0:T(1024)S(1)} %get-tuple-element.978, f32[80]{0:T(128)S(1)} %get-tuple-element.981, f32[80]{0:T(128)S(1)} %negate_multiply_fusion, ...), channel_id=1, replica_groups=mesh['dp'=4,'seq'=32] {'dp','seq'}, use_global_device_ids=true, to_apply=%region_31.32 | all-reduce | flops 5616 | bytes 44928 | tf_op jit(solution)/shard_map/psum | solution.py:203
  1057.0 65.2 %all-reduce.18.cloned.1.call-done = f32[4,5376]{1,0:T(4,128)} async-done(((f32[4,5376]{1,0:T(4,128)}), f32[4,5376]{1,0:T(4,128)}) %all-reduce.18.cloned.1.call-update) | async-done | bytes 86032 | tf_op jit(solution)/shard_map/psum | solution.py:203
  (441 shorter events, 289.2 us)
Async XLA Ops:
  7.2 14.3 %copy-start.37 = (f32[5376]{0:T(1024)S(1)}, f32[5376]{0:T(1024)}, u32[]{:S(2)}) copy-start(f32[5376]{0:T(1024)} %param.20) | copy-start | bytes 64516
  7.2 347.1 %all-gather.6.cloned.1.call-start = ((), (), s32[]{:S(2)}) async-start(), calls=%async_computation.1 | async-start | bytes 86507520 | tf_op jit(solution)/shard_map/all_gather | solution.py:25
  8.4 7.2 copy-start.50
  9.4 12.0 %collective-permute-start = (bf16[3,5376]{1,0:T(4,128)(2,1)S(1)}, bf16[3,5376]{1,0:T(4,128)(2,1)S(1)}, u32[]{:S(2)}, u32[]{:S(2)}) collective-permute-start(bf16[3,5376]{1,0:T(4,128)(2,1)S(1)} %slice_multiply_fusion), channel_id=1, source_target_pairs={{0,1},{1,2},{2,3},{3,4},{4,5},{5,6},{6,7},{7,8},{8,9},{9,10},{10,1... | collective-permute-start | bytes 96776 | tf_op jit(solution)/shard_map/ppermute | solution.py:20
  14.9 14.0 %copy-start.26 = (f32[128,80]{1,0:T(8,128)}, f32[128,80]{1,0:T(8,128)S(1)}, u32[]{:S(2)}) copy-start(f32[128,80]{1,0:T(8,128)S(1)} %copy.111) | copy-start | bytes 122884
  16.1 12.8 %copy-start.39 = (f32[128]{0:T(128)}, f32[128]{0:T(128)S(1)}, u32[]{:S(2)}) copy-start(f32[128]{0:T(128)S(1)} %get-tuple-element.1103) | copy-start | bytes 1540
  16.1 12.8 %copy-start.41 = (f32[128]{0:T(128)}, f32[128]{0:T(128)S(1)}, u32[]{:S(2)}) copy-start(f32[128]{0:T(128)S(1)} %get-tuple-element.1104) | copy-start | bytes 1540
  16.1 12.9 %copy-start.43 = (f32[128]{0:T(128)}, f32[128]{0:T(128)S(1)}, u32[]{:S(2)}) copy-start(f32[128]{0:T(128)S(1)} %get-tuple-element.1105) | copy-start | bytes 1540
  16.1 97.4 %copy-start.45 = (f32[128]{0:T(128)}, f32[128]{0:T(128)S(1)}, u32[]{:S(2)}) copy-start(f32[128]{0:T(128)S(1)} %get-tuple-element.1102) | copy-start | bytes 1540
  18.1 10.8 copy-start.29
  18.1 10.8 copy-start.31
  18.2 10.8 copy-start.33
  18.2 10.8 copy-start.35
  21.4 7.6 copy-start.22
  31.3 5.2 copy-start.38
  107.3 583.2 %all-gather.8.cloned.1.call-start = ((), (), s32[]{:S(2)}) async-start(), calls=%async_computation.2 | async-start | bytes 86507520 | tf_op jit(solution)/shard_map/all_gather | solution.py:25
  112.9 241.4 %copy-start.24 = (f32[128,80]{1,0:T(8,128)}, f32[128,80]{1,0:T(8,128)S(1)}, u32[]{:S(2)}) copy-start(f32[128,80]{1,0:T(8,128)S(1)} %reduce_window_sum.84) | copy-start | bytes 122884
  431.3 8.7 copy-start.5
  446.6 675.6 %all-reduce.18.cloned.1.call-start = ((), (), s32[]{:S(2)}) async-start(), calls=%async_computation | async-start | bytes 172032 | tf_op jit(solution)/shard_map/psum | solution.py:203
  797.3 9.1 copy-start
  806.4 5.2 copy-start.2
  830.5 6.4 copy-start.10
  847.5 4.8 copy-start.1
  847.5 4.8 copy-start.4
  881.3 9.1 copy-start
  890.4 5.2 copy-start.2
  914.8 6.4 copy-start.10
  931.5 4.8 copy-start.1
  954.8 5.5 copy-start.6
  954.8 12.9 %copy-start.23 = (f32[3,5376]{1,0:T(4,128)S(1)}, f32[3,5376]{1,0:T(4,128)}, u32[]{:S(2)}) copy-start(f32[3,5376]{1,0:T(4,128)} %copy-done.22) | copy-start | bytes 193540
  960.3 7.4 copy-start.17
  960.3 7.4 copy-start.20
  960.3 7.4 copy-start.40
  960.3 7.4 copy-start.42
  960.3 7.4 copy-start.44
  967.7 5.6 copy-start.30
  967.7 5.6 copy-start.32
  967.7 5.6 copy-start.34
  967.7 5.6 copy-start.36
  980.3 5.0 copy-start.28
  980.3 5.0 copy-start.46
  980.3 6.2 copy-start.27
  980.3 6.2 copy-start.47
  980.3 6.2 copy-start.49
  980.3 6.3 copy-start.52
  981.0 142.8 %copy-start.13 = (f32[128,5376]{1,0:T(8,128)S(1)}, f32[128,5376]{1,0:T(8,128)}, u32[]{:S(2)}) copy-start(f32[128,5376]{1,0:T(8,128)} %copy-done.12) | copy-start | bytes 8257540
  981.0 142.8 %copy-start.51 = (f32[3]{0:T(128)S(1)}, f32[3]{0:T(128)}, u32[]{:S(2)}) copy-start(f32[3]{0:T(128)} %copy-done.50) | copy-start | bytes 40
  981.0 142.8 %collective-permute-start.1 = (f32[3,5376]{1,0:T(4,128)S(1)}, f32[3,5376]{1,0:T(4,128)S(1)}, u32[]{:S(2)}, u32[]{:S(2)}) collective-permute-start(f32[3,5376]{1,0:T(4,128)S(1)} %pad_add_fusion.1), channel_id=1, source_target_pairs={{1,0},{2,1},{3,2},{4,3},{5,4},{6,5},{7,6},{8,7},{9,8},{10,9},{11,1... | collective-permute-start | bytes 193544 | tf_op jit(solution)/shard_map/ppermute | solution.py:20
  (17 other events, 46.8 us)
Sparse Core Ops, SparseCore 0:
  107.4 246.8 all-gather.5
  446.8 243.7 all-gather.7
  984.7 137.4 all-reduce.17
where the time goes:
time: 1140 us; the launch traced here: 1130 us
  waiting for transfers between devices  489 us (43%)
  other arithmetic  218 us (19%)
  matrix products  153 us (13%)
  local copies, waits for them, and re-layouts  151 us (13%)
  blocking collectives  87.7 us (8%)
  between operations  14.8 us (1%)
  loops' own time  12 us (1%)
    all_gather x2, waiting for transfers between devices, prefix(): everything = jax.tree.map(lambda part: lax.all_gather(part, axis), array)  424 us
    select_n x64, other arithmetic, step(): return jax.tree.map(lambda a, b: jnp.where(reached, a, b), new, before)  151 us
    psum x1, blocking collectives, on_device(): lax.psum((grad_weight, grad_bias, grad_dtb, grad_alog, grad_gain), ('dp',...  66 us
    psum x1, waiting for transfers between devices, on_device(): lax.psum((grad_weight, grad_bias, grad_dtb, grad_alog, grad_gain), ('dp',...  65.2 us
    dot_general x6, matrix products, scan_block(): output = jnp.einsum('hts,shp->thp', weights, values_x, precision=exact_mode)  46.7 us
    dot_general x8, matrix products, scan_block(): jnp.einsum('tn,hpn->thp', reads_c, carry_state, precision=exact_mode)  46.1 us
    dot_general x6, matrix products, scan_block(): jnp.einsum('shp,sn->hpn', leave_weight[:, :, None] * values_x, keys_b, pr...  37.8 us
    unnamed x97, local copies, waits for them, and re-layouts  28 us
  transfers between devices with their start and end apart: 5, of which 3 were waited for; matrix products, arithmetic and copies ran while one was open for 5% of the time, Pallas kernels for 0%

commit v1 on v0

v1 whole, which is shorter than its diff:
```python
import functools

import jax
import jax.numpy as jnp
from jax import lax
from jax.experimental import pallas as pl
from jax.experimental.pallas import tpu as pltpu
from jax.sharding import PartitionSpec as P

HEADS = 80
HEAD_DIM = 64
STATE = 128
CONV = 4
INNER = 5120
CH = 5376
ROWS = 128
TILE = 512
TILES = INNER // TILE
TILE_HEADS = TILE // HEAD_DIM
LANES = 128

F32 = jnp.float32
BF16 = jnp.bfloat16
EXACT = lax.Precision.HIGHEST
VMEM_BYTES = 48 << 20


def iota(shape, axis):
    return lax.broadcasted_iota(jnp.int32, shape, axis)


def halves(value):
    high = value.astype(BF16)
    return high, (value - high.astype(F32)).astype(BF16)


def mm(a, b):
    return lax.dot_general(a, b, (((1,), (0,)), ((), ())), preferred_element_type=F32)


def mm_nt(a, b):
    return lax.dot_general(a, b, (((1,), (1,)), ((), ())), preferred_element_type=F32)


def exact(a, b):
    return lax.dot_general(
        a, b, (((1,), (0,)), ((), ())), precision=EXACT, preferred_element_type=F32
    )


def interleave(group, late):
    row, col = iota((2 * STATE, STATE), 0), iota((2 * STATE, STATE), 1)
    place = row % (2 * group)
    first = group if late else 0
    here = (place >= first) & (place < first + group)
    return jnp.where(here & (col == group * (row // (2 * group)) + place - first), 1.0, 0.0)


def head_columns(tile):
    head, col = iota((LANES, TILE), 0), iota((LANES, TILE), 1)
    return jnp.where(head == TILE_HEADS * tile + col // HEAD_DIM, 1.0, 0.0).astype(BF16)


def spread_heads(both_ref, tile):
    one_hot = head_columns(tile)
    return mm(both_ref[...], jnp.concatenate([one_hot, one_hot], axis=0))


def convolve(tail, rows, taps, valid):
    extended = jnp.concatenate([tail, rows], axis=0)
    total = taps[4:5] + taps[3:4] * rows
    shifted = [rows]
    for back in range(1, CONV):
        moved = extended[8 - back : 8 - back + ROWS] * valid[:, back - 1 : back]
        shifted.append(moved)
        total = total + taps[3 - back : 4 - back] * moved
    return total, shifted


def sigmoid(v):
    return 1.0 / (1.0 + jnp.exp(-v))


def head_kernel(raw_ref, small_ref, col_ref, row_ref, run_ref, runT_ref, dt_ref, dtT_ref, both_ref,
                sig_ref, sigsum_ref, through_ref, mask_ref):
    reset_col, reset_row = col_ref[:, 0:1], row_ref[0:1, :]
    low = iota((ROWS, ROWS), 0) >= iota((ROWS, ROWS), 1)
    segment_col = jnp.sum(jnp.where(low, reset_row, 0.0), axis=1, keepdims=True)
    high = iota((ROWS, ROWS), 0) <= iota((ROWS, ROWS), 1)
    segment_row = jnp.sum(jnp.where(high, reset_col, 0.0), axis=0, keepdims=True)
    mask_ref[0] = jnp.where(low & (segment_col == segment_row), 1.0, 0.0)
    mask_ref[1] = jnp.where(high & (segment_col == segment_row), 1.0, 0.0)
    biased = raw_ref[...] + small_ref[0:1, :]
    dt = jnp.maximum(biased, 0.0) + jnp.log1p(jnp.exp(-jnp.abs(biased)))
    decay = -jnp.exp(small_ref[1:2, :]) * dt
    lower = jnp.where(low, 1.0, 0.0)
    running = exact(lower, decay)
    sig = sigmoid(biased)
    sig_ref[...] = sig
    sigsum_ref[...] = exact(lower, sig)
    run_ref[...] = running
    runT_ref[...] = running.T
    dt_ref[...] = dt
    dtT_ref[...] = dt.T
    last = running[ROWS - 1 : ROWS]
    count = segment_col[ROWS - 1 : ROWS]
    untouched = jnp.where(segment_col == 0.0, 1.0, 0.0)
    entry = jnp.exp(running) * untouched
    leave = jnp.exp(last - running) * jnp.where(segment_col == count, 1.0, 0.0) * dt
    for at, part in ((0, leave), (ROWS, entry)):
        first, second = halves(part)
        both_ref[at : at + ROWS, :LANES] = first
        both_ref[at : at + ROWS, LANES:] = second
    through_ref[...] = jnp.broadcast_to(entry[ROWS - 1 : ROWS], (8, LANES))


def head_stage(raw, small, col, row):
    square = jax.ShapeDtypeStruct((ROWS, LANES), F32)
    return pl.pallas_call(
        head_kernel,
        out_shape=(
            square, square, square, square,
            jax.ShapeDtypeStruct((2 * ROWS, 2 * LANES), BF16),
            square, square,
            jax.ShapeDtypeStruct((8, LANES), F32),
            jax.ShapeDtypeStruct((2, ROWS, ROWS), F32),
        ),
        name="heads",
    )(raw, small, col, row)


def local_kernel(group, x_ref, tail_ref, taps_ref, xs_ref, tails_ref, tapss_ref, valid_ref, cot_ref, both_ref,
                 act_ref, pair_ref, bc_ref, lhs_hi, lhs_lo):
    tile = pl.program_id(0)
    valid = valid_ref[...]

    @pl.when(tile == 0)
    def _():
        total, _ = convolve(tails_ref[...].astype(F32), xs_ref[...].astype(F32), tapss_ref[...], valid)
        small = total * sigmoid(total)
        bc_ref[...] = small
        for at, late in ((0, False), (STATE, True)):
            pick = interleave(group, late).astype(BF16)
            first, second = halves(small[:, at : at + STATE])
            lhs_hi[:, at : at + ROWS] = mm_nt(pick, first).astype(BF16)
            lhs_lo[:, at : at + ROWS] = mm_nt(pick, second).astype(BF16)

    total, _ = convolve(tail_ref[...].astype(F32), x_ref[...].astype(F32), taps_ref[...], valid)
    act = total * sigmoid(total)
    act_ref[...] = act
    weight = spread_heads(both_ref, tile)
    first, second = halves(weight * jnp.concatenate([act, cot_ref[...].astype(F32)], axis=0))
    result = mm(lhs_hi[...], first) + mm(lhs_hi[...], second) + mm(lhs_lo[...], first)
    pair_ref[...] = result.reshape(pair_ref.shape)


def tile_spec(rows):
    return pl.BlockSpec((rows, TILE), lambda i: (0, i))


def small_spec(rows):
    return pl.BlockSpec((rows, 2 * STATE), lambda i: (0, INNER // (2 * STATE)))


def whole(shape):
    return pl.BlockSpec(shape, lambda i: (0,) * len(shape))


def local_stage(group, conv_input, tail, taps, valid, cotangent, both):
    groups = STATE // group
    return pl.pallas_call(
        functools.partial(local_kernel, group),
        grid=(TILES,),
        in_specs=[
            tile_spec(ROWS), tile_spec(8), tile_spec(8),
            small_spec(ROWS), small_spec(8), small_spec(8),
            whole((ROWS, 8)), tile_spec(ROWS), whole((2 * ROWS, 2 * LANES)),
        ],
        out_specs=[
            tile_spec(ROWS),
            pl.BlockSpec((groups, 2 * group, TILE), lambda i: (0, 0, i)),
            whole((ROWS, 2 * STATE)),
        ],
        out_shape=(
            jax.ShapeDtypeStruct((ROWS, INNER), F32),
            jax.ShapeDtypeStruct((groups, 2 * group, INNER), F32),
            jax.ShapeDtypeStruct((ROWS, 2 * STATE), F32),
        ),
        scratch_shapes=[pltpu.VMEM((2 * STATE, 2 * ROWS), BF16)] * 2,
        compiler_params=pltpu.CompilerParams(vmem_limit_bytes=VMEM_BYTES),
        name="local",
    )(conv_input, tail, taps, conv_input, tail, taps, valid, cotangent, both)


def within_kernel(act_ref, cot_ref, bc_ref, run_ref, runT_ref, dt_ref, dtT_ref, mask_ref,
                  out_ref, grad_ref, score_grad_ref, score, scoreT):
    tile = pl.program_id(0)

    @pl.when(tile == 0)
    def _():
        keys, reads = bc_ref[:, :STATE], bc_ref[:, STATE:]
        keys_hi, keys_lo = halves(keys)
        reads_hi, reads_lo = halves(reads)
        score[...] = mask_ref[0] * (mm_nt(reads_hi, keys_hi) + mm_nt(reads_hi, keys_lo) + mm_nt(reads_lo, keys_hi))
        scoreT[...] = mask_ref[1] * (mm_nt(keys_hi, reads_hi) + mm_nt(keys_hi, reads_lo) + mm_nt(keys_lo, reads_hi))
        score_grad_ref[...] = jnp.zeros_like(score_grad_ref)

    turn = lax.rem(LANES - TILE_HEADS * tile, LANES)
    run = pltpu.roll(run_ref[...], turn, 1)
    dt = pltpu.roll(dt_ref[...], turn, 1)
    left = iota((ROWS, LANES), 1) < HEAD_DIM
    left = jnp.where(left, 1.0, 0.0).astype(BF16)
    right = 1.0 - left
    score_grad = score_grad_ref[...]
    for pair in range(TILE_HEADS // 2):
        lanes = slice(LANES * pair, LANES * (pair + 1))
        spread, weights, weightsT = [], [], []
        for head in (2 * pair, 2 * pair + 1):
            run_col, run_row = run[:, head : head + 1], runT_ref[head : head + 1, :]
            difference = run_col - run_row
            step = jnp.exp(jnp.minimum(difference, 0.0)) * dtT_ref[head : head + 1, :]
            spread.append(step)
            weights.append(step * score[...])
            weightsT.append(jnp.exp(jnp.minimum(-difference, 0.0)) * dt[:, head : head + 1] * scoreT[...])
        x_hi, x_lo = halves(act_ref[:, lanes])
        upstream = cot_ref[:, lanes]
        x_hi2 = jnp.concatenate([x_hi * left, x_hi * right], axis=0)
        x_lo2 = jnp.concatenate([x_lo * left, x_lo * right], axis=0)
        upstream2 = jnp.concatenate([upstream * left, upstream * right], axis=0)
        w_hi, w_lo = halves(jnp.concatenate(weights, axis=1))
        wide = mm(w_hi, jnp.concatenate([x_hi2, x_lo2], axis=1))
        out_ref[:, lanes] = wide[:, :LANES] + wide[:, LANES:] + mm(w_lo, x_hi2)
        wt_hi, wt_lo = halves(jnp.concatenate(weightsT, axis=1))
        grad_ref[:, lanes] = mm(wt_hi, upstream2) + mm(wt_lo, upstream2)
        inner = mm_nt(upstream2, jnp.concatenate([x_hi, x_lo], axis=0))
        inner = inner[:, :ROWS] + inner[:, ROWS:]
        score_grad = score_grad + inner[:ROWS] * spread[0] + inner[ROWS:] * spread[1]
    score_grad_ref[...] = score_grad

    @pl.when(tile == TILES - 1)
    def _():
        score_grad_ref[...] = score_grad_ref[...] * mask_ref[0]


def within_stage(act, cotangent, bc, run, runT, dt, dtT, mask):
    square = whole((ROWS, LANES))
    rows = pl.BlockSpec((TILE_HEADS, LANES), lambda i: (i, 0))
    wide = jax.ShapeDtypeStruct((ROWS, INNER), F32)
    return pl.pallas_call(
        within_kernel,
        grid=(TILES,),
        in_specs=[
            tile_spec(ROWS), tile_spec(ROWS), whole((ROWS, 2 * STATE)), square, rows, square, rows,
            whole((2, ROWS, ROWS)),
        ],
        out_specs=[tile_spec(ROWS), tile_spec(ROWS), whole((ROWS, ROWS))],
        out_shape=(wide, wide, jax.ShapeDtypeStruct((ROWS, ROWS), F32)),
        scratch_shapes=[pltpu.VMEM((ROWS, ROWS), F32)] * 2,
        compiler_params=pltpu.CompilerParams(vmem_limit_bytes=VMEM_BYTES),
        name="within",
    )(act, cotangent, bc, run, runT, dt, dtT, mask)


def carry_kernel(shards, pair_ref, through_ref, out_ref, decay):
    tile = pl.program_id(0)
    decay[...] = exact(through_ref[...], head_columns(tile).astype(F32))
    group = pair_ref.shape[1] // 2
    early = iota(pair_ref.shape[1:], 0) < group
    state = jnp.zeros(pair_ref.shape[1:], F32)
    for shard in range(shards):
        out_ref[shard] = state
        state = decay[shard : shard + 1, :] * state + pair_ref[shard]
    state = jnp.zeros(pair_ref.shape[1:], F32)
    for shard in reversed(range(shards)):
        out_ref[shard] = jnp.where(early, out_ref[shard], state)
        state = decay[shard : shard + 1, :] * state + pair_ref[shard]


def carry_stage(pairs, through):
    shards, rows, _ = pairs.shape
    block = pl.BlockSpec((shards, rows, TILE), lambda i: (0, 0, i))
    return pl.pallas_call(
        functools.partial(carry_kernel, shards),
        grid=(TILES,),
        in_specs=[block, whole((shards, LANES))],
        out_specs=block,
        out_shape=jax.ShapeDtypeStruct(pairs.shape, F32),
        scratch_shapes=[pltpu.VMEM((shards, TILE), F32)],
        compiler_params=pltpu.CompilerParams(vmem_limit_bytes=VMEM_BYTES),
        name="carry",
    )(pairs, through)


def conv_backward(grad, shifted, taps, valid):
    width = grad.shape[1]
    zeros = jnp.zeros((8, width), F32)
    total = jnp.concatenate([zeros, grad * taps[3:4]], axis=0)
    parts = [jnp.sum(grad * shifted[0], axis=0, keepdims=True)]
    for back in range(1, CONV):
        parts.insert(0, jnp.sum(grad * shifted[back], axis=0, keepdims=True))
        moved = jnp.concatenate([zeros, grad * valid[:, back - 1 : back] * taps[3 - back : 4 - back], zeros], axis=0)
        total = total + moved[back : back + ROWS + 8]
    parts.append(jnp.sum(grad, axis=0, keepdims=True))
    parts.append(jnp.zeros((3, width), F32))
    return total, jnp.concatenate(parts, axis=0)


def finish_kernel(group, x_ref, tail_ref, taps_ref, xs_ref, tails_ref, tapss_ref, valid_ref, cot_ref, both_ref,
                  out_in_ref, grad_in_ref, pair_ref, bc_ref, score_grad_ref, gain_ref, run_ref, dt_ref, sig_ref,
                  sigsum_ref, small_ref, through_ref,
                  out_ref, grad_ref, end_ref, borrowed_ref, taps_grad_ref, grads_ref, ends_ref, borroweds_ref,
                  tapss_grad_ref, heads_ref,
                  lhs_hi, lhs_lo, bc_grad, by_head, by_token):
    tile = pl.program_id(0)
    valid = valid_ref[...]

    @pl.when(tile == 0)
    def _():
        for at, source, late in ((0, STATE, False), (ROWS, 0, True)):
            pick = interleave(group, late).astype(BF16)
            first, second = halves(bc_ref[:, source : source + STATE])
            lhs_hi[at : at + ROWS, :] = mm_nt(first, pick).astype(BF16)
            lhs_lo[at : at + ROWS, :] = mm_nt(second, pick).astype(BF16)
        bc_grad[...] = jnp.zeros_like(bc_grad)
        by_head[...] = jnp.zeros_like(by_head)
        by_token[...] = jnp.zeros_like(by_token)

    total, shifted = convolve(tail_ref[...].astype(F32), x_ref[...].astype(F32), taps_ref[...], valid)
    gate = sigmoid(total)
    act = total * gate
    upstream = cot_ref[...].astype(F32)
    weight = spread_heads(both_ref, tile)
    leave, entry = weight[:ROWS], weight[ROWS:]
    states = pair_ref[...].reshape(2 * STATE, TILE)
    states_hi, states_lo = halves(states)
    read = mm(lhs_hi[...], states_hi) + mm(lhs_hi[...], states_lo) + mm(lhs_lo[...], states_hi)
    gain = gain_ref[...]
    through_state = out_in_ref[...] + entry * read[:ROWS]
    out_ref[...] = (through_state + gain * act).astype(BF16)
    act_grad_late = leave * read[ROWS:]
    act_grad = grad_in_ref[...] + act_grad_late

    first, second = halves(jnp.concatenate([entry * upstream, leave * act], axis=0))
    bc_grad[...] += mm_nt(first, states_hi) + mm_nt(first, states_lo) + mm_nt(second, states_hi)

    one_hot = head_columns(tile)
    first, second = halves(jnp.concatenate([upstream * through_state, act * act_grad], axis=0))
    by_token[...] += mm_nt(first, one_hot) + mm_nt(second, one_hot)
    crossed = states * pltpu.roll(states, group, 0)
    crossed = jnp.where(iota((2 * STATE, TILE), 0) % (2 * group) >= group, crossed, 0.0)
    sums = jnp.concatenate(
        [
            jnp.sum(act * act_grad_late, axis=0, keepdims=True),
            jnp.sum(crossed, axis=0, keepdims=True),
            jnp.sum(upstream * act, axis=0, keepdims=True),
            jnp.zeros((5, TILE), F32),
        ],
        axis=0,
    )
    by_head[...] += lax.dot_general(
        sums, one_hot.astype(F32), (((1,), (1,)), ((), ())), precision=EXACT, preferred_element_type=F32
    )

    act_grad = act_grad + gain * upstream
    conv_grad = act_grad * (gate + act * (1.0 - gate))
    full, taps_grad_ref[...] = conv_backward(conv_grad, shifted, taps_ref[...], valid)
    borrowed_ref[...] = full[:8]
    grad_ref[...] = full[8:].astype(BF16)
    end_ref[...] = full[ROWS - 8 :]

    @pl.when(tile == TILES - 1)
    def _():
        score_grad = score_grad_ref[...]
        keys, reads = bc_ref[:, :STATE], bc_ref[:, STATE:]
        reads_grad = exact(bc_grad[:ROWS], interleave(group, False)) + exact(score_grad, keys)
        keys_grad = exact(bc_grad[ROWS:], interleave(group, True)) + exact(score_grad.T, reads)
        total, shifted = convolve(tails_ref[...].astype(F32), xs_ref[...].astype(F32), tapss_ref[...], valid)
        gate = sigmoid(total)
        small_grad = jnp.concatenate([keys_grad, reads_grad], axis=1) * (gate + total * gate * (1.0 - gate))
        full, tapss_grad_ref[...] = conv_backward(small_grad, shifted, tapss_ref[...], valid)
        borroweds_ref[...] = full[:8]
        grads_ref[...] = full[8:].astype(BF16)
        ends_ref[...] = full[ROWS - 8 :]

        read_sum, added_sum = by_token[:ROWS], by_token[ROWS:]
        at_end = by_head[0:1, :] + through_ref[0:1, :] * by_head[1:2, :]
        run_grad = read_sum - added_sum + jnp.where(iota((ROWS, LANES), 0) == ROWS - 1, at_end, 0.0)
        alog_grad = jnp.sum(run_grad * run_ref[...], axis=0, keepdims=True)
        bias_grad = jnp.sum(added_sum / dt_ref[...] * sig_ref[...], axis=0, keepdims=True)
        rate = jnp.exp(small_ref[1:2, :])
        bias_grad = bias_grad - rate * jnp.sum(run_grad * sigsum_ref[...], axis=0, keepdims=True)
        heads_ref[...] = jnp.concatenate([bias_grad, alog_grad, by_head[2:3, :], jnp.zeros((5, LANES), F32)], axis=0)


def finish_stage(group, conv_input, tail, taps, valid, cotangent, both, out_in, grad_in, pairs, bc, score_grad,
                 gain, run, dt, sig, sigsum, small, through):
    groups = STATE // group
    square = whole((ROWS, LANES))
    eight = pl.BlockSpec((8, 2 * STATE), lambda i: (0, 0))
    return pl.pallas_call(
        functools.partial(finish_kernel, group),
        grid=(TILES,),
        in_specs=[
            tile_spec(ROWS), tile_spec(8), tile_spec(8),
            small_spec(ROWS), small_spec(8), small_spec(8),
            whole((ROWS, 8)), tile_spec(ROWS), whole((2 * ROWS, 2 * LANES)),
            tile_spec(ROWS), tile_spec(ROWS),
            pl.BlockSpec((groups, 2 * group, TILE), lambda i: (0, 0, i)),
            whole((ROWS, 2 * STATE)), whole((ROWS, ROWS)), tile_spec(1),
            square, square, square, square, whole((8, LANES)), whole((8, LANES)),
        ],
        out_specs=[
            tile_spec(ROWS), tile_spec(ROWS), tile_spec(16), tile_spec(8), tile_spec(8),
            whole((ROWS, 2 * STATE)), whole((16, 2 * STATE)), eight, eight, whole((8, LANES)),
        ],
        out_shape=(
            jax.ShapeDtypeStruct((ROWS, INNER), BF16),
            jax.ShapeDtypeStruct((ROWS, INNER), BF16),
            jax.ShapeDtypeStruct((16, INNER), F32),
            jax.ShapeDtypeStruct((8, INNER), F32),
            jax.ShapeDtypeStruct((8, INNER), F32),
            jax.ShapeDtypeStruct((ROWS, 2 * STATE), BF16),
            jax.ShapeDtypeStruct((16, 2 * STATE), F32),
            jax.ShapeDtypeStruct((8, 2 * STATE), F32),
            jax.ShapeDtypeStruct((8, 2 * STATE), F32),
            jax.ShapeDtypeStruct((8, LANES), F32),
        ),
        scratch_shapes=[
            pltpu.VMEM((2 * ROWS, 2 * STATE), BF16), pltpu.VMEM((2 * ROWS, 2 * STATE), BF16),
            pltpu.VMEM((2 * ROWS, 2 * STATE), F32), pltpu.VMEM((8, LANES), F32), pltpu.VMEM((2 * ROWS, LANES), F32),
        ],
        compiler_params=pltpu.CompilerParams(vmem_limit_bytes=VMEM_BYTES),
        name="finish",
    )(conv_input, tail, taps, conv_input, tail, taps, valid, cotangent, both, out_in, grad_in, pairs, bc, score_grad,
      gain, run, dt, sig, sigsum, small, through)


def exchange(array, axis):
    return lax.all_to_all(array, axis, 0, 0, tiled=True)


def pad_heads(array):
    return jnp.pad(array, ((0, 0), (0, LANES - HEADS)))


def neighbour(array, by):
    size = lax.axis_size("seq")
    return lax.ppermute(array, "seq", [(i, i + by) for i in range(size) if 0 <= i + by < size])


def total_over_all(flat):
    size = lax.axis_size("dp") * lax.axis_size("seq")
    piece = exchange(flat.reshape(size, flat.shape[0] // size), ("dp", "seq")).sum(0)
    return exchange(jnp.broadcast_to(piece[None], (size,) + piece.shape), ("dp", "seq")).reshape(-1)


def on_device(conv_input, doc_start, conv_weight, conv_bias, dt_raw, dt_bias, a_log, skip_gain, cotangent):
    shards = lax.axis_size("seq")
    group = STATE // shards
    resets = doc_start.astype(F32)
    kept = 1.0 - resets
    keep = jnp.stack([kept[ROWS - 2] * kept[ROWS - 1], kept[ROWS - 1], jnp.ones((), F32)])
    tail_out = conv_input[ROWS - CONV + 1 :] * keep[:, None].astype(BF16)
    tail = neighbour(jnp.pad(tail_out, ((8 - CONV + 1, 0), (0, 0))), 1)
    one_back = jnp.concatenate([jnp.ones((1,), F32), kept[:-1]])
    two_back = jnp.concatenate([jnp.ones((2,), F32), kept[:-2]])
    valid = jnp.stack([kept, kept * one_back, kept * one_back * two_back] + [kept] * 5, axis=1)
    taps = jnp.concatenate([conv_weight, conv_bias[None], jnp.zeros((3, CH), F32)], axis=0)
    small = jnp.pad(jnp.stack([dt_bias, a_log]), ((0, 6), (0, LANES - HEADS)))
    gain = jnp.repeat(skip_gain, HEAD_DIM)[None]

    run, runT, dt, dtT, both, sig, sigsum, through, mask = head_stage(
        pad_heads(dt_raw), small, jnp.broadcast_to(resets[:, None], (ROWS, 8)), resets[None]
    )
    all_through = exchange(jnp.broadcast_to(through[None, 0], (shards, LANES)), "seq")
    act, pairs, bc = local_stage(group, conv_input, tail, taps, valid, cotangent, both)
    gathered = exchange(pairs, "seq")
    out_in, grad_in, score_grad = within_stage(act, cotangent, bc, run, runT, dt, dtT, mask)
    carried = exchange(carry_stage(gathered, all_through), "seq")
    out, grad, end, borrowed, taps_grad, grads, ends, borroweds, tapss_grad, heads = finish_stage(
        group, conv_input, tail, taps, valid, cotangent, both, out_in, grad_in, carried, bc, score_grad, gain,
        run, dt, sig, sigsum, small, through,
    )
    returned = neighbour(jnp.concatenate([borrowed, borroweds], axis=1), -1)[8 - CONV + 1 :]
    tail_rows = jnp.concatenate([end, ends], axis=1)
    tail_rows = jnp.concatenate([tail_rows[: 16 - CONV + 1], tail_rows[16 - CONV + 1 :] + returned * keep[:, None]])
    whole_grad = jnp.concatenate(
        [jnp.concatenate([grad[: ROWS - 16], grads[: ROWS - 16]], axis=1), tail_rows.astype(BF16)], axis=0
    )
    params = jnp.concatenate([taps_grad[:5], tapss_grad[:5]], axis=1).reshape(-1)
    params = jnp.concatenate([params, heads[:3].reshape(-1)])
    size = lax.axis_size("dp") * shards
    used = params.shape[0]
    params = jnp.pad(params, (0, -used % (size * LANES)))
    params = total_over_all(params) * float(size * ROWS) ** (-0.5)
    heads = params[5 * CH : 5 * CH + 3 * LANES].reshape(3, LANES)[:, :HEADS]
    params = params[: 5 * CH].reshape(5, CH)
    return (out, whole_grad, params[:CONV], params[CONV], heads[0], heads[1], heads[2])


def solution(mesh):
    sharded = P(("dp", "seq"), None)
    return jax.shard_map(
        on_device,
        mesh=mesh,
        in_specs=(sharded, P(("dp", "seq")), P(), P(), sharded, P(), P(), P(), sharded),
        out_specs=(sharded, sharded, P(), P(), P(), P(), P()),
        check_vma=False,
    )
```

time: 1140 us -> 258 us (0.23)
  waiting for transfers between devices: 489 us -> 56.6 us
  other arithmetic: 218 us -> 11.1 us
  matrix products: 153 us -> 0 us
  local copies, waits for them, and re-layouts: 151 us -> 30.3 us
  Pallas kernels: 0 us -> 52.5 us
  starting transfers between devices: 7.43 us -> 34.4 us
  blocking collectives: 87.7 us -> 69.6 us
  between operations: 14.8 us -> 2.24 us
  loops' own time: 12 us -> 0 us
    all_gather x2 -> x0, waiting for transfers between devices: 424 us -> none  [prefix(): everything = jax.tree.map(lambda part: lax.all_gather(part, axis), array)]
    dot_general x31 -> x0, matrix products: 153 us -> none  [the longest x6 46.7 us: scan_block(): output = jnp.einsum('hts,shp->thp', weights, values_x, precision=exact_mode)]
    select_n x65 -> x0, other arithmetic: 151 us -> none  [the longest x64 151 us: step(): return jax.tree.map(lambda a, b: jnp.where(reached, a, b), new, before)]
    all_to_all x0 -> x1, blocking collectives: none -> 69.6 us  [exchange(): return lax.all_to_all(array, axis, 0, 0, tiled=True)]
    psum x1 -> x0, blocking collectives: 66 us -> none  [on_device(): lax.psum((grad_weight, grad_bias, grad_dtb, grad_alog, grad_gain), ('dp',...]
    psum x1 -> x0, waiting for transfers between devices: 65.2 us -> none  [on_device(): lax.psum((grad_weight, grad_bias, grad_dtb, grad_alog, grad_gain), ('dp',...]
    all_to_all x0 -> x4, waiting for transfers between devices: none -> 56.6 us  [exchange(): return lax.all_to_all(array, axis, 0, 0, tiled=True)]
    pallas_call x0 -> x5, Pallas kernels: none -> 52.5 us  [the longest x1 21.4 us: finish_stage(): pl.pallas_call(functools.partial(finish_kernel, group), grid=(TILES,), in...]
  transfers between devices with their start and end apart: 5 -> 6, of which waited for: 3 -> 3; matrix products, arithmetic and copies ran while one was open for 5% -> 6% of each run, Pallas kernels for 0% -> 9%
where the time goes in v1:
time: 258 us; the launch traced here: 257 us
  blocking collectives  69.6 us (27%)
  waiting for transfers between devices  56.6 us (22%)
  Pallas kernels  52.5 us (20%)
  starting transfers between devices  34.4 us (13%)
  local copies, waits for them, and re-layouts  30.3 us (12%)
  other arithmetic  11.1 us (4%)
    all_to_all x1, blocking collectives, exchange(): return lax.all_to_all(array, axis, 0, 0, tiled=True)  69.6 us
    all_to_all x4, waiting for transfers between devices, exchange(): return lax.all_to_all(array, axis, 0, 0, tiled=True)  56.6 us
    all_to_all x4, starting transfers between devices, exchange(): return lax.all_to_all(array, axis, 0, 0, tiled=True)  26.9 us
    pallas_call x1, Pallas kernels, finish_stage(): pl.pallas_call(functools.partial(finish_kernel, group), grid=(TILES,), in...  21.4 us
    unnamed x58, local copies, waits for them, and re-layouts  20.8 us
    pallas_call x1, Pallas kernels, within_stage(): pl.pallas_call(within_kernel, grid=(TILES,), in_specs=[tile_spec(ROWS), t...  11.3 us
    pallas_call x1, Pallas kernels, local_stage(): pl.pallas_call(functools.partial(local_kernel, group), grid=(TILES,), in_...  9.79 us
    pallas_call x1, Pallas kernels, carry_stage(): pl.pallas_call(functools.partial(carry_kernel, shards), grid=(TILES,), in...  7.98 us
  transfers between devices with their start and end apart: 6, of which 3 were waited for; matrix products, arithmetic and copies ran while one was open for 6% of the time, Pallas kernels for 9%

profile of v1, /device:TPU:1, one launch (start us, length us, event | category | flops | bytes accessed | tf_op | source)
XLA Modules:
  0.0 256.8 jit_solution(12231118217922818770)
XLA Ops:
  3.2 1.2 fusion.3
  4.4 1.0 slice_multiply_fusion.1
  5.4 4.6 %collective-permute-start = (bf16[8,5376]{1,0:T(8,128)(2,1)S(1)}, bf16[8,5376]{1,0:T(8,128)(2,1)S(1)}, u32[]{:S(2)}, u32[]{:S(2)}) collective-permute-start(bf16[8,5376]{1,0:T(8,128)(2,1)S(1)} %pad.17), channel_id=1, source_target_pairs={{0,1},{1,2},{2,3},{3,4},{4,5},{5,6},{6,7},{7,8},{8,9},{9,10},{10,1... | collective-permute-start | bytes 258056 | tf_op jit(solution)/shard_map/ppermute | solution.py:448
  10.0 1.2 convert_bitcast_fusion
  11.2 0.9 copy.40
  12.1 1.3 select_maximum_fusion.1.small_ref
  14.0 0.7 broadcast_in_dim.16.col_ref
  14.7 2.0 heads.1
  16.7 0.7 slice_bitcast_fusion.4
  18.0 7.9 %all-to-all-start.1 = ((f32[32,1,128]{2,1,0:T(1,128)}), f32[32,1,128]{2,1,0:T(1,128)S(1)}, u32[]{:S(2)}, u32[]{:S(2)}) async-start(f32[32,1,128]{2,1,0:T(1,128)} %broadcast_in_dim.35), calls=%async_computation.1 | async-start | bytes 32768 | tf_op jit(solution)/shard_map/all_to_all | solution.py:439
  26.0 0.8 broadcast_in_dim.14
  26.8 1.0 maximum_maximum_fusion.taps_ref.tapss_ref
  27.8 0.7 multiply_bitcast_fusion
  28.7 1.3 copy-done
  30.0 1.3 copy-done.3
  31.3 0.9 copy-done.9
  32.2 9.8 %local.1 = (f32[128,5120]{1,0:T(8,128)S(1)}, f32[32,8,5120]{2,1,0:T(8,128)}, f32[128,256]{1,0:T(8,128)S(1)}) custom-call(bf16[128,5376]{1,0:T(8,128)(2,1)S(1)} %copy-done, bf16[8,5376]{1,0:T(8,128)(2,1)S(1)} %collective-permute-done.tail_ref.tails_ref, f32[8,5376]{1,0:T(8,128)S(1)} %maximum_maximum_fusion.taps_ref.tapss_ref, bf16[128,5376]{1,0:T(8,128)(2,1)S(1)} %copy-done, ...), custom_call_target="tpu_custom_call" | custom-call | tf_op jit(solution)/shard_map/local/pallas_call | solution.py:171
  42.0 1.6 copy-done.6
  43.6 69.6 %all_to_all.33.pair_ref = f32[32,8,5120]{2,1,0:T(8,128)} all-to-all(f32[32,8,5120]{2,1,0:T(8,128)} %get-tuple-element.42), channel_id=1, replica_groups=mesh['dp'=4,'seq'=32] {'seq'}, dimensions={0} | all-to-all | bytes 10485760 | tf_op jit(solution)/shard_map/all_to_all | solution.py:439
  113.2 8.0 %carry.1 = f32[32,8,5120]{2,1,0:T(8,128)S(1)} custom-call(f32[32,8,5120]{2,1,0:T(8,128)} %all_to_all.33.pair_ref, f32[32,128]{1,0:T(8,128)S(1)} %bitcast.27), custom_call_target="tpu_custom_call" | custom-call | tf_op jit(solution)/shard_map/carry/pallas_call | solution.py:282
  121.2 2.4 copy-done.2
  123.6 5.0 %all-to-all-start.2 = ((f32[32,8,5120]{2,1,0:T(8,128)}), f32[32,8,5120]{2,1,0:T(8,128)}, u32[]{:S(2)}, u32[]{:S(2)}) async-start(f32[32,8,5120]{2,1,0:T(8,128)} %copy-done.2), calls=%async_computation.2 | async-start | bytes 10485760 | tf_op jit(solution)/shard_map/all_to_all | solution.py:439
  128.7 0.7 broadcast_in_dim.36
  129.3 0.9 broadcast_in_dim_reshape.3.gain_ref
  130.3 0.8 copy-done.18
  131.1 0.8 copy-done.19
  131.9 11.3 %within.1 = (f32[128,5120]{1,0:T(8,128)S(1)}, f32[128,5120]{1,0:T(8,128)}, f32[128,128]{1,0:T(8,128)S(1)}) custom-call(f32[128,5120]{1,0:T(8,128)} %copy-done.6, bf16[128,5120]{1,0:T(8,128)(2,1)S(1)} %copy-done.4, f32[128,256]{1,0:T(8,128)S(1)} %get-tuple-element.34.bc_ref, f32[128,128]{1,0:T(8,128)S(1)} %copy-done.12, f32[128,128]{1,0:T(8,128)S(1)} %copy-done.18, ...), custom_call_target="tpu_custom_call" | custom-call | tf_op jit(solution)/shard_map/within/pallas_call | solution.py:249
  143.2 1.6 copy-done.5
  145.5 44.7 %all-to-all-done.2.pair_ref = f32[32,8,5120]{2,1,0:T(8,128)} async-done(((f32[32,8,5120]{2,1,0:T(8,128)}), f32[32,8,5120]{2,1,0:T(8,128)}, u32[]{:S(2)}, u32[]{:S(2)}) %all-to-all-start.2) | async-done | bytes 5242912 | tf_op jit(solution)/shard_map/all_to_all | solution.py:439
  190.2 0.8 copy-done.16
  191.0 0.8 copy-done.17
  191.9 0.8 copy-done.21
  192.7 0.7 copy-done.22
  194.1 21.4 %finish.1 = (bf16[128,5120]{1,0:T(8,128)(2,1)}, bf16[128,5120]{1,0:T(8,128)(2,1)S(1)}, f32[16,5120]{1,0:T(8,128)S(1)}, f32[8,5120]{1,0:T(8,128)S(1)}, f32[8,5120...) custom-call(bf16[128,5376]{1,0:T(8,128)(2,1)S(1)} %copy-done.1, ...), custom_call_target="tpu_custom_call" | custom-call | tf_op jit(solution)/shard_map/finish/pallas_call | solution.py:400
  215.5 1.1 copy-done.7
  216.5 0.7 copy-done.11
  219.8 8.9 %all-to-all-start.3 = ((f32[128,1,256]{2,1,0:T(1,128)}), f32[128,1,256]{2,1,0:T(1,128)S(1)}, u32[]{:S(2)}, u32[]{:S(2)}) async-start(f32[128,1,256]{2,1,0:T(1,128)} %bitcast.9), calls=%async_computation.3 | async-start | bytes 262144 | tf_op jit(solution)/shard_map/all_to_all | solution.py:439
  228.7 0.9 pad_maximum_fusion.1
  229.7 3.0 %collective-permute-start.1 = (f32[8,5376]{1,0:T(8,128)S(1)}, f32[8,5376]{1,0:T(8,128)}, u32[]{:S(2)}, u32[]{:S(2)}) collective-permute-start(f32[8,5376]{1,0:T(8,128)S(1)} %pad_maximum_fusion.1), channel_id=1, source_target_pairs={{1,0},{2,1},{3,2},{4,3},{5,4},{6,5},{7,6},{8,7},{9,8},{10,9},{11,1... | collective-permute-start | bytes 516104 | tf_op jit(solution)/shard_map/ppermute | solution.py:448
  232.6 1.0 constant_dynamic-update-slice_fusion.1
  233.7 0.7 constant_dynamic-update-slice_fusion
  234.5 4.2 %all-to-all-done.3 = f32[128,1,256]{2,1,0:T(1,128)S(1)} async-done(((f32[128,1,256]{2,1,0:T(1,128)}), f32[128,1,256]{2,1,0:T(1,128)S(1)}, u32[]{:S(2)}, u32[]{:S(2)}) %all-to-all-start.3) | async-done | bytes 131104 | tf_op jit(solution)/shard_map/all_to_all | solution.py:439
  238.8 0.7 broadcast_in_dim.37
  239.5 5.1 %all-to-all-start.4 = ((f32[128,1,256]{2,1,0:T(1,128)}), f32[128,1,256]{2,1,0:T(1,128)S(1)}, u32[]{:S(2)}, u32[]{:S(2)}) async-start(f32[128,1,256]{2,1,0:T(1,128)} %broadcast_in_dim.37), calls=%async_computation.4 | async-start | bytes 262144 | tf_op jit(solution)/shard_map/all_to_all | solution.py:439
  244.6 1.0 fusion.1
  245.7 1.2 pad_maximum_fusion
  246.8 7.7 %all-to-all-done.4 = f32[128,1,256]{2,1,0:T(1,128)S(1)} async-done(((f32[128,1,256]{2,1,0:T(1,128)}), f32[128,1,256]{2,1,0:T(1,128)S(1)}, u32[]{:S(2)}, u32[]{:S(2)}) %all-to-all-start.4) | async-done | bytes 131104 | tf_op jit(solution)/shard_map/all_to_all | solution.py:439
  255.5 0.7 slice.99
  (67 shorter events, 8.5 us)
Async XLA Ops:
  5.4 23.2 %collective-permute-start = (bf16[8,5376]{1,0:T(8,128)(2,1)S(1)}, bf16[8,5376]{1,0:T(8,128)(2,1)S(1)}, u32[]{:S(2)}, u32[]{:S(2)}) collective-permute-start(bf16[8,5376]{1,0:T(8,128)(2,1)S(1)} %pad.17), channel_id=1, source_target_pairs={{0,1},{1,2},{2,3},{3,4},{4,5},{5,6},{6,7},{7,8},{8,9},{9,10},{10,1... | collective-permute-start | bytes 258056 | tf_op jit(solution)/shard_map/ppermute | solution.py:448
  18.0 25.6 %all-to-all-start.1 = ((f32[32,1,128]{2,1,0:T(1,128)}), f32[32,1,128]{2,1,0:T(1,128)S(1)}, u32[]{:S(2)}, u32[]{:S(2)}) async-start(f32[32,1,128]{2,1,0:T(1,128)} %broadcast_in_dim.35), calls=%async_computation.1 | async-start | bytes 32768 | tf_op jit(solution)/shard_map/all_to_all | solution.py:439
  28.7 1.3 copy-start
  30.0 1.3 copy-start.3
  31.3 0.9 copy-start.9
  42.0 1.6 copy-start.6
  121.2 2.4 copy-start.2
  123.6 5.0 %copy-start.27 = (f32[80]{0:T(128)S(1)}, f32[80]{0:T(128)}, u32[]{:S(2)}) copy-start(f32[80]{0:T(128)} %param.16) | copy-start | bytes 964
  123.6 6.6 %copy-start.4 = (bf16[128,5120]{1,0:T(8,128)(2,1)S(1)}, bf16[128,5120]{1,0:T(8,128)(2,1)}, u32[]{:S(2)}) copy-start(bf16[128,5120]{1,0:T(8,128)(2,1)} %cot_ref.5) | copy-start | bytes 3932164
  123.6 6.6 %copy-start.12 = (f32[128,128]{1,0:T(8,128)S(1)}, f32[128,128]{1,0:T(8,128)}, u32[]{:S(2)}) copy-start(f32[128,128]{1,0:T(8,128)} %get-tuple-element.35.run_ref) | copy-start | bytes 196612
  123.6 6.6 %copy-start.13 = (f32[128,128]{1,0:T(8,128)S(1)}, f32[128,128]{1,0:T(8,128)}, u32[]{:S(2)}) copy-start(f32[128,128]{1,0:T(8,128)} %get-tuple-element.37.dt_ref) | copy-start | bytes 196612
  123.6 6.7 %copy-start.15 = (f32[2,128,128]{2,1,0:T(8,128)S(1)}, f32[2,128,128]{2,1,0:T(8,128)}, u32[]{:S(2)}) copy-start(f32[2,128,128]{2,1,0:T(8,128)} %get-tuple-element.39.mask_ref) | copy-start | bytes 393220
  123.6 66.6 %all-to-all-start.2 = ((f32[32,8,5120]{2,1,0:T(8,128)}), f32[32,8,5120]{2,1,0:T(8,128)}, u32[]{:S(2)}, u32[]{:S(2)}) async-start(f32[32,8,5120]{2,1,0:T(8,128)} %copy-done.2), calls=%async_computation.2 | async-start | bytes 10485760 | tf_op jit(solution)/shard_map/all_to_all | solution.py:439
  128.6 61.5 %copy-start.1 = (bf16[128,5376]{1,0:T(8,128)(2,1)S(1)}, bf16[128,5376]{1,0:T(8,128)(2,1)}, u32[]{:S(2)}) copy-start(bf16[128,5376]{1,0:T(8,128)(2,1)} %xs_ref.3) | copy-start | bytes 4128772
  128.6 61.5 %copy-start.10 = (bf16[256,256]{1,0:T(8,128)(2,1)S(1)}, bf16[256,256]{1,0:T(8,128)(2,1)}, u32[]{:S(2)}) copy-start(bf16[256,256]{1,0:T(8,128)(2,1)} %get-tuple-element.32.both_ref) | copy-start | bytes 393220
  130.3 0.8 copy-start.18
  131.1 0.8 copy-start.19
  143.2 1.6 copy-start.5
  144.8 0.6 copy-start.20
  190.2 0.8 copy-start.16
  191.0 0.8 copy-start.17
  191.9 0.8 copy-start.21
  192.7 0.7 copy-start.22
  193.4 0.7 copy-start.25
  215.5 1.1 copy-start.7
  216.5 0.7 copy-start.11
  217.2 0.7 copy-start.14
  217.9 0.6 copy-start.23
  218.5 0.6 copy-start.24
  219.1 15.3 %copy-start.8 = (bf16[128,5120]{1,0:T(8,128)(2,1)S(1)}, bf16[128,5120]{1,0:T(8,128)(2,1)}, u32[]{:S(2)}) copy-start(bf16[128,5120]{1,0:T(8,128)(2,1)} %copy-done.7) | copy-start | bytes 3932164
  219.1 25.5 %copy-start.26 = (f32[3]{0:T(128)S(1)}, f32[3]{0:T(128)}, u32[]{:S(2)}) copy-start(f32[3]{0:T(128)} %get-tuple-element.60) | copy-start | bytes 40
  219.8 18.8 %all-to-all-start.3 = ((f32[128,1,256]{2,1,0:T(1,128)}), f32[128,1,256]{2,1,0:T(1,128)S(1)}, u32[]{:S(2)}, u32[]{:S(2)}) async-start(f32[128,1,256]{2,1,0:T(1,128)} %bitcast.9), calls=%async_computation.3 | async-start | bytes 262144 | tf_op jit(solution)/shard_map/all_to_all | solution.py:439
  229.7 15.0 %collective-permute-start.1 = (f32[8,5376]{1,0:T(8,128)S(1)}, f32[8,5376]{1,0:T(8,128)}, u32[]{:S(2)}, u32[]{:S(2)}) collective-permute-start(f32[8,5376]{1,0:T(8,128)S(1)} %pad_maximum_fusion.1), channel_id=1, source_target_pairs={{1,0},{2,1},{3,2},{4,3},{5,4},{6,5},{7,6},{8,7},{9,8},{10,9},{11,1... | collective-permute-start | bytes 516104 | tf_op jit(solution)/shard_map/ppermute | solution.py:448
  239.5 15.0 %all-to-all-start.4 = ((f32[128,1,256]{2,1,0:T(1,128)}), f32[128,1,256]{2,1,0:T(1,128)S(1)}, u32[]{:S(2)}, u32[]{:S(2)}) async-start(f32[128,1,256]{2,1,0:T(1,128)} %broadcast_in_dim.37), calls=%async_computation.4 | async-start | bytes 262144 | tf_op jit(solution)/shard_map/all_to_all | solution.py:439

commit v2 on v1

--- a/solution.py
+++ b/solution.py
@@ -22,7 +22,8 @@
 F32 = jnp.float32
 BF16 = jnp.bfloat16
 EXACT = lax.Precision.HIGHEST
-VMEM_BYTES = 48 << 20
+HALF_TILES = TILES // 2
+VMEM_BYTES = 60 << 20
 
 
 def iota(shape, axis):
@@ -81,16 +82,32 @@
     return 1.0 / (1.0 + jnp.exp(-v))
 
 
-def head_kernel(raw_ref, small_ref, col_ref, row_ref, run_ref, runT_ref, dt_ref, dtT_ref, both_ref,
-                sig_ref, sigsum_ref, through_ref, mask_ref):
-    reset_col, reset_row = col_ref[:, 0:1], row_ref[0:1, :]
-    low = iota((ROWS, ROWS), 0) >= iota((ROWS, ROWS), 1)
+def head_kernel(raw_in_ref, small_ref, row_ref, end_ref, run_ref, runT_ref, dt_ref, dtT_ref, both_ref, sig_ref,
+                sigsum_ref, through_ref, mask_ref, valid_ref, keep_ref, tail_ref, raw):
+    reset_row = row_ref[...].astype(F32)
+    token, other = iota((ROWS, ROWS), 0), iota((ROWS, ROWS), 1)
+    reset_col = jnp.sum(jnp.where(token == other, reset_row, 0.0), axis=1, keepdims=True)
+    low, high = token >= other, token <= other
     segment_col = jnp.sum(jnp.where(low, reset_row, 0.0), axis=1, keepdims=True)
-    high = iota((ROWS, ROWS), 0) <= iota((ROWS, ROWS), 1)
     segment_row = jnp.sum(jnp.where(high, reset_col, 0.0), axis=0, keepdims=True)
     mask_ref[0] = jnp.where(low & (segment_col == segment_row), 1.0, 0.0)
     mask_ref[1] = jnp.where(high & (segment_col == segment_row), 1.0, 0.0)
-    biased = raw_ref[...] + small_ref[0:1, :]
+
+    kept = jnp.broadcast_to(1.0 - reset_col, (ROWS, LANES))
+    one_back = jnp.where(token < 1, 1.0, pltpu.roll(kept, 1, 0))
+    two_back = jnp.where(token < 2, 1.0, pltpu.roll(kept, 2, 0))
+    valid = jnp.where(other == 0, kept, jnp.where(other == 1, kept * one_back, kept * one_back * two_back))
+    valid_ref[...] = valid[:, :8]
+    one_on, two_on = pltpu.roll(kept, ROWS - 1, 0), pltpu.roll(kept, ROWS - 2, 0)
+    keep = jnp.where(
+        token == ROWS - 1, 1.0, jnp.where(token == ROWS - 2, one_on, jnp.where(token == ROWS - 3, one_on * two_on, 0.0))
+    )[ROWS - 8 :]
+    keep_ref[...] = keep
+    tail_ref[...] = (end_ref[8:, :].astype(F32) * keep[:, 0:1]).astype(BF16)
+
+    raw[...] = jnp.zeros_like(raw)
+    raw[:, :HEADS] = raw_in_ref[...]
+    biased = raw[...] + small_ref[0:1, :]
     dt = jnp.maximum(biased, 0.0) + jnp.log1p(jnp.exp(-jnp.abs(biased)))
     decay = -jnp.exp(small_ref[1:2, :]) * dt
     lower = jnp.where(low, 1.0, 0.0)
@@ -111,30 +128,75 @@
         first, second = halves(part)
         both_ref[at : at + ROWS, :LANES] = first
         both_ref[at : at + ROWS, LANES:] = second
-    through_ref[...] = jnp.broadcast_to(entry[ROWS - 1 : ROWS], (8, LANES))
-
-
-def head_stage(raw, small, col, row):
+    through_ref[...] = jnp.broadcast_to(entry[ROWS - 1 : ROWS], through_ref.shape)
+
+
+def head_stage(shards, raw, small, row, conv_input):
     square = jax.ShapeDtypeStruct((ROWS, LANES), F32)
+    shapes = (
+        square, square, square, square,
+        jax.ShapeDtypeStruct((2 * ROWS, 2 * LANES), BF16),
+        square, square,
+        jax.ShapeDtypeStruct((shards, LANES), F32),
+        jax.ShapeDtypeStruct((2, ROWS, ROWS), F32),
+        jax.ShapeDtypeStruct((ROWS, 8), F32),
+        jax.ShapeDtypeStruct((8, LANES), F32),
+        jax.ShapeDtypeStruct((8, CH), BF16),
+    )
     return pl.pallas_call(
         head_kernel,
-        out_shape=(
-            square, square, square, square,
-            jax.ShapeDtypeStruct((2 * ROWS, 2 * LANES), BF16),
-            square, square,
-            jax.ShapeDtypeStruct((8, LANES), F32),
-            jax.ShapeDtypeStruct((2, ROWS, ROWS), F32),
+        grid=(1,),
+        in_specs=[
+            whole(raw.shape), whole((8, LANES)), whole((1, ROWS)),
+            pl.BlockSpec((16, CH), lambda *at: (ROWS // 16 - 1, 0)),
+        ],
+        out_specs=[whole(shape.shape) for shape in shapes],
+        out_shape=shapes,
+        scratch_shapes=[pltpu.VMEM((ROWS, LANES), F32)],
+        compiler_params=pltpu.CompilerParams(vmem_limit_bytes=VMEM_BYTES),
+        name="heads",
+    )(raw, small, row, conv_input)
+
+
+def whole(shape):
+    return pl.BlockSpec(shape, lambda *at: (0,) * len(shape))
+
+
+def call(kernel, name, half, grid, in_specs, out_specs, out_shape, scratch_shapes, operands):
+    return pl.pallas_call(
+        kernel,
+        grid_spec=pltpu.PrefetchScalarGridSpec(
+            num_scalar_prefetch=1, grid=(grid,), in_specs=in_specs, out_specs=out_specs, scratch_shapes=scratch_shapes
         ),
-        name="heads",
-    )(raw, small, col, row)
-
-
-def local_kernel(group, x_ref, tail_ref, taps_ref, xs_ref, tails_ref, tapss_ref, valid_ref, cot_ref, both_ref,
-                 act_ref, pair_ref, bc_ref, lhs_hi, lhs_lo):
-    tile = pl.program_id(0)
+        out_shape=out_shape,
+        compiler_params=pltpu.CompilerParams(vmem_limit_bytes=VMEM_BYTES),
+        name=name,
+    )(half, *operands)
+
+
+def tile_at(i, half):
+    return lax.rem(i + HALF_TILES * half[0], TILES)
+
+
+def tile_spec(rows):
+    return pl.BlockSpec((rows, TILE), lambda i, half: (0, tile_at(i, half)))
+
+
+def small_spec(rows):
+    return pl.BlockSpec((rows, 2 * STATE), lambda *at: (0, INNER // (2 * STATE)))
+
+
+def pair_spec(shape, first):
+    if first:
+        return pl.BlockSpec(shape[:2] + (TILE,), lambda i, half: (0, 0, jnp.minimum(i, HALF_TILES - 1)))
+    return pl.BlockSpec(shape[:2] + (TILE,), lambda i, half: (0, 0, jnp.maximum(i - HALF_TILES, 0)))
+
+
+def local_kernel(group, half_ref, x_ref, tail_ref, taps_ref, xs_ref, tails_ref, tapss_ref, valid_ref, cot_ref,
+                 both_ref, pair_ref, bc_ref, lhs_hi, lhs_lo):
     valid = valid_ref[...]
 
-    @pl.when(tile == 0)
+    @pl.when(pl.program_id(0) == 0)
     def _():
         total, _ = convolve(tails_ref[...].astype(F32), xs_ref[...].astype(F32), tapss_ref[...], valid)
         small = total * sigmoid(total)
@@ -147,53 +209,30 @@
 
     total, _ = convolve(tail_ref[...].astype(F32), x_ref[...].astype(F32), taps_ref[...], valid)
     act = total * sigmoid(total)
-    act_ref[...] = act
-    weight = spread_heads(both_ref, tile)
+    weight = spread_heads(both_ref, tile_at(pl.program_id(0), half_ref))
     first, second = halves(weight * jnp.concatenate([act, cot_ref[...].astype(F32)], axis=0))
     result = mm(lhs_hi[...], first) + mm(lhs_hi[...], second) + mm(lhs_lo[...], first)
     pair_ref[...] = result.reshape(pair_ref.shape)
 
 
-def tile_spec(rows):
-    return pl.BlockSpec((rows, TILE), lambda i: (0, i))
-
-
-def small_spec(rows):
-    return pl.BlockSpec((rows, 2 * STATE), lambda i: (0, INNER // (2 * STATE)))
-
-
-def whole(shape):
-    return pl.BlockSpec(shape, lambda i: (0,) * len(shape))
-
-
-def local_stage(group, conv_input, tail, taps, valid, cotangent, both):
-    groups = STATE // group
-    return pl.pallas_call(
-        functools.partial(local_kernel, group),
-        grid=(TILES,),
-        in_specs=[
+def local_stage(group, half, conv_input, tail, taps, valid, cotangent, both):
+    shape = (STATE // group, 2 * group, INNER // 2)
+    return call(
+        functools.partial(local_kernel, group), "local", half, HALF_TILES,
+        [
             tile_spec(ROWS), tile_spec(8), tile_spec(8),
             small_spec(ROWS), small_spec(8), small_spec(8),
             whole((ROWS, 8)), tile_spec(ROWS), whole((2 * ROWS, 2 * LANES)),
         ],
-        out_specs=[
-            tile_spec(ROWS),
-            pl.BlockSpec((groups, 2 * group, TILE), lambda i: (0, 0, i)),
-            whole((ROWS, 2 * STATE)),
-        ],
-        out_shape=(
-            jax.ShapeDtypeStruct((ROWS, INNER), F32),
-            jax.ShapeDtypeStruct((groups, 2 * group, INNER), F32),
-            jax.ShapeDtypeStruct((ROWS, 2 * STATE), F32),
-        ),
-        scratch_shapes=[pltpu.VMEM((2 * STATE, 2 * ROWS), BF16)] * 2,
-        compiler_params=pltpu.CompilerParams(vmem_limit_bytes=VMEM_BYTES),
-        name="local",
-    )(conv_input, tail, taps, conv_input, tail, taps, valid, cotangent, both)
-
-
-def within_kernel(act_ref, cot_ref, bc_ref, run_ref, runT_ref, dt_ref, dtT_ref, mask_ref,
-                  out_ref, grad_ref, score_grad_ref, score, scoreT):
+        [pair_spec(shape, True), whole((ROWS, 2 * STATE))],
+        (jax.ShapeDtypeStruct(shape, F32), jax.ShapeDtypeStruct((ROWS, 2 * STATE), F32)),
+        [pltpu.VMEM((2 * STATE, 2 * ROWS), BF16)] * 2,
+        (conv_input, tail, taps, conv_input, tail, taps, valid, cotangent, both),
+    )
+
+
+def within_kernel(half_ref, x_ref, tail_ref, taps_ref, valid_ref, cot_ref, bc_ref, run_ref, runT_ref, dt_ref, dtT_ref,
+                  mask_ref, out_ref, grad_ref, score_grad_ref, score, scoreT):
     tile = pl.program_id(0)
 
     @pl.when(tile == 0)
@@ -205,7 +244,9 @@
         scoreT[...] = mask_ref[1] * (mm_nt(keys_hi, reads_hi) + mm_nt(keys_hi, reads_lo) + mm_nt(keys_lo, reads_hi))
         score_grad_ref[...] = jnp.zeros_like(score_grad_ref)
 
-    turn = lax.rem(LANES - TILE_HEADS * tile, LANES)
+    total, _ = convolve(tail_ref[...].astype(F32), x_ref[...].astype(F32), taps_ref[...], valid_ref[...])
+    act = total * sigmoid(total)
+    turn = lax.rem(LANES - TILE_HEADS * tile_at(tile, half_ref), LANES)
     run = pltpu.roll(run_ref[...], turn, 1)
     dt = pltpu.roll(dt_ref[...], turn, 1)
     left = iota((ROWS, LANES), 1) < HEAD_DIM
@@ -222,7 +263,7 @@
             spread.append(step)
             weights.append(step * score[...])
             weightsT.append(jnp.exp(jnp.minimum(-difference, 0.0)) * dt[:, head : head + 1] * scoreT[...])
-        x_hi, x_lo = halves(act_ref[:, lanes])
+        x_hi, x_lo = halves(act[:, lanes])
         upstream = cot_ref[:, lanes]
         x_hi2 = jnp.concatenate([x_hi * left, x_hi * right], axis=0)
         x_lo2 = jnp.concatenate([x_lo * left, x_lo * right], axis=0)
@@ -242,53 +283,102 @@
         score_grad_ref[...] = score_grad_ref[...] * mask_ref[0]
 
 
-def within_stage(act, cotangent, bc, run, runT, dt, dtT, mask):
+def within_stage(half, conv_input, tail, taps, valid, cotangent, bc, run, runT, dt, dtT, mask):
     square = whole((ROWS, LANES))
-    rows = pl.BlockSpec((TILE_HEADS, LANES), lambda i: (i, 0))
+    rows = pl.BlockSpec((TILE_HEADS, LANES), lambda i, half: (tile_at(i, half), 0))
     wide = jax.ShapeDtypeStruct((ROWS, INNER), F32)
-    return pl.pallas_call(
-        within_kernel,
-        grid=(TILES,),
-        in_specs=[
-            tile_spec(ROWS), tile_spec(ROWS), whole((ROWS, 2 * STATE)), square, rows, square, rows,
-            whole((2, ROWS, ROWS)),
+    return call(
+        within_kernel, "within", half, TILES,
+        [
+            tile_spec(ROWS), tile_spec(8), tile_spec(8), whole((ROWS, 8)), tile_spec(ROWS),
+            whole((ROWS, 2 * STATE)), square, rows, square, rows, whole((2, ROWS, ROWS)),
         ],
-        out_specs=[tile_spec(ROWS), tile_spec(ROWS), whole((ROWS, ROWS))],
-        out_shape=(wide, wide, jax.ShapeDtypeStruct((ROWS, ROWS), F32)),
-        scratch_shapes=[pltpu.VMEM((ROWS, ROWS), F32)] * 2,
-        compiler_params=pltpu.CompilerParams(vmem_limit_bytes=VMEM_BYTES),
-        name="within",
-    )(act, cotangent, bc, run, runT, dt, dtT, mask)
-
-
-def carry_kernel(shards, pair_ref, through_ref, out_ref, decay):
-    tile = pl.program_id(0)
-    decay[...] = exact(through_ref[...], head_columns(tile).astype(F32))
-    group = pair_ref.shape[1] // 2
-    early = iota(pair_ref.shape[1:], 0) < group
-    state = jnp.zeros(pair_ref.shape[1:], F32)
-    for shard in range(shards):
-        out_ref[shard] = state
-        state = decay[shard : shard + 1, :] * state + pair_ref[shard]
-    state = jnp.zeros(pair_ref.shape[1:], F32)
-    for shard in reversed(range(shards)):
-        out_ref[shard] = jnp.where(early, out_ref[shard], state)
-        state = decay[shard : shard + 1, :] * state + pair_ref[shard]
-
-
-def carry_stage(pairs, through):
-    shards, rows, _ = pairs.shape
-    block = pl.BlockSpec((shards, rows, TILE), lambda i: (0, 0, i))
-    return pl.pallas_call(
-        functools.partial(carry_kernel, shards),
-        grid=(TILES,),
-        in_specs=[block, whole((shards, LANES))],
-        out_specs=block,
-        out_shape=jax.ShapeDtypeStruct(pairs.shape, F32),
-        scratch_shapes=[pltpu.VMEM((shards, TILE), F32)],
-        compiler_params=pltpu.CompilerParams(vmem_limit_bytes=VMEM_BYTES),
-        name="carry",
-    )(pairs, through)
+        [tile_spec(ROWS), tile_spec(ROWS), whole((ROWS, ROWS))],
+        (wide, wide, jax.ShapeDtypeStruct((ROWS, ROWS), F32)),
+        [pltpu.VMEM((ROWS, ROWS), F32)] * 2,
+        (conv_input, tail, taps, valid, cotangent, bc, run, runT, dt, dtT, mask),
+    )
+
+
+def chip_decay(half_ref, through_ref, rows):
+    one_hot = head_columns(tile_at(pl.program_id(0), half_ref)).astype(F32)
+    return exact(through_ref[rows, :], one_hot)
+
+
+def own_pair(half_ref):
+    return pl.ds(pl.multiple_of(8 * (half_ref[1] // 4), 8), 8)
+
+
+def even_odd(half_ref, through_ref):
+    chips = chip_decay(half_ref, through_ref, own_pair(half_ref))
+    place = lax.rem(half_ref[1], 4)
+    row = iota(chips.shape, 0)
+    earlier = jnp.sum(jnp.where(row == 2 * place, chips, 0.0), axis=0, keepdims=True)
+    later = jnp.sum(jnp.where(row == 2 * place + 1, chips, 0.0), axis=0, keepdims=True)
+    return earlier[None], later[None]
+
+
+def join_kernel(group, half_ref, mine_ref, other_ref, through_ref, out_ref):
+    earlier, later = even_odd(half_ref, through_ref)
+    even = half_ref[0] == 0
+    mine, other = mine_ref[...], other_ref[...]
+    first, second = jnp.where(even, mine, other), jnp.where(even, other, mine)
+    out_ref[:, :group, :] = later * first[:, :group] + second[:, :group]
+    out_ref[:, group:, :] = first[:, group:] + earlier * second[:, group:]
+
+
+def join_stage(group, half, mine, other, through):
+    spec = pair_spec(mine.shape, True)
+    return call(
+        functools.partial(join_kernel, group), "join", half, HALF_TILES,
+        [spec, spec, whole(through.shape)], spec, jax.ShapeDtypeStruct(mine.shape, F32), [], (mine, other, through),
+    )
+
+
+def part_kernel(group, half_ref, chip_ref, mine_ref, other_ref, through_ref, keep_ref, send_ref):
+    earlier, later = even_odd(half_ref, through_ref)
+    even = half_ref[0] == 0
+    chip, mine, other = chip_ref[...], mine_ref[...], other_ref[...]
+    state, adjoint = chip[:, :group], chip[:, group:]
+    state_later = earlier * state + jnp.where(even, mine[:, :group], other[:, :group])
+    adjoint_earlier = later * adjoint + jnp.where(even, other[:, group:], mine[:, group:])
+    keep_ref[:, :group, :] = jnp.where(even, state, state_later)
+    keep_ref[:, group:, :] = jnp.where(even, adjoint_earlier, adjoint)
+    send_ref[:, :group, :] = jnp.where(even, state_later, state)
+    send_ref[:, group:, :] = jnp.where(even, adjoint, adjoint_earlier)
+
+
+def part_stage(group, half, chip, mine, other, through):
+    spec = pair_spec(mine.shape, True)
+    shape = jax.ShapeDtypeStruct(mine.shape, F32)
+    return call(
+        functools.partial(part_kernel, group), "part", half, HALF_TILES,
+        [spec, spec, spec, whole(through.shape)], [spec, spec], (shape, shape), [], (chip, mine, other, through),
+    )
+
+
+def carry_kernel(group, half_ref, pair_ref, through_ref, out_ref, decay):
+    chips = pair_ref.shape[0]
+    decay[...] = chip_decay(half_ref, through_ref, slice(None))
+    state = jnp.zeros((group, TILE), F32)
+    for chip in range(chips):
+        out_ref[chip, :group, :] = state
+        state = decay[2 * chip : 2 * chip + 1, :] * decay[2 * chip + 1 : 2 * chip + 2, :] * state
+        state = state + pair_ref[chip, :group, :]
+    state = jnp.zeros((group, TILE), F32)
+    for chip in reversed(range(chips)):
+        out_ref[chip, group:, :] = state
+        state = decay[2 * chip : 2 * chip + 1, :] * decay[2 * chip + 1 : 2 * chip + 2, :] * state
+        state = state + pair_ref[chip, group:, :]
+
+
+def carry_stage(group, half, pairs, through):
+    spec = pair_spec(pairs.shape, True)
+    return call(
+        functools.partial(carry_kernel, group), "carry", half, HALF_TILES,
+        [spec, whole(through.shape)], spec, jax.ShapeDtypeStruct(pairs.shape, F32),
+        [pltpu.VMEM((through.shape[0], TILE), F32)], (pairs, through),
+    )
 
 
 def conv_backward(grad, shifted, taps, valid):
@@ -305,8 +395,8 @@
     return total, jnp.concatenate(parts, axis=0)
 
 
-def finish_kernel(group, x_ref, tail_ref, taps_ref, xs_ref, tails_ref, tapss_ref, valid_ref, cot_ref, both_ref,
-                  out_in_ref, grad_in_ref, pair_ref, bc_ref, score_grad_ref, gain_ref, run_ref, dt_ref, sig_ref,
+def finish_kernel(group, half_ref, x_ref, tail_ref, taps_ref, xs_ref, tails_ref, tapss_ref, valid_ref, cot_ref, both_ref,
+                  out_in_ref, grad_in_ref, pair_a_ref, pair_b_ref, bc_ref, score_grad_ref, run_ref, dt_ref, sig_ref,
                   sigsum_ref, small_ref, through_ref,
                   out_ref, grad_ref, end_ref, borrowed_ref, taps_grad_ref, grads_ref, ends_ref, borroweds_ref,
                   tapss_grad_ref, heads_ref,
@@ -329,12 +419,14 @@
     gate = sigmoid(total)
     act = total * gate
     upstream = cot_ref[...].astype(F32)
-    weight = spread_heads(both_ref, tile)
+    here = tile_at(tile, half_ref)
+    weight = spread_heads(both_ref, here)
     leave, entry = weight[:ROWS], weight[ROWS:]
-    states = pair_ref[...].reshape(2 * STATE, TILE)
+    states = jnp.where(tile < HALF_TILES, pair_a_ref[...], pair_b_ref[...]).reshape(2 * STATE, TILE)
     states_hi, states_lo = halves(states)
     read = mm(lhs_hi[...], states_hi) + mm(lhs_hi[...], states_lo) + mm(lhs_lo[...], states_hi)
-    gain = gain_ref[...]
+    one_hot = head_columns(here)
+    gain = exact(small_ref[...], one_hot.astype(F32))[2:3]
     through_state = out_in_ref[...] + entry * read[:ROWS]
     out_ref[...] = (through_state + gain * act).astype(BF16)
     act_grad_late = leave * read[ROWS:]
@@ -343,7 +435,6 @@
     first, second = halves(jnp.concatenate([entry * upstream, leave * act], axis=0))
     bc_grad[...] += mm_nt(first, states_hi) + mm_nt(first, states_lo) + mm_nt(second, states_hi)
 
-    one_hot = head_columns(tile)
     first, second = halves(jnp.concatenate([upstream * through_state, act * act_grad], axis=0))
     by_token[...] += mm_nt(first, one_hot) + mm_nt(second, one_hot)
     crossed = states * pltpu.roll(states, group, 0)
@@ -392,55 +483,44 @@
         heads_ref[...] = jnp.concatenate([bias_grad, alog_grad, by_head[2:3, :], jnp.zeros((5, LANES), F32)], axis=0)
 
 
-def finish_stage(group, conv_input, tail, taps, valid, cotangent, both, out_in, grad_in, pairs, bc, score_grad,
-                 gain, run, dt, sig, sigsum, small, through):
-    groups = STATE // group
+def finish_stage(group, half, conv_input, tail, taps, valid, cotangent, both, out_in, grad_in, pairs_a, pairs_b, bc,
+                 score_grad, run, dt, sig, sigsum, small, through):
     square = whole((ROWS, LANES))
-    eight = pl.BlockSpec((8, 2 * STATE), lambda i: (0, 0))
-    return pl.pallas_call(
-        functools.partial(finish_kernel, group),
-        grid=(TILES,),
-        in_specs=[
+    shapes = (
+        jax.ShapeDtypeStruct((ROWS, INNER), BF16),
+        jax.ShapeDtypeStruct((ROWS, INNER), BF16),
+        jax.ShapeDtypeStruct((16, INNER), F32),
+        jax.ShapeDtypeStruct((8, INNER), F32),
+        jax.ShapeDtypeStruct((8, INNER), F32),
+        jax.ShapeDtypeStruct((ROWS, 2 * STATE), BF16),
+        jax.ShapeDtypeStruct((16, 2 * STATE), F32),
+        jax.ShapeDtypeStruct((8, 2 * STATE), F32),
+        jax.ShapeDtypeStruct((8, 2 * STATE), F32),
+        jax.ShapeDtypeStruct((8, LANES), F32),
+    )
+    return call(
+        functools.partial(finish_kernel, group), "finish", half, TILES,
+        [
             tile_spec(ROWS), tile_spec(8), tile_spec(8),
             small_spec(ROWS), small_spec(8), small_spec(8),
             whole((ROWS, 8)), tile_spec(ROWS), whole((2 * ROWS, 2 * LANES)),
-            tile_spec(ROWS), tile_spec(ROWS),
-            pl.BlockSpec((groups, 2 * group, TILE), lambda i: (0, 0, i)),
-            whole((ROWS, 2 * STATE)), whole((ROWS, ROWS)), tile_spec(1),
+            tile_spec(ROWS), tile_spec(ROWS), pair_spec(pairs_a.shape, True), pair_spec(pairs_b.shape, False),
+            whole((ROWS, 2 * STATE)), whole((ROWS, ROWS)),
             square, square, square, square, whole((8, LANES)), whole((8, LANES)),
         ],
-        out_specs=[
-            tile_spec(ROWS), tile_spec(ROWS), tile_spec(16), tile_spec(8), tile_spec(8),
-            whole((ROWS, 2 * STATE)), whole((16, 2 * STATE)), eight, eight, whole((8, LANES)),
-        ],
-        out_shape=(
-            jax.ShapeDtypeStruct((ROWS, INNER), BF16),
-            jax.ShapeDtypeStruct((ROWS, INNER), BF16),
-            jax.ShapeDtypeStruct((16, INNER), F32),
-            jax.ShapeDtypeStruct((8, INNER), F32),
-            jax.ShapeDtypeStruct((8, INNER), F32),
-            jax.ShapeDtypeStruct((ROWS, 2 * STATE), BF16),
-            jax.ShapeDtypeStruct((16, 2 * STATE), F32),
-            jax.ShapeDtypeStruct((8, 2 * STATE), F32),
-            jax.ShapeDtypeStruct((8, 2 * STATE), F32),
-            jax.ShapeDtypeStruct((8, LANES), F32),
-        ),
-        scratch_shapes=[
+        [tile_spec(shape.shape[0]) for shape in shapes[:5]] + [whole(shape.shape) for shape in shapes[5:]],
+        shapes,
+        [
             pltpu.VMEM((2 * ROWS, 2 * STATE), BF16), pltpu.VMEM((2 * ROWS, 2 * STATE), BF16),
             pltpu.VMEM((2 * ROWS, 2 * STATE), F32), pltpu.VMEM((8, LANES), F32), pltpu.VMEM((2 * ROWS, LANES), F32),
         ],
-        compiler_params=pltpu.CompilerParams(vmem_limit_bytes=VMEM_BYTES),
-        name="finish",
-    )(conv_input, tail, taps, conv_input, tail, taps, valid, cotangent, both, out_in, grad_in, pairs, bc, score_grad,
-      gain, run, dt, sig, sigsum, small, through)
+        (conv_input, tail, taps, conv_input, tail, taps, valid, cotangent, both, out_in, grad_in, pairs_a, pairs_b, bc,
+         score_grad, run, dt, sig, sigsum, small, through),
+    )
 
 
 def exchange(array, axis):
     return lax.all_to_all(array, axis, 0, 0, tiled=True)
-
-
-def pad_heads(array):
-    return jnp.pad(array, ((0, 0), (0, LANES - HEADS)))
 
 
 def neighbour(array, by):
@@ -454,36 +534,48 @@
     return exchange(jnp.broadcast_to(piece[None], (size,) + piece.shape), ("dp", "seq")).reshape(-1)
 
 
+def swap(array):
+    return lax.ppermute(array, "seq", [(i, i ^ 1) for i in range(lax.axis_size("seq"))])
+
+
+def between_chips(array):
+    size = lax.axis_size("seq")
+    groups = [list(range(0, size, 2)), list(range(1, size, 2))]
+    return lax.all_to_all(array, "seq", 0, 0, axis_index_groups=groups, tiled=True)
+
+
 def on_device(conv_input, doc_start, conv_weight, conv_bias, dt_raw, dt_bias, a_log, skip_gain, cotangent):
-    shards = lax.axis_size("seq")
-    group = STATE // shards
-    resets = doc_start.astype(F32)
-    kept = 1.0 - resets
-    keep = jnp.stack([kept[ROWS - 2] * kept[ROWS - 1], kept[ROWS - 1], jnp.ones((), F32)])
-    tail_out = conv_input[ROWS - CONV + 1 :] * keep[:, None].astype(BF16)
-    tail = neighbour(jnp.pad(tail_out, ((8 - CONV + 1, 0), (0, 0))), 1)
-    one_back = jnp.concatenate([jnp.ones((1,), F32), kept[:-1]])
-    two_back = jnp.concatenate([jnp.ones((2,), F32), kept[:-2]])
-    valid = jnp.stack([kept, kept * one_back, kept * one_back * two_back] + [kept] * 5, axis=1)
+    shards, place = lax.axis_size("seq"), lax.axis_index("seq")
+    group = 2 * STATE // shards
+    core = lax.rem(place, 2)
+    half = jnp.stack([core, place // 2])
+    other_half = jnp.stack([1 - core, place // 2])
     taps = jnp.concatenate([conv_weight, conv_bias[None], jnp.zeros((3, CH), F32)], axis=0)
-    small = jnp.pad(jnp.stack([dt_bias, a_log]), ((0, 6), (0, LANES - HEADS)))
-    gain = jnp.repeat(skip_gain, HEAD_DIM)[None]
-
-    run, runT, dt, dtT, both, sig, sigsum, through, mask = head_stage(
-        pad_heads(dt_raw), small, jnp.broadcast_to(resets[:, None], (ROWS, 8)), resets[None]
-    )
-    all_through = exchange(jnp.broadcast_to(through[None, 0], (shards, LANES)), "seq")
-    act, pairs, bc = local_stage(group, conv_input, tail, taps, valid, cotangent, both)
-    gathered = exchange(pairs, "seq")
-    out_in, grad_in, score_grad = within_stage(act, cotangent, bc, run, runT, dt, dtT, mask)
-    carried = exchange(carry_stage(gathered, all_through), "seq")
+    small = jnp.pad(jnp.stack([dt_bias, a_log, skip_gain]), ((0, 5), (0, LANES - HEADS)))
+
+    run, runT, dt, dtT, both, sig, sigsum, through, mask, valid, keep, tail = head_stage(
+        shards, dt_raw, small, doc_start[None], conv_input
+    )
+    tail = neighbour(tail, 1)
+    all_through = exchange(through, "seq")
+    theirs, bc = local_stage(group, other_half, conv_input, tail, taps, valid, cotangent, both)
+    other = swap(theirs)
+    mine, _ = local_stage(group, half, conv_input, tail, taps, valid, cotangent, both)
+    gathered = between_chips(join_stage(group, half, mine, other, all_through))
+    out_in, grad_in, score_grad = within_stage(
+        half, conv_input, tail, taps, valid, cotangent, bc, run, runT, dt, dtT, mask
+    )
+    chip = between_chips(carry_stage(group, half, gathered, all_through))
+    pairs_a, pairs_b = part_stage(group, half, chip, mine, other, all_through)
+    pairs_b = swap(pairs_b)
     out, grad, end, borrowed, taps_grad, grads, ends, borroweds, tapss_grad, heads = finish_stage(
-        group, conv_input, tail, taps, valid, cotangent, both, out_in, grad_in, carried, bc, score_grad, gain,
-        run, dt, sig, sigsum, small, through,
-    )
+        group, half, conv_input, tail, taps, valid, cotangent, both, out_in, grad_in, pairs_a, pairs_b, bc, score_grad,
+        run, dt, sig, sigsum, small, through[:8],
+    )
+    keep = keep[8 - CONV + 1 :, 0:1]
     returned = neighbour(jnp.concatenate([borrowed, borroweds], axis=1), -1)[8 - CONV + 1 :]
     tail_rows = jnp.concatenate([end, ends], axis=1)
-    tail_rows = jnp.concatenate([tail_rows[: 16 - CONV + 1], tail_rows[16 - CONV + 1 :] + returned * keep[:, None]])
+    tail_rows = jnp.concatenate([tail_rows[: 16 - CONV + 1], tail_rows[16 - CONV + 1 :] + returned * keep])
     whole_grad = jnp.concatenate(
         [jnp.concatenate([grad[: ROWS - 16], grads[: ROWS - 16]], axis=1), tail_rows.astype(BF16)], axis=0
     )

time: 258 us -> 222 us (0.86)
  waiting for transfers between devices: 56.6 us -> 12 us
  Pallas kernels: 52.5 us -> 79.8 us
  local copies, waits for them, and re-layouts: 30.3 us -> 13.6 us
  blocking collectives: 69.6 us -> 77.1 us
  starting transfers between devices: 34.4 us -> 29.1 us
  other arithmetic: 11.1 us -> 8.2 us
    all_to_all x4 -> x3, waiting for transfers between devices: 56.6 us -> 12 us  [exchange(): return lax.all_to_all(array, axis, 0, 0, tiled=True)]
    pallas_call x5 -> x8, Pallas kernels: 52.5 us -> 79.8 us  [the longest x7 77.6 us: call(): pl.pallas_call(kernel, grid_spec=pltpu.PrefetchScalarGridSpec(num_scalar_...]
    unnamed x58 -> x14, local copies, waits for them, and re-layouts: 20.8 us -> 6.18 us
    all_to_all x4 -> x3, starting transfers between devices: 26.9 us -> 18.9 us  [exchange(): return lax.all_to_all(array, axis, 0, 0, tiled=True)]
    all_to_all x1 -> x2, blocking collectives: 69.6 us -> 77.1 us  [between_chips(): lax.all_to_all(array, 'seq', 0, 0, axis_index_groups=groups, tiled=True)]
  transfers between devices with their start and end apart: 6 -> 7, of which waited for: 3 -> 2; matrix products, arithmetic and copies ran while one was open for 6% -> 5% of each run, Pallas kernels for 9% -> 10%
where the time goes in v2:
time: 222 us; the launch traced here: 221 us
  Pallas kernels  79.8 us (36%)
  blocking collectives  77.1 us (35%)
  starting transfers between devices  29.1 us (13%)
  local copies, waits for them, and re-layouts  13.6 us (6%)
  waiting for transfers between devices  12 us (5%)
  other arithmetic  8.2 us (4%)
    pallas_call x7, Pallas kernels, call(): pl.pallas_call(kernel, grid_spec=pltpu.PrefetchScalarGridSpec(num_scalar_...  77.6 us
    all_to_all x2, blocking collectives, between_chips(): lax.all_to_all(array, 'seq', 0, 0, axis_index_groups=groups, tiled=True)  77.1 us
    all_to_all x3, starting transfers between devices, exchange(): return lax.all_to_all(array, axis, 0, 0, tiled=True)  18.9 us
    all_to_all x3, waiting for transfers between devices, exchange(): return lax.all_to_all(array, axis, 0, 0, tiled=True)  12 us
    ppermute x2, starting transfers between devices, neighbour(): lax.ppermute(array, 'seq', [(i, i + by) for i in range(size) if 0 <= i +...  7.58 us
    unnamed x14, local copies, waits for them, and re-layouts  6.18 us
  transfers between devices with their start and end apart: 7, of which 2 were waited for; matrix products, arithmetic and copies ran while one was open for 5% of the time, Pallas kernels for 10%

profile of v2, /device:TPU:1, one launch (start us, length us, event | category | flops | bytes accessed | tf_op | source)
XLA Modules:
  0.0 220.6 jit_solution(9743281535613760696)
XLA Ops:
  0.6 1.5 copy.22.raw_in_ref
  2.1 1.3 select_maximum_fusion.1.small_ref
  3.4 2.2 %heads.1 = (f32[128,128]{1,0:T(8,128)}, f32[128,128]{1,0:T(8,128)}, f32[128,128]{1,0:T(8,128)}, f32[128,128]{1,0:T(8,128)}, bf16[256,256]{1,0:T(8,128)(2,1)}, /*...) custom-call(f32[128,80]{1,0:T(8,128)} %copy.22.raw_in_ref, ...), custom_call_target="tpu_custom_call" | custom-call | tf_op jit(solution)/shard_map/heads/pallas_call | solution.py:146
  5.6 4.6 %collective-permute-start = (bf16[8,5376]{1,0:T(8,128)(2,1)}, bf16[8,5376]{1,0:T(8,128)(2,1)S(1)}, u32[]{:S(2)}, u32[]{:S(2)}) collective-permute-start(bf16[8,5376]{1,0:T(8,128)(2,1)} %get-tuple-element.37), channel_id=1, source_target_pairs={{0,1},{1,2},{2,3},{3,4},{4,5},{5,6},{6,7},{7,8},{8,9},{9,10},{10,1... | collective-permute-start | bytes 258056 | tf_op jit(solution)/shard_map/ppermute | solution.py:528
  10.3 0.8 broadcast_in_dim.16
  11.0 0.1 pad.24.clone
  11.1 1.7 maximum_maximum_fusion.taps_ref.tapss_ref
  12.8 0.6 pad_add_fusion.1.half_ref
  13.4 0.6 copy-done.1
  14.0 7.9 %local.2 = (f32[16,16,2560]{2,1,0:T(8,128)}, f32[128,256]{1,0:T(8,128)}) custom-call(s32[2]{0:T(128)} %pad_add_fusion.1.half_ref, bf16[128,5376]{1,0:T(8,128)(2,1)} %xs_ref.5, bf16[8,5376]{1,0:T(8,128)(2,1)} %copy-done.1, f32[8,5376]{1,0:T(8,128)} %maximum_maximum_fusion.taps_ref.tapss_ref, bf16[128,5376]{1,0:T(8,128)(2,1)} %xs_ref.5, ...), custom_call_target="tpu_custom_call" | custom-call | tf_op jit(solution)/shard_map/local/pallas_call | solution.py:166
  21.9 8.3 %all-to-all-start = ((f32[32,1,128]{2,1,0:T(1,128)}), f32[32,1,128]{2,1,0:T(1,128)S(1)}, u32[]{:S(2)}, u32[]{:S(2)}) async-start(f32[32,1,128]{2,1,0:T(1,128)} %bitcast.8), calls=%async_computation | async-start | bytes 32768 | tf_op jit(solution)/shard_map/all_to_all | solution.py:523
  30.2 0.6 pad_add_fusion.half_ref
  30.8 8.0 %local.3 = (f32[16,16,2560]{2,1,0:T(8,128)}, f32[128,256]{1,0:T(8,128)}) custom-call(s32[2]{0:T(128)} %pad_add_fusion.half_ref, bf16[128,5376]{1,0:T(8,128)(2,1)} %xs_ref.5, bf16[8,5376]{1,0:T(8,128)(2,1)} %copy-done.1, f32[8,5376]{1,0:T(8,128)} %maximum_maximum_fusion.taps_ref.tapss_ref, bf16[128,5376]{1,0:T(8,128)(2,1)} %xs_ref.5, ...), custom_call_target="tpu_custom_call" | custom-call | tf_op jit(solution)/shard_map/local/pallas_call | solution.py:166
  38.7 0.6 copy-done.4
  39.3 0.9 copy-done
  40.2 6.8 %join.1 = f32[16,16,2560]{2,1,0:T(8,128)} custom-call(s32[2]{0:T(128)} %pad_add_fusion.half_ref, f32[16,16,2560]{2,1,0:T(8,128)} %get-tuple-element.48.mine_ref, f32[16,16,2560]{2,1,0:T(8,128)} %copy-done, f32[32,128]{1,0:T(8,128)} %bitcast.24), custom_call_target="tpu_custom_call" | custom-call | tf_op jit(solution)/shard_map/join/pallas_call | solution.py:166
  47.0 40.0 %all_to_all.36.pair_ref = f32[16,16,2560]{2,1,0:T(8,128)} all-to-all(f32[16,16,2560]{2,1,0:T(8,128)} %join.1), channel_id=1, replica_groups={{0,2,4,6,8,10,12,14,16,18,20,22,24,26,28,30},{1,3,5,7,9,11,13,15,17,19,..., dimensions={0} | all-to-all | bytes 5242880 | tf_op jit(solution)/shard_map/all_to_all | solution.py:544
  87.0 6.2 %carry.1 = f32[16,16,2560]{2,1,0:T(8,128)} custom-call(s32[2]{0:T(128)} %pad_add_fusion.half_ref, f32[16,16,2560]{2,1,0:T(8,128)} %all_to_all.36.pair_ref, f32[32,128]{1,0:T(8,128)} %bitcast.25), custom_call_target="tpu_custom_call" | custom-call | tf_op jit(solution)/shard_map/carry/pallas_call | solution.py:166
  93.2 37.1 %all_to_all.37.chip_ref = f32[16,16,2560]{2,1,0:T(8,128)} all-to-all(f32[16,16,2560]{2,1,0:T(8,128)} %carry.1), channel_id=1, replica_groups={{0,2,4,6,8,10,12,14,16,18,20,22,24,26,28,30},{1,3,5,7,9,11,13,15,17,19,..., dimensions={0} | all-to-all | bytes 5242880 | tf_op jit(solution)/shard_map/all_to_all | solution.py:544
  130.3 8.9 %part.1 = (f32[16,16,2560]{2,1,0:T(8,128)}, f32[16,16,2560]{2,1,0:T(8,128)}) custom-call(s32[2]{0:T(128)} %pad_add_fusion.half_ref, f32[16,16,2560]{2,1,0:T(8,128)} %all_to_all.37.chip_ref, f32[16,16,2560]{2,1,0:T(8,128)} %get-tuple-element.48.mine_ref, f32[16,16,2560]{2,1,0:T(8,128)} %copy-done, f32[32,128]{1,0:T(8,128)} %bitcast.26), custom_call_target="tpu_custom_call" | custom-call | tf_op jit(solution)/shard_map/part/pallas_call | solution.py:166
  139.2 2.6 %collective-permute-start.2 = (f32[16,16,2560]{2,1,0:T(8,128)}, f32[16,16,2560]{2,1,0:T(8,128)S(1)}, u32[]{:S(2)}, u32[]{:S(2)}) collective-permute-start(f32[16,16,2560]{2,1,0:T(8,128)} %get-tuple-element.52), channel_id=1, source_target_pairs={{0,1},{1,0},{2,3},{3,2},{4,5},{5,4},{6,7},{7,6},{8,9},{9,8},{10,11... | collective-permute-start | bytes 7864328 | tf_op jit(solution)/shard_map/ppermute | solution.py:538
  141.7 1.3 slice.68.through_ref
  143.0 0.1 slice_reduce_fusion.2
  143.1 15.0 %within.1 = (f32[128,5120]{1,0:T(8,128)}, f32[128,5120]{1,0:T(8,128)}, f32[128,128]{1,0:T(8,128)}) custom-call(s32[2]{0:T(128)} %pad_add_fusion.half_ref, bf16[128,5376]{1,0:T(8,128)(2,1)} %xs_ref.5, bf16[8,5376]{1,0:T(8,128)(2,1)} %copy-done.1, f32[8,5376]{1,0:T(8,128)} %maximum_maximum_fusion.taps_ref.tapss_ref, f32[128,8]{1,0:T(8,128)} %get-tuple-element.38.valid_ref, ...), custom_call_target="tpu_custom_call" | custom-call | tf_op jit(solution)/shard_map/within/pallas_call | solution.py:166
  158.1 1.6 copy-done.2
  159.6 24.9 %finish.1 = (bf16[128,5120]{1,0:T(8,128)(2,1)}, bf16[128,5120]{1,0:T(8,128)(2,1)}, f32[16,5120]{1,0:T(8,128)}, f32[8,5120]{1,0:T(8,128)}, f32[8,5120]{1,0:T(8,12...) custom-call(s32[2]{0:T(128)} %pad_add_fusion.half_ref, ...), custom_call_target="tpu_custom_call" | custom-call | tf_op jit(solution)/shard_map/finish/pallas_call | solution.py:166
  184.6 0.8 slice_bitcast_fusion
  185.4 1.0 pad_maximum_fusion.2
  186.4 0.6 select_maximum_fusion
  187.0 5.0 %all-to-all-start.3 = ((f32[128,1,256]{2,1,0:T(1,128)}), f32[128,1,256]{2,1,0:T(1,128)S(1)}, u32[]{:S(2)}, u32[]{:S(2)}) async-start(f32[128,1,256]{2,1,0:T(1,128)} %bitcast.11), calls=%async_computation.3 | async-start | bytes 262144 | tf_op jit(solution)/shard_map/all_to_all | solution.py:523
  192.0 0.9 pad_maximum_fusion.1
  192.9 3.0 %collective-permute-start.3 = (f32[8,5376]{1,0:T(8,128)S(1)}, f32[8,5376]{1,0:T(8,128)S(1)}, u32[]{:S(2)}, u32[]{:S(2)}) collective-permute-start(f32[8,5376]{1,0:T(8,128)S(1)} %pad_maximum_fusion.1), channel_id=1, source_target_pairs={{1,0},{2,1},{3,2},{4,3},{5,4},{6,5},{7,6},{8,7},{9,8},{10,9},{11,1... | collective-permute-start | bytes 516104 | tf_op jit(solution)/shard_map/ppermute | solution.py:528
  195.9 1.0 constant_dynamic-update-slice_fusion.1
  196.9 0.8 slice.70
  197.8 0.7 constant_dynamic-update-slice_fusion
  198.5 0.1 slice.69
  198.6 3.4 %all-to-all-done.3 = f32[128,1,256]{2,1,0:T(1,128)S(1)} async-done(((f32[128,1,256]{2,1,0:T(1,128)}), f32[128,1,256]{2,1,0:T(1,128)S(1)}, u32[]{:S(2)}, u32[]{:S(2)}) %all-to-all-start.3) | async-done | bytes 131104 | tf_op jit(solution)/shard_map/all_to_all | solution.py:523
  201.9 0.2 reduce_sum.9
  202.1 0.7 broadcast_in_dim.18
  202.8 5.7 %all-to-all-start.4 = ((f32[128,1,256]{2,1,0:T(1,128)}), f32[128,1,256]{2,1,0:T(1,128)S(1)}, u32[]{:S(2)}, u32[]{:S(2)}) async-start(f32[128,1,256]{2,1,0:T(1,128)} %broadcast_in_dim.18), calls=%async_computation.4 | async-start | bytes 262144 | tf_op jit(solution)/shard_map/all_to_all | solution.py:523
  208.5 0.1 fusion.1
  208.6 1.2 pad_maximum_fusion
  209.8 8.7 %all-to-all-done.4 = f32[128,1,256]{2,1,0:T(1,128)S(1)} async-done(((f32[128,1,256]{2,1,0:T(1,128)}), f32[128,1,256]{2,1,0:T(1,128)S(1)}, u32[]{:S(2)}, u32[]{:S(2)}) %all-to-all-start.4) | async-done | bytes 131104 | tf_op jit(solution)/shard_map/all_to_all | solution.py:523
  218.4 0.1 broadcast_multiply_fusion
  218.6 0.2 slice_reduce_fusion
  218.8 0.5 slice_bitcast_fusion.1
  219.4 0.7 slice.79
  220.0 0.6 slice.81
  (18 shorter events, 0.1 us)
Async XLA Ops:
  5.6 7.7 %collective-permute-start = (bf16[8,5376]{1,0:T(8,128)(2,1)}, bf16[8,5376]{1,0:T(8,128)(2,1)S(1)}, u32[]{:S(2)}, u32[]{:S(2)}) collective-permute-start(bf16[8,5376]{1,0:T(8,128)(2,1)} %get-tuple-element.37), channel_id=1, source_target_pairs={{0,1},{1,2},{2,3},{3,4},{4,5},{5,6},{6,7},{7,8},{8,9},{9,10},{10,1... | collective-permute-start | bytes 258056 | tf_op jit(solution)/shard_map/ppermute | solution.py:528
  13.3 0.6 copy-start.1
  21.8 16.9 %collective-permute-start.1 = (f32[16,16,2560]{2,1,0:T(8,128)}, f32[16,16,2560]{2,1,0:T(8,128)S(1)}, u32[]{:S(2)}, u32[]{:S(2)}) collective-permute-start(f32[16,16,2560]{2,1,0:T(8,128)} %get-tuple-element.49), channel_id=1, source_target_pairs={{0,1},{1,0},{2,3},{3,2},{4,5},{5,4},{6,7},{7,6},{8,9},{9,8},{10,11... | collective-permute-start | bytes 7864328 | tf_op jit(solution)/shard_map/ppermute | solution.py:538
  21.9 16.9 %all-to-all-start = ((f32[32,1,128]{2,1,0:T(1,128)}), f32[32,1,128]{2,1,0:T(1,128)S(1)}, u32[]{:S(2)}, u32[]{:S(2)}) async-start(f32[32,1,128]{2,1,0:T(1,128)} %bitcast.8), calls=%async_computation | async-start | bytes 32768 | tf_op jit(solution)/shard_map/all_to_all | solution.py:523
  38.7 0.6 copy-start.4
  38.7 1.5 copy-start
  130.3 12.7 %copy-start.5 = (f32[8,128]{1,0:T(8,128)S(1)}, f32[8,128]{1,0:T(8,128)}, u32[]{:S(2)}) copy-start(f32[8,128]{1,0:T(8,128)} %get-tuple-element.63) | copy-start | bytes 12292
  139.2 18.9 %collective-permute-start.2 = (f32[16,16,2560]{2,1,0:T(8,128)}, f32[16,16,2560]{2,1,0:T(8,128)S(1)}, u32[]{:S(2)}, u32[]{:S(2)}) collective-permute-start(f32[16,16,2560]{2,1,0:T(8,128)} %get-tuple-element.52), channel_id=1, source_target_pairs={{0,1},{1,0},{2,3},{3,2},{4,5},{5,4},{6,7},{7,6},{8,9},{9,8},{10,11... | collective-permute-start | bytes 7864328 | tf_op jit(solution)/shard_map/ppermute | solution.py:538
  158.1 1.6 copy-start.2
  184.6 13.9 %copy-start.3 = (bf16[128,5120]{1,0:T(8,128)(2,1)S(1)}, bf16[128,5120]{1,0:T(8,128)(2,1)}, u32[]{:S(2)}) copy-start(bf16[128,5120]{1,0:T(8,128)(2,1)} %get-tuple-element.57) | copy-start | bytes 3932164
  187.0 14.9 %all-to-all-start.3 = ((f32[128,1,256]{2,1,0:T(1,128)}), f32[128,1,256]{2,1,0:T(1,128)S(1)}, u32[]{:S(2)}, u32[]{:S(2)}) async-start(f32[128,1,256]{2,1,0:T(1,128)} %bitcast.11), calls=%async_computation.3 | async-start | bytes 262144 | tf_op jit(solution)/shard_map/all_to_all | solution.py:523
  192.9 15.5 %collective-permute-start.3 = (f32[8,5376]{1,0:T(8,128)S(1)}, f32[8,5376]{1,0:T(8,128)S(1)}, u32[]{:S(2)}, u32[]{:S(2)}) collective-permute-start(f32[8,5376]{1,0:T(8,128)S(1)} %pad_maximum_fusion.1), channel_id=1, source_target_pairs={{1,0},{2,1},{3,2},{4,3},{5,4},{6,5},{7,6},{8,7},{9,8},{10,9},{11,1... | collective-permute-start | bytes 516104 | tf_op jit(solution)/shard_map/ppermute | solution.py:528
  202.8 15.6 %all-to-all-start.4 = ((f32[128,1,256]{2,1,0:T(1,128)}), f32[128,1,256]{2,1,0:T(1,128)S(1)}, u32[]{:S(2)}, u32[]{:S(2)}) async-start(f32[128,1,256]{2,1,0:T(1,128)} %broadcast_in_dim.18), calls=%async_computation.4 | async-start | bytes 262144 | tf_op jit(solution)/shard_map/all_to_all | solution.py:523

commit v3 on v2

--- a/solution.py
+++ b/solution.py
@@ -24,6 +24,7 @@
 EXACT = lax.Precision.HIGHEST
 HALF_TILES = TILES // 2
 VMEM_BYTES = 60 << 20
+MESH = pl.DeviceIdType.MESH
 
 
 def iota(shape, axis):
@@ -47,6 +48,13 @@
     return lax.dot_general(
         a, b, (((1,), (0,)), ((), ())), precision=EXACT, preferred_element_type=F32
     )
+
+
+def spread_exact(rows, one_hot):
+    first, rest = rows.astype(BF16), rows
+    rest = rest - first.astype(F32)
+    second, third = halves(rest)
+    return mm(first, one_hot) + mm(second, one_hot) + mm(third, one_hot)
 
 
 def interleave(group, late):
@@ -82,8 +90,56 @@
     return 1.0 / (1.0 + jnp.exp(-v))
 
 
-def head_kernel(raw_in_ref, small_ref, row_ref, end_ref, run_ref, runT_ref, dt_ref, dtT_ref, both_ref, sig_ref,
-                sigsum_ref, through_ref, mask_ref, valid_ref, keep_ref, tail_ref, raw):
+def greet(axes):
+    barrier = pltpu.get_barrier_semaphore()
+    for axis, size in axes:
+        place = lax.axis_index(axis)
+
+        def signal(k, carry):
+            pl.semaphore_signal(
+                barrier, inc=1, device_id={axis: lax.rem(place + k, size)}, device_id_type=MESH
+            )
+            return carry
+
+        lax.fori_loop(1, size, signal, 0)
+    pl.semaphore_wait(barrier, sum(size - 1 for _, size in axes))
+
+
+def remote(source, target, send, receive, axis, peer):
+    return pltpu.make_async_remote_copy(
+        src_ref=source, dst_ref=target, send_sem=send, recv_sem=receive, device_id={axis: peer}, device_id_type=MESH
+    )
+
+
+def send_all(axis, size, source, target, send, receive):
+    place = lax.axis_index(axis)
+
+    def start(k, carry):
+        peer = lax.rem(place + k, size)
+        remote(source(peer), target.at[place], send.at[peer], receive.at[place], axis, peer).start()
+        return carry
+
+    lax.fori_loop(1, size, start, 0)
+
+
+def wait_all(axis, size, source, target, send, receive):
+    place = lax.axis_index(axis)
+
+    def wait(k, carry):
+        peer = lax.rem(place + k, size)
+        copy = remote(source(peer), target.at[peer], send.at[peer], receive.at[peer], axis, peer)
+        copy.wait_send()
+        copy.wait_recv()
+        return carry
+
+    lax.fori_loop(1, size, wait, 0)
+
+
+def head_kernel(shards, raw_in_ref, small_ref, row_ref, end_ref, run_ref, runT_ref, dt_ref, dtT_ref, both_ref, sig_ref,
+                sigsum_ref, through_ref, mask_ref, valid_ref, keep_ref, tail_ref, own_ref, raw, own, slots, tail_out, send,
+                receive, tail_send, tail_receive):
+    greet((("seq", shards),))
+    place = lax.axis_index("seq")
     reset_row = row_ref[...].astype(F32)
     token, other = iota((ROWS, ROWS), 0), iota((ROWS, ROWS), 1)
     reset_col = jnp.sum(jnp.where(token == other, reset_row, 0.0), axis=1, keepdims=True)
@@ -103,15 +159,27 @@
         token == ROWS - 1, 1.0, jnp.where(token == ROWS - 2, one_on, jnp.where(token == ROWS - 3, one_on * two_on, 0.0))
     )[ROWS - 8 :]
     keep_ref[...] = keep
-    tail_ref[...] = (end_ref[8:, :].astype(F32) * keep[:, 0:1]).astype(BF16)
+    tail_out[...] = (end_ref[8:, :].astype(F32) * keep[:, 0:1]).astype(BF16)
+    onward = remote(tail_out, tail_ref, tail_send, tail_receive, "seq", lax.rem(place + 1, shards))
+
+    @pl.when(place < shards - 1)
+    def _():
+        onward.start()
 
     raw[...] = jnp.zeros_like(raw)
-    raw[:, :HEADS] = raw_in_ref[...]
-    biased = raw[...] + small_ref[0:1, :]
+    raw[:HEADS, :] = raw_in_ref[...]
+    biased = raw[...].T + small_ref[0:1, :]
     dt = jnp.maximum(biased, 0.0) + jnp.log1p(jnp.exp(-jnp.abs(biased)))
     decay = -jnp.exp(small_ref[1:2, :]) * dt
     lower = jnp.where(low, 1.0, 0.0)
     running = exact(lower, decay)
+    last = running[ROWS - 1 : ROWS]
+    count = segment_col[ROWS - 1 : ROWS]
+    untouched = jnp.where(segment_col == 0.0, 1.0, 0.0)
+    entry = jnp.exp(running) * untouched
+    own[...] = jnp.broadcast_to(entry[ROWS - 1 : ROWS], own.shape)
+    own_ref[...] = own[...]
+    send_all("seq", shards, lambda peer: own, slots, send, receive)
     sig = sigmoid(biased)
     sig_ref[...] = sig
     sigsum_ref[...] = exact(lower, sig)
@@ -119,19 +187,30 @@
     runT_ref[...] = running.T
     dt_ref[...] = dt
     dtT_ref[...] = dt.T
-    last = running[ROWS - 1 : ROWS]
-    count = segment_col[ROWS - 1 : ROWS]
-    untouched = jnp.where(segment_col == 0.0, 1.0, 0.0)
-    entry = jnp.exp(running) * untouched
     leave = jnp.exp(last - running) * jnp.where(segment_col == count, 1.0, 0.0) * dt
     for at, part in ((0, leave), (ROWS, entry)):
         first, second = halves(part)
         both_ref[at : at + ROWS, :LANES] = first
         both_ref[at : at + ROWS, LANES:] = second
-    through_ref[...] = jnp.broadcast_to(entry[ROWS - 1 : ROWS], through_ref.shape)
-
-
-def head_stage(shards, raw, small, row, conv_input):
+    slots[place] = own[...]
+    wait_all("seq", shards, lambda peer: own, slots, send, receive)
+    for shard in range(shards):
+        through_ref[shard : shard + 1, :] = slots[shard, 0:1, :]
+
+    @pl.when(place < shards - 1)
+    def _():
+        onward.wait_send()
+
+    @pl.when(place > 0)
+    def _():
+        onward.wait_recv()
+
+    @pl.when(place == 0)
+    def _():
+        tail_ref[...] = jnp.zeros_like(tail_ref)
+
+
+def head_stage(shards, raw, small, row, end):
     square = jax.ShapeDtypeStruct((ROWS, LANES), F32)
     shapes = (
         square, square, square, square,
@@ -142,20 +221,24 @@
         jax.ShapeDtypeStruct((ROWS, 8), F32),
         jax.ShapeDtypeStruct((8, LANES), F32),
         jax.ShapeDtypeStruct((8, CH), BF16),
-    )
+        jax.ShapeDtypeStruct((8, LANES), F32),
+    )
+    in_vmem = pl.BlockSpec(memory_space=pltpu.VMEM)
     return pl.pallas_call(
-        head_kernel,
-        grid=(1,),
-        in_specs=[
-            whole(raw.shape), whole((8, LANES)), whole((1, ROWS)),
-            pl.BlockSpec((16, CH), lambda *at: (ROWS // 16 - 1, 0)),
+        functools.partial(head_kernel, shards),
+        in_specs=[in_vmem] * 4,
+        out_specs=[in_vmem] * len(shapes),
+        out_shape=shapes,
+        scratch_shapes=[
+            pltpu.VMEM((ROWS, LANES), F32), pltpu.VMEM((8, LANES), F32), pltpu.VMEM((shards, 8, LANES), F32),
+            pltpu.VMEM((8, CH), BF16), pltpu.SemaphoreType.DMA((shards,)), pltpu.SemaphoreType.DMA((shards,)),
+            pltpu.SemaphoreType.DMA, pltpu.SemaphoreType.DMA,
         ],
-        out_specs=[whole(shape.shape) for shape in shapes],
-        out_shape=shapes,
-        scratch_shapes=[pltpu.VMEM((ROWS, LANES), F32)],
-        compiler_params=pltpu.CompilerParams(vmem_limit_bytes=VMEM_BYTES),
+        compiler_params=pltpu.CompilerParams(
+            vmem_limit_bytes=VMEM_BYTES, collective_id=0, has_side_effects=True
+        ),
         name="heads",
-    )(raw, small, row, conv_input)
+    )(raw, small, row, end)
 
 
 def whole(shape):
@@ -301,8 +384,7 @@
 
 
 def chip_decay(half_ref, through_ref, rows):
-    one_hot = head_columns(tile_at(pl.program_id(0), half_ref)).astype(F32)
-    return exact(through_ref[rows, :], one_hot)
+    return spread_exact(through_ref[rows, :], head_columns(tile_at(pl.program_id(0), half_ref)))
 
 
 def own_pair(half_ref):
@@ -426,7 +508,7 @@
     states_hi, states_lo = halves(states)
     read = mm(lhs_hi[...], states_hi) + mm(lhs_hi[...], states_lo) + mm(lhs_lo[...], states_hi)
     one_hot = head_columns(here)
-    gain = exact(small_ref[...], one_hot.astype(F32))[2:3]
+    gain = spread_exact(small_ref[...], one_hot)[2:3]
     through_state = out_in_ref[...] + entry * read[:ROWS]
     out_ref[...] = (through_state + gain * act).astype(BF16)
     act_grad_late = leave * read[ROWS:]
@@ -519,19 +601,104 @@
     )
 
 
-def exchange(array, axis):
-    return lax.all_to_all(array, axis, 0, 0, tiled=True)
-
-
-def neighbour(array, by):
-    size = lax.axis_size("seq")
-    return lax.ppermute(array, "seq", [(i, i + by) for i in range(size) if 0 <= i + by < size])
-
-
-def total_over_all(flat):
-    size = lax.axis_size("dp") * lax.axis_size("seq")
-    piece = exchange(flat.reshape(size, flat.shape[0] // size), ("dp", "seq")).sum(0)
-    return exchange(jnp.broadcast_to(piece[None], (size,) + piece.shape), ("dp", "seq")).reshape(-1)
+def total_kernel(shards, groups, scale, taps_ref, small_ref, heads_ref, borrowed_ref, borroweds_ref, end_ref, ends_ref,
+                 keep_ref, weight_ref, bias_ref, heads_out_ref, last_ref,
+                 parts, slots, piece, dp_slots, result, got, got_small, send, receive, dp_send, dp_receive, back_send,
+                 back_receive, rows_send, rows_receive):
+    greet((("seq", shards), ("dp", groups)))
+    place, group = lax.axis_index("seq"), lax.axis_index("dp")
+    before = lax.rem(place + shards - 1, shards)
+    returns = [
+        remote(borrowed_ref, got, rows_send.at[0], rows_receive.at[0], "seq", before),
+        remote(borroweds_ref, got_small, rows_send.at[1], rows_receive.at[1], "seq", before),
+    ]
+    wide = CH // LANES
+    parts[...] = jnp.zeros_like(parts)
+    for at in range(wide + 1):
+        if at < INNER // LANES:
+            block = taps_ref[:, LANES * at : LANES * (at + 1)]
+        elif at < wide:
+            block = small_ref[:, LANES * at - INNER : LANES * (at + 1) - INNER]
+        else:
+            block = heads_ref[...]
+        parts[at % shards, 8 * (at // shards) : 8 * (at // shards) + 8, :] = block
+    send_all("seq", shards, lambda peer: parts.at[peer], slots, send, receive)
+
+    @pl.when(place > 0)
+    def _():
+        for copy in returns:
+            copy.start()
+
+    slots[place] = parts[place]
+    wait_all("seq", shards, lambda peer: parts.at[peer], slots, send, receive)
+    piece[...] = jnp.sum(slots[...], axis=0)
+    send_all("dp", groups, lambda peer: piece, dp_slots, dp_send, dp_receive)
+    dp_slots[group] = piece[...]
+    wait_all("dp", groups, lambda peer: piece, dp_slots, dp_send, dp_receive)
+    piece[...] = jnp.sum(dp_slots[...], axis=0) * scale
+    send_all("seq", shards, lambda peer: piece, result, back_send, back_receive)
+    result[place] = piece[...]
+
+    @pl.when(place > 0)
+    def _():
+        for copy in returns:
+            copy.wait_send()
+
+    rows = 8 - CONV + 1
+
+    @pl.when(place < shards - 1)
+    def _():
+        for copy in returns:
+            copy.wait_recv()
+        keep = keep_ref[:, 0:1]
+        for lanes, source, end in ((slice(0, INNER), got, end_ref), (slice(INNER, CH), got_small, ends_ref)):
+            last_ref[:8, lanes] = end[:8, :].astype(BF16)
+            late = iota(source.shape, 0) >= rows
+            last_ref[8:, lanes] = (end[8:, :] + jnp.where(late, source[...] * keep, 0.0)).astype(BF16)
+
+    @pl.when(place == shards - 1)
+    def _():
+        last_ref[:, :INNER] = end_ref[...].astype(BF16)
+        last_ref[:, INNER:] = ends_ref[...].astype(BF16)
+
+    wait_all("seq", shards, lambda peer: piece, result, back_send, back_receive)
+    for at in range(wide + 1):
+        block = result[at % shards, 8 * (at // shards) : 8 * (at // shards) + 8, :]
+        if at < wide:
+            weight_ref[:, LANES * at : LANES * (at + 1)] = block[:CONV]
+            bias_ref[:, LANES * at : LANES * (at + 1)] = block[CONV : CONV + 1]
+        else:
+            heads_out_ref[...] = block
+
+
+def total_stage(shards, groups, scale, *operands):
+    depth = 8 * pl.cdiv(CH // LANES + 1, shards)
+    in_vmem = pl.BlockSpec(memory_space=pltpu.VMEM)
+    shapes = (
+        jax.ShapeDtypeStruct((CONV, CH), F32),
+        jax.ShapeDtypeStruct((1, CH), F32),
+        jax.ShapeDtypeStruct((8, LANES), F32),
+        jax.ShapeDtypeStruct((16, CH), BF16),
+    )
+    dma = pltpu.SemaphoreType.DMA
+    return pl.pallas_call(
+        functools.partial(total_kernel, shards, groups, scale),
+        in_specs=[in_vmem] * len(operands),
+        out_specs=[in_vmem] * len(shapes),
+        out_shape=shapes,
+        scratch_shapes=[
+            pltpu.VMEM((shards, depth, LANES), F32), pltpu.VMEM((shards, depth, LANES), F32),
+            pltpu.VMEM((depth, LANES), F32), pltpu.VMEM((groups, depth, LANES), F32),
+            pltpu.VMEM((shards, depth, LANES), F32),
+            pltpu.VMEM((8, INNER), F32), pltpu.VMEM((8, 2 * STATE), F32),
+            dma((shards,)), dma((shards,)), dma((groups,)), dma((groups,)), dma((shards,)), dma((shards,)),
+            dma((2,)), dma((2,)),
+        ],
+        compiler_params=pltpu.CompilerParams(
+            vmem_limit_bytes=VMEM_BYTES, collective_id=1, has_side_effects=True
+        ),
+        name="totals",
+    )(*operands)
 
 
 def swap(array):
@@ -553,11 +720,9 @@
     taps = jnp.concatenate([conv_weight, conv_bias[None], jnp.zeros((3, CH), F32)], axis=0)
     small = jnp.pad(jnp.stack([dt_bias, a_log, skip_gain]), ((0, 5), (0, LANES - HEADS)))
 
-    run, runT, dt, dtT, both, sig, sigsum, through, mask, valid, keep, tail = head_stage(
-        shards, dt_raw, small, doc_start[None], conv_input
-    )
-    tail = neighbour(tail, 1)
-    all_through = exchange(through, "seq")
+    run, runT, dt, dtT, both, sig, sigsum, all_through, mask, valid, keep, tail, through = head_stage(
+        shards, dt_raw.T, small, doc_start[None], conv_input[ROWS - 16 :]
+    )
     theirs, bc = local_stage(group, other_half, conv_input, tail, taps, valid, cotangent, both)
     other = swap(theirs)
     mine, _ = local_stage(group, half, conv_input, tail, taps, valid, cotangent, both)
@@ -570,24 +735,17 @@
     pairs_b = swap(pairs_b)
     out, grad, end, borrowed, taps_grad, grads, ends, borroweds, tapss_grad, heads = finish_stage(
         group, half, conv_input, tail, taps, valid, cotangent, both, out_in, grad_in, pairs_a, pairs_b, bc, score_grad,
-        run, dt, sig, sigsum, small, through[:8],
-    )
-    keep = keep[8 - CONV + 1 :, 0:1]
-    returned = neighbour(jnp.concatenate([borrowed, borroweds], axis=1), -1)[8 - CONV + 1 :]
-    tail_rows = jnp.concatenate([end, ends], axis=1)
-    tail_rows = jnp.concatenate([tail_rows[: 16 - CONV + 1], tail_rows[16 - CONV + 1 :] + returned * keep])
+        run, dt, sig, sigsum, small, through,
+    )
+    groups = lax.axis_size("dp")
+    weight_grad, bias_grad, heads, last = total_stage(
+        shards, groups, float(groups * shards * ROWS) ** (-0.5), taps_grad, tapss_grad, heads, borrowed, borroweds,
+        end, ends, keep,
+    )
     whole_grad = jnp.concatenate(
-        [jnp.concatenate([grad[: ROWS - 16], grads[: ROWS - 16]], axis=1), tail_rows.astype(BF16)], axis=0
-    )
-    params = jnp.concatenate([taps_grad[:5], tapss_grad[:5]], axis=1).reshape(-1)
-    params = jnp.concatenate([params, heads[:3].reshape(-1)])
-    size = lax.axis_size("dp") * shards
-    used = params.shape[0]
-    params = jnp.pad(params, (0, -used % (size * LANES)))
-    params = total_over_all(params) * float(size * ROWS) ** (-0.5)
-    heads = params[5 * CH : 5 * CH + 3 * LANES].reshape(3, LANES)[:, :HEADS]
-    params = params[: 5 * CH].reshape(5, CH)
-    return (out, whole_grad, params[:CONV], params[CONV], heads[0], heads[1], heads[2])
+        [jnp.concatenate([grad[: ROWS - 16], grads[: ROWS - 16]], axis=1), last], axis=0
+    )
+    return (out, whole_grad, weight_grad, bias_grad[0], heads[0, :HEADS], heads[1, :HEADS], heads[2, :HEADS])
 
 
 def solution(mesh):

time: 222 us -> 211 us (0.950)
  Pallas kernels: 79.8 us -> 114 us
  starting transfers between devices: 29.1 us -> 2.69 us
  waiting for transfers between devices: 12 us -> 0.01 us
  local copies, waits for them, and re-layouts: 13.6 us -> 9.57 us
    pallas_call x1 -> x2, Pallas kernels: 2.21 us -> 37.6 us  [the longest x1 21.8 us: total_stage(): pl.pallas_call(functools.partial(total_kernel, shards, groups, scale), in...]
    all_to_all x3 -> x0, starting transfers between devices: 18.9 us -> none  [exchange(): return lax.all_to_all(array, axis, 0, 0, tiled=True)]
    all_to_all x3 -> x0, waiting for transfers between devices: 12 us -> none  [exchange(): return lax.all_to_all(array, axis, 0, 0, tiled=True)]
    ppermute x2 -> x0, starting transfers between devices: 7.58 us -> none  [neighbour(): lax.ppermute(array, 'seq', [(i, i + by) for i in range(size) if 0 <= i +...]
    concatenate x3 -> x0, other arithmetic: 2.54 us -> none  [the longest x1 0.95 us: on_device(): jnp.concatenate([taps_grad[:5], tapss_grad[:5]], axis=1).reshape(-1)]
    unnamed x14 -> x7, local copies, waits for them, and re-layouts: 6.18 us -> 3.66 us
  transfers between devices with their start and end apart: 7 -> 2, of which waited for: 2 -> 0; matrix products, arithmetic and copies ran while one was open for 5% -> 0% of each run, Pallas kernels for 10% -> 11%
where the time goes in v3:
time: 211 us; the launch traced here: 210 us
  Pallas kernels  114 us (54%)
  blocking collectives  75.9 us (36%)
  local copies, waits for them, and re-layouts  9.57 us (5%)
  other arithmetic  7.59 us (4%)
  starting transfers between devices  2.69 us (1%)
    pallas_call x7, Pallas kernels, call(): pl.pallas_call(kernel, grid_spec=pltpu.PrefetchScalarGridSpec(num_scalar_...  76 us
    all_to_all x2, blocking collectives, between_chips(): lax.all_to_all(array, 'seq', 0, 0, axis_index_groups=groups, tiled=True)  75.9 us
    pallas_call x1, Pallas kernels, total_stage(): pl.pallas_call(functools.partial(total_kernel, shards, groups, scale), in...  21.8 us
    pallas_call x1, Pallas kernels, head_stage(): pl.pallas_call(functools.partial(head_kernel, shards), in_specs=[in_vmem]...  15.8 us
  transfers between devices with their start and end apart: 2, of which 0 were waited for; matrix products, arithmetic and copies ran while one was open for 0% of the time, Pallas kernels for 11%

profile of v3, /device:TPU:1, one launch (start us, length us, event | category | flops | bytes accessed | tf_op | source)
XLA Modules:
  0.0 210.1 jit_solution(17804787932354202916)
XLA Ops:
  0.6 0.8 broadcast_in_dim.10
  1.4 1.6 slice.18.end_ref
  3.0 0.6 pad_add_fusion.1.half_ref
  3.6 0.1 pad.12.clone
  3.7 1.3 select_maximum_fusion.small_ref
  5.0 1.7 maximum_maximum_fusion.taps_ref.tapss_ref
  6.6 15.8 %heads.1 = (f32[128,128]{1,0:T(8,128)}, f32[128,128]{1,0:T(8,128)}, f32[128,128]{1,0:T(8,128)}, f32[128,128]{1,0:T(8,128)}, bf16[256,256]{1,0:T(8,128)(2,1)}, /*...) custom-call(f32[80,128]{1,0:T(8,128)} %bitcast.14, ...), custom_call_target="tpu_custom_call" | custom-call | tf_op jit(solution)/shard_map/heads/pallas_call | solution.py:227
  22.5 7.9 %local.2 = (f32[16,16,2560]{2,1,0:T(8,128)}, f32[128,256]{1,0:T(8,128)}) custom-call(s32[2]{0:T(128)} %pad_add_fusion.1.half_ref, bf16[128,5376]{1,0:T(8,128)(2,1)} %xs_ref.5, bf16[8,5376]{1,0:T(8,128)(2,1)} %get-tuple-element.42.tail_ref.tails_ref, f32[8,5376]{1,0:T(8,128)} %maximum_maximum_fusion.taps_ref.tapss_ref, bf16[128,5376]{1,0:T(8,128)(2,1)} %xs_ref.5, ...), custom_call_target="tpu_custom_call" | custom-call | tf_op jit(solution)/shard_map/local/pallas_call | solution.py:249
  30.4 0.4 collective-permute-start
  30.8 0.6 pad_add_fusion.half_ref
  31.4 7.9 %local.3 = (f32[16,16,2560]{2,1,0:T(8,128)}, f32[128,256]{1,0:T(8,128)}) custom-call(s32[2]{0:T(128)} %pad_add_fusion.half_ref, bf16[128,5376]{1,0:T(8,128)(2,1)} %xs_ref.5, bf16[8,5376]{1,0:T(8,128)(2,1)} %get-tuple-element.42.tail_ref.tails_ref, f32[8,5376]{1,0:T(8,128)} %maximum_maximum_fusion.taps_ref.tapss_ref, bf16[128,5376]{1,0:T(8,128)(2,1)} %xs_ref.5, ...), custom_call_target="tpu_custom_call" | custom-call | tf_op jit(solution)/shard_map/local/pallas_call | solution.py:249
  39.2 0.0 collective-permute-done.other_ref
  39.2 0.0 copy-start
  39.2 1.5 copy-done
  40.7 6.6 %join.1 = f32[16,16,2560]{2,1,0:T(8,128)} custom-call(s32[2]{0:T(128)} %pad_add_fusion.half_ref, f32[16,16,2560]{2,1,0:T(8,128)} %get-tuple-element.53.mine_ref, f32[16,16,2560]{2,1,0:T(8,128)} %copy-done, f32[32,128]{1,0:T(8,128)} %get-tuple-element.55.through_ref), custom_call_target="tpu_custom_call" | custom-call | tf_op jit(solution)/shard_map/join/pallas_call | solution.py:249
  47.3 38.8 %all_to_all.10.pair_ref = f32[16,16,2560]{2,1,0:T(8,128)} all-to-all(f32[16,16,2560]{2,1,0:T(8,128)} %join.1), channel_id=1, replica_groups={{0,2,4,6,8,10,12,14,16,18,20,22,24,26,28,30},{1,3,5,7,9,11,13,15,17,19,..., dimensions={0} | all-to-all | bytes 5242880 | tf_op jit(solution)/shard_map/all_to_all | solution.py:711
  86.0 6.0 %carry.1 = f32[16,16,2560]{2,1,0:T(8,128)} custom-call(s32[2]{0:T(128)} %pad_add_fusion.half_ref, f32[16,16,2560]{2,1,0:T(8,128)} %all_to_all.10.pair_ref, f32[32,128]{1,0:T(8,128)} %get-tuple-element.55.through_ref), custom_call_target="tpu_custom_call" | custom-call | tf_op jit(solution)/shard_map/carry/pallas_call | solution.py:249
  92.0 37.1 %all_to_all.11.chip_ref = f32[16,16,2560]{2,1,0:T(8,128)} all-to-all(f32[16,16,2560]{2,1,0:T(8,128)} %carry.1), channel_id=1, replica_groups={{0,2,4,6,8,10,12,14,16,18,20,22,24,26,28,30},{1,3,5,7,9,11,13,15,17,19,..., dimensions={0} | all-to-all | bytes 5242880 | tf_op jit(solution)/shard_map/all_to_all | solution.py:711
  129.1 8.6 %part.1 = (f32[16,16,2560]{2,1,0:T(8,128)}, f32[16,16,2560]{2,1,0:T(8,128)}) custom-call(s32[2]{0:T(128)} %pad_add_fusion.half_ref, f32[16,16,2560]{2,1,0:T(8,128)} %all_to_all.11.chip_ref, f32[16,16,2560]{2,1,0:T(8,128)} %get-tuple-element.53.mine_ref, f32[16,16,2560]{2,1,0:T(8,128)} %copy-done, f32[32,128]{1,0:T(8,128)} %get-tuple-element.55.through_ref), custom_call_target="tpu_custom_call" | custom-call | tf_op jit(solution)/shard_map/part/pallas_call | solution.py:249
  137.7 2.3 %collective-permute-start.1 = (f32[16,16,2560]{2,1,0:T(8,128)}, f32[16,16,2560]{2,1,0:T(8,128)S(1)}, u32[]{:S(2)}, u32[]{:S(2)}) collective-permute-start(f32[16,16,2560]{2,1,0:T(8,128)} %get-tuple-element.57), channel_id=1, source_target_pairs={{0,1},{1,0},{2,3},{3,2},{4,5},{5,4},{6,7},{7,6},{8,9},{9,8},{10,11... | collective-permute-start | bytes 7864328 | tf_op jit(solution)/shard_map/ppermute | solution.py:705
  140.0 14.9 %within.1 = (f32[128,5120]{1,0:T(8,128)}, f32[128,5120]{1,0:T(8,128)}, f32[128,128]{1,0:T(8,128)}) custom-call(s32[2]{0:T(128)} %pad_add_fusion.half_ref, bf16[128,5376]{1,0:T(8,128)(2,1)} %xs_ref.5, bf16[8,5376]{1,0:T(8,128)(2,1)} %get-tuple-element.42.tail_ref.tails_ref, f32[8,5376]{1,0:T(8,128)} %maximum_maximum_fusion.taps_ref.tapss_ref, ...), custom_call_target="tpu_custom_call" | custom-call | tf_op jit(solution)/shard_map/within/pallas_call | solution.py:249
  155.0 0.0 collective-permute-done.1.pair_b_ref
  155.0 0.0 copy-start.1
  155.0 1.5 copy-done.1
  156.5 24.1 %finish.1 = (bf16[128,5120]{1,0:T(8,128)(2,1)}, bf16[128,5120]{1,0:T(8,128)(2,1)}, f32[16,5120]{1,0:T(8,128)}, f32[8,5120]{1,0:T(8,128)}, f32[8,5120]{1,0:T(8,12...) custom-call(s32[2]{0:T(128)} %pad_add_fusion.half_ref, ...), custom_call_target="tpu_custom_call" | custom-call | tf_op jit(solution)/shard_map/finish/pallas_call | solution.py:249
  180.6 0.8 slice.20
  181.5 21.8 %totals.1 = (f32[4,5376]{1,0:T(4,128)}, f32[1,5376]{1,0:T(1,128)}, f32[8,128]{1,0:T(8,128)}, bf16[16,5376]{1,0:T(8,128)(2,1)}) custom-call(f32[8,5120]{1,0:T(8,128)} %get-tuple-element.65.taps_ref, f32[8,256]{1,0:T(8,128)} %get-tuple-element.66.small_ref, f32[8,128]{1,0:T(8,128)} %get-tuple-element.67.heads_ref, f32[8,5120]{1,0:T(8,128)} %get-tuple-element.68.borrowed_ref, ...), custom_call_target="tpu_custom_call" | custom-call | tf_op jit(solution)/shard_map/totals/pallas_call | solution.py:684
  203.3 0.0 copy-start.2
  203.3 1.3 slice_bitcast_fusion
  204.6 1.3 slice.19
  205.9 1.4 reduce
  207.3 2.1 pad_maximum_fusion
  209.4 0.0 copy-done.2
  209.4 0.6 copy.17
  (1 shorter events, 0.0 us)
Async XLA Ops:
  30.4 8.8 %collective-permute-start = (f32[16,16,2560]{2,1,0:T(8,128)}, f32[16,16,2560]{2,1,0:T(8,128)S(1)}, u32[]{:S(2)}, u32[]{:S(2)}) collective-permute-start(f32[16,16,2560]{2,1,0:T(8,128)} %get-tuple-element.54), channel_id=1, source_target_pairs={{0,1},{1,0},{2,3},{3,2},{4,5},{5,4},{6,7},{7,6},{8,9},{9,8},{10,11... | collective-permute-start | bytes 7864328 | tf_op jit(solution)/shard_map/ppermute | solution.py:705
  39.2 1.5 copy-start
  137.7 17.2 %collective-permute-start.1 = (f32[16,16,2560]{2,1,0:T(8,128)}, f32[16,16,2560]{2,1,0:T(8,128)S(1)}, u32[]{:S(2)}, u32[]{:S(2)}) collective-permute-start(f32[16,16,2560]{2,1,0:T(8,128)} %get-tuple-element.57), channel_id=1, source_target_pairs={{0,1},{1,0},{2,3},{3,2},{4,5},{5,4},{6,7},{7,6},{8,9},{9,8},{10,11... | collective-permute-start | bytes 7864328 | tf_op jit(solution)/shard_map/ppermute | solution.py:705
  155.0 1.5 copy-start.1
  203.3 6.2 %copy-start.2 = (f32[4,5376]{1,0:T(4,128)S(1)}, f32[4,5376]{1,0:T(4,128)}, u32[]{:S(2)}) copy-start(f32[4,5376]{1,0:T(4,128)} %get-tuple-element.89) | copy-start | bytes 258052

commit v4 on v3

--- a/solution.py
+++ b/solution.py
@@ -245,13 +245,14 @@
     return pl.BlockSpec(shape, lambda *at: (0,) * len(shape))
 
 
-def call(kernel, name, half, grid, in_specs, out_specs, out_shape, scratch_shapes, operands):
+def call(kernel, name, half, grid, in_specs, out_specs, out_shape, scratch_shapes, operands, aliases={}):
     return pl.pallas_call(
         kernel,
         grid_spec=pltpu.PrefetchScalarGridSpec(
             num_scalar_prefetch=1, grid=(grid,), in_specs=in_specs, out_specs=out_specs, scratch_shapes=scratch_shapes
         ),
         out_shape=out_shape,
+        input_output_aliases=aliases,
         compiler_params=pltpu.CompilerParams(vmem_limit_bytes=VMEM_BYTES),
         name=name,
     )(half, *operands)
@@ -402,7 +403,7 @@
 
 def join_kernel(group, half_ref, mine_ref, other_ref, through_ref, out_ref):
     earlier, later = even_odd(half_ref, through_ref)
-    even = half_ref[0] == 0
+    even = half_ref[2] == 0
     mine, other = mine_ref[...], other_ref[...]
     first, second = jnp.where(even, mine, other), jnp.where(even, other, mine)
     out_ref[:, :group, :] = later * first[:, :group] + second[:, :group]
@@ -414,28 +415,6 @@
     return call(
         functools.partial(join_kernel, group), "join", half, HALF_TILES,
         [spec, spec, whole(through.shape)], spec, jax.ShapeDtypeStruct(mine.shape, F32), [], (mine, other, through),
-    )
-
-
-def part_kernel(group, half_ref, chip_ref, mine_ref, other_ref, through_ref, keep_ref, send_ref):
-    earlier, later = even_odd(half_ref, through_ref)
-    even = half_ref[0] == 0
-    chip, mine, other = chip_ref[...], mine_ref[...], other_ref[...]
-    state, adjoint = chip[:, :group], chip[:, group:]
-    state_later = earlier * state + jnp.where(even, mine[:, :group], other[:, :group])
-    adjoint_earlier = later * adjoint + jnp.where(even, other[:, group:], mine[:, group:])
-    keep_ref[:, :group, :] = jnp.where(even, state, state_later)
-    keep_ref[:, group:, :] = jnp.where(even, adjoint_earlier, adjoint)
-    send_ref[:, :group, :] = jnp.where(even, state_later, state)
-    send_ref[:, group:, :] = jnp.where(even, adjoint, adjoint_earlier)
-
-
-def part_stage(group, half, chip, mine, other, through):
-    spec = pair_spec(mine.shape, True)
-    shape = jax.ShapeDtypeStruct(mine.shape, F32)
-    return call(
-        functools.partial(part_kernel, group), "part", half, HALF_TILES,
-        [spec, spec, spec, whole(through.shape)], [spec, spec], (shape, shape), [], (chip, mine, other, through),
     )
 
 
@@ -477,12 +456,16 @@
     return total, jnp.concatenate(parts, axis=0)
 
 
-def finish_kernel(group, half_ref, x_ref, tail_ref, taps_ref, xs_ref, tails_ref, tapss_ref, valid_ref, cot_ref, both_ref,
-                  out_in_ref, grad_in_ref, pair_a_ref, pair_b_ref, bc_ref, score_grad_ref, run_ref, dt_ref, sig_ref,
-                  sigsum_ref, small_ref, through_ref,
-                  out_ref, grad_ref, end_ref, borrowed_ref, taps_grad_ref, grads_ref, ends_ref, borroweds_ref,
-                  tapss_grad_ref, heads_ref,
-                  lhs_hi, lhs_lo, bc_grad, by_head, by_token):
+def finish_kernel(group, final, half_ref, x_ref, tail_ref, taps_ref, xs_ref, tails_ref, tapss_ref, valid_ref, cot_ref, both_ref,
+                  out_in_ref, grad_in_ref, chip_ref, partner_ref, bc_ref, small_ref, through_ref, *refs):
+    if final:
+        score_grad_ref, run_ref, dt_ref, sig_ref, sigsum_ref, own_ref = refs[:6]
+        bc_before, head_before, token_before = refs[6:9]
+        out_ref, grad_ref, end_ref, borrowed_ref, taps_grad_ref = refs[14:19]
+        grads_ref, ends_ref, borroweds_ref, tapss_grad_ref, heads_ref = refs[19:24]
+        lhs_hi, lhs_lo, bc_grad, by_head, by_token = refs[24:]
+    else:
+        out_ref, grad_ref, end_ref, borrowed_ref, taps_grad_ref, bc_grad, by_head, by_token, lhs_hi, lhs_lo = refs
     tile = pl.program_id(0)
     valid = valid_ref[...]
 
@@ -493,9 +476,14 @@
             first, second = halves(bc_ref[:, source : source + STATE])
             lhs_hi[at : at + ROWS, :] = mm_nt(first, pick).astype(BF16)
             lhs_lo[at : at + ROWS, :] = mm_nt(second, pick).astype(BF16)
-        bc_grad[...] = jnp.zeros_like(bc_grad)
-        by_head[...] = jnp.zeros_like(by_head)
-        by_token[...] = jnp.zeros_like(by_token)
+        if final:
+            bc_grad[...] = bc_before[...]
+            by_head[...] = head_before[...]
+            by_token[...] = token_before[...]
+        else:
+            bc_grad[...] = jnp.zeros_like(bc_grad)
+            by_head[...] = jnp.zeros_like(by_head)
+            by_token[...] = jnp.zeros_like(by_token)
 
     total, shifted = convolve(tail_ref[...].astype(F32), x_ref[...].astype(F32), taps_ref[...], valid)
     gate = sigmoid(total)
@@ -504,7 +492,17 @@
     here = tile_at(tile, half_ref)
     weight = spread_heads(both_ref, here)
     leave, entry = weight[:ROWS], weight[ROWS:]
-    states = jnp.where(tile < HALF_TILES, pair_a_ref[...], pair_b_ref[...]).reshape(2 * STATE, TILE)
+    earlier, later = even_odd(half_ref, through_ref)
+    even = half_ref[2] == 0
+    weight_state, weight_adjoint = jnp.where(even, 1.0, earlier), jnp.where(even, later, 1.0)
+    with_state, with_adjoint = jnp.where(even, 0.0, 1.0), jnp.where(even, 1.0, 0.0)
+    states = jnp.concatenate(
+        [
+            weight_state * chip_ref[:, :group, :] + with_state * partner_ref[:, :group, :],
+            weight_adjoint * chip_ref[:, group:, :] + with_adjoint * partner_ref[:, group:, :],
+        ],
+        axis=1,
+    ).reshape(2 * STATE, TILE)
     states_hi, states_lo = halves(states)
     read = mm(lhs_hi[...], states_hi) + mm(lhs_hi[...], states_lo) + mm(lhs_lo[...], states_hi)
     one_hot = head_columns(here)
@@ -541,7 +539,10 @@
     grad_ref[...] = full[8:].astype(BF16)
     end_ref[...] = full[ROWS - 8 :]
 
-    @pl.when(tile == TILES - 1)
+    if not final:
+        return
+
+    @pl.when(tile == HALF_TILES - 1)
     def _():
         score_grad = score_grad_ref[...]
         keys, reads = bc_ref[:, :STATE], bc_ref[:, STATE:]
@@ -556,7 +557,7 @@
         ends_ref[...] = full[ROWS - 8 :]
 
         read_sum, added_sum = by_token[:ROWS], by_token[ROWS:]
-        at_end = by_head[0:1, :] + through_ref[0:1, :] * by_head[1:2, :]
+        at_end = by_head[0:1, :] + own_ref[0:1, :] * by_head[1:2, :]
         run_grad = read_sum - added_sum + jnp.where(iota((ROWS, LANES), 0) == ROWS - 1, at_end, 0.0)
         alog_grad = jnp.sum(run_grad * run_ref[...], axis=0, keepdims=True)
         bias_grad = jnp.sum(added_sum / dt_ref[...] * sig_ref[...], axis=0, keepdims=True)
@@ -565,39 +566,50 @@
         heads_ref[...] = jnp.concatenate([bias_grad, alog_grad, by_head[2:3, :], jnp.zeros((5, LANES), F32)], axis=0)
 
 
-def finish_stage(group, half, conv_input, tail, taps, valid, cotangent, both, out_in, grad_in, pairs_a, pairs_b, bc,
-                 score_grad, run, dt, sig, sigsum, small, through):
+def finish_stage(group, half, operands, chip, partner, bc, small, through, last=None, before=None):
+    final = last is not None
     square = whole((ROWS, LANES))
-    shapes = (
+    wide = (
         jax.ShapeDtypeStruct((ROWS, INNER), BF16),
         jax.ShapeDtypeStruct((ROWS, INNER), BF16),
         jax.ShapeDtypeStruct((16, INNER), F32),
         jax.ShapeDtypeStruct((8, INNER), F32),
         jax.ShapeDtypeStruct((8, INNER), F32),
+    )
+    sums = (
+        jax.ShapeDtypeStruct((2 * ROWS, 2 * STATE), F32),
+        jax.ShapeDtypeStruct((8, LANES), F32),
+        jax.ShapeDtypeStruct((2 * ROWS, LANES), F32),
+    )
+    ends = (
         jax.ShapeDtypeStruct((ROWS, 2 * STATE), BF16),
         jax.ShapeDtypeStruct((16, 2 * STATE), F32),
         jax.ShapeDtypeStruct((8, 2 * STATE), F32),
         jax.ShapeDtypeStruct((8, 2 * STATE), F32),
         jax.ShapeDtypeStruct((8, LANES), F32),
     )
+    in_specs = [
+        tile_spec(ROWS), tile_spec(8), tile_spec(8),
+        small_spec(ROWS), small_spec(8), small_spec(8),
+        whole((ROWS, 8)), tile_spec(ROWS), whole((2 * ROWS, 2 * LANES)),
+        tile_spec(ROWS), tile_spec(ROWS), pair_spec(chip.shape, True), pair_spec(partner.shape, True),
+        whole((ROWS, 2 * STATE)), whole((8, LANES)), whole(through.shape),
+    ]
+    given = tuple(operands) + (chip, partner, bc, small, through)
+    lhs = [pltpu.VMEM((2 * ROWS, 2 * STATE), BF16)] * 2
+    aliases = {}
+    if final:
+        in_specs += [whole((ROWS, ROWS)), square, square, square, square, whole((8, LANES))]
+        in_specs += [whole(part.shape) for part in sums] + [pl.BlockSpec(memory_space=pl.ANY)] * len(wide)
+        aliases = {1 + len(given) + len(last) + len(sums) + at: at for at in range(len(wide))}
+        given += tuple(last) + tuple(before[len(wide):]) + tuple(before[: len(wide)])
+        rest, scratch = ends, lhs + [pltpu.VMEM(part.shape, F32) for part in sums]
+    else:
+        rest, scratch = sums, lhs
     return call(
-        functools.partial(finish_kernel, group), "finish", half, TILES,
-        [
-            tile_spec(ROWS), tile_spec(8), tile_spec(8),
-            small_spec(ROWS), small_spec(8), small_spec(8),
-            whole((ROWS, 8)), tile_spec(ROWS), whole((2 * ROWS, 2 * LANES)),
-            tile_spec(ROWS), tile_spec(ROWS), pair_spec(pairs_a.shape, True), pair_spec(pairs_b.shape, False),
-            whole((ROWS, 2 * STATE)), whole((ROWS, ROWS)),
-            square, square, square, square, whole((8, LANES)), whole((8, LANES)),
-        ],
-        [tile_spec(shape.shape[0]) for shape in shapes[:5]] + [whole(shape.shape) for shape in shapes[5:]],
-        shapes,
-        [
-            pltpu.VMEM((2 * ROWS, 2 * STATE), BF16), pltpu.VMEM((2 * ROWS, 2 * STATE), BF16),
-            pltpu.VMEM((2 * ROWS, 2 * STATE), F32), pltpu.VMEM((8, LANES), F32), pltpu.VMEM((2 * ROWS, LANES), F32),
-        ],
-        (conv_input, tail, taps, conv_input, tail, taps, valid, cotangent, both, out_in, grad_in, pairs_a, pairs_b, bc,
-         score_grad, run, dt, sig, sigsum, small, through),
+        functools.partial(finish_kernel, group, final), "finish_second" if final else "finish_first", half, HALF_TILES,
+        in_specs, [tile_spec(part.shape[0]) for part in wide] + [whole(part.shape) for part in rest], wide + rest,
+        scratch, given, aliases,
     )
 
 
@@ -715,8 +727,8 @@
     shards, place = lax.axis_size("seq"), lax.axis_index("seq")
     group = 2 * STATE // shards
     core = lax.rem(place, 2)
-    half = jnp.stack([core, place // 2])
-    other_half = jnp.stack([1 - core, place // 2])
+    half = jnp.stack([core, place // 2, core])
+    other_half = jnp.stack([1 - core, place // 2, core])
     taps = jnp.concatenate([conv_weight, conv_bias[None], jnp.zeros((3, CH), F32)], axis=0)
     small = jnp.pad(jnp.stack([dt_bias, a_log, skip_gain]), ((0, 5), (0, LANES - HEADS)))
 
@@ -726,16 +738,19 @@
     theirs, bc = local_stage(group, other_half, conv_input, tail, taps, valid, cotangent, both)
     other = swap(theirs)
     mine, _ = local_stage(group, half, conv_input, tail, taps, valid, cotangent, both)
+    other_second = swap(mine)
     gathered = between_chips(join_stage(group, half, mine, other, all_through))
     out_in, grad_in, score_grad = within_stage(
         half, conv_input, tail, taps, valid, cotangent, bc, run, runT, dt, dtT, mask
     )
+    gathered, out_in, grad_in = lax.optimization_barrier((gathered, out_in, grad_in))
     chip = between_chips(carry_stage(group, half, gathered, all_through))
-    pairs_a, pairs_b = part_stage(group, half, chip, mine, other, all_through)
-    pairs_b = swap(pairs_b)
+    chip_second = swap(chip)
+    operands = (conv_input, tail, taps, conv_input, tail, taps, valid, cotangent, both, out_in, grad_in)
+    first = finish_stage(group, half, operands, chip, other, bc, small, all_through)
     out, grad, end, borrowed, taps_grad, grads, ends, borroweds, tapss_grad, heads = finish_stage(
-        group, half, conv_input, tail, taps, valid, cotangent, both, out_in, grad_in, pairs_a, pairs_b, bc, score_grad,
-        run, dt, sig, sigsum, small, through,
+        group, other_half, operands, chip_second, other_second, bc, small, all_through,
+        (score_grad, run, dt, sig, sigsum, through), first,
     )
     groups = lax.axis_size("dp")
     weight_grad, bias_grad, heads, last = total_stage(

time: 211 us -> 205 us (0.972)
  blocking collectives: 75.9 us -> 0 us
  waiting for transfers between devices: 0.01 us -> 61.2 us
  starting transfers between devices: 2.69 us -> 13.4 us
  Pallas kernels: 114 us -> 111 us
    all_to_all x2 -> x0, blocking collectives: 75.9 us -> none  [between_chips(): lax.all_to_all(array, 'seq', 0, 0, axis_index_groups=groups, tiled=True)]
    all_to_all x0 -> x2, waiting for transfers between devices: none -> 61.2 us  [between_chips(): lax.all_to_all(array, 'seq', 0, 0, axis_index_groups=groups, tiled=True)]
    all_to_all x0 -> x2, starting transfers between devices: none -> 8.88 us  [between_chips(): lax.all_to_all(array, 'seq', 0, 0, axis_index_groups=groups, tiled=True)]
    pallas_call x7, Pallas kernels: 76 us -> 72.1 us  [call(): pl.pallas_call(kernel, grid_spec=pltpu.PrefetchScalarGridSpec(num_scalar_...]
    ppermute x2 -> x3, starting transfers between devices: 2.69 us -> 4.47 us  [swap(): lax.ppermute(array, 'seq', [(i, i ^ 1) for i in range(lax.axis_size('seq'...]
  transfers between devices with their start and end apart: 2 -> 5, of which waited for: 0 -> 2; matrix products, arithmetic and copies ran while one was open for 0% -> 0% of each run, Pallas kernels for 11% -> 18%
where the time goes in v4:
time: 205 us; the launch traced here: 204 us
  Pallas kernels  111 us (54%)
  waiting for transfers between devices  61.2 us (30%)
  starting transfers between devices  13.4 us (7%)
  local copies, waits for them, and re-layouts  9.46 us (5%)
  other arithmetic  7.67 us (4%)
    pallas_call x7, Pallas kernels, call(): pl.pallas_call(kernel, grid_spec=pltpu.PrefetchScalarGridSpec(num_scalar_...  72.1 us
    all_to_all x2, waiting for transfers between devices, between_chips(): lax.all_to_all(array, 'seq', 0, 0, axis_index_groups=groups, tiled=True)  61.2 us
    pallas_call x1, Pallas kernels, total_stage(): pl.pallas_call(functools.partial(total_kernel, shards, groups, scale), in...  23.2 us
    pallas_call x1, Pallas kernels, head_stage(): pl.pallas_call(functools.partial(head_kernel, shards), in_specs=[in_vmem]...  15.8 us
    all_to_all x2, starting transfers between devices, between_chips(): lax.all_to_all(array, 'seq', 0, 0, axis_index_groups=groups, tiled=True)  8.88 us
    ppermute x3, starting transfers between devices, swap(): lax.ppermute(array, 'seq', [(i, i ^ 1) for i in range(lax.axis_size('seq'...  4.47 us
  transfers between devices with their start and end apart: 5, of which 2 were waited for; matrix products, arithmetic and copies ran while one was open for 0% of the time, Pallas kernels for 18%

profile of v4, /device:TPU:1, one launch (start us, length us, event | category | flops | bytes accessed | tf_op | source)
XLA Modules:
  0.0 203.6 jit_solution(1658828895900439086)
XLA Ops:
  0.6 0.8 broadcast_in_dim.10
  1.4 1.6 slice.18.end_ref
  3.0 0.1 pad.13.clone
  3.1 0.7 add_add_fusion.half_ref
  3.7 1.3 select_maximum_fusion.small_ref
  5.0 1.6 maximum_maximum_fusion.taps_ref.tapss_ref
  6.7 15.8 %heads.1 = (f32[128,128]{1,0:T(8,128)}, f32[128,128]{1,0:T(8,128)}, f32[128,128]{1,0:T(8,128)}, f32[128,128]{1,0:T(8,128)}, bf16[256,256]{1,0:T(8,128)(2,1)}, /*...) custom-call(f32[80,128]{1,0:T(8,128)} %bitcast.14, ...), custom_call_target="tpu_custom_call" | custom-call | tf_op jit(solution)/shard_map/heads/pallas_call | solution.py:227
  22.5 7.9 %local.3 = (f32[16,16,2560]{2,1,0:T(8,128)}, f32[128,256]{1,0:T(8,128)}) custom-call(s32[3]{0:T(128)} %add_add_fusion.half_ref, bf16[128,5376]{1,0:T(8,128)(2,1)} %xs_ref.7, bf16[8,5376]{1,0:T(8,128)(2,1)} %get-tuple-element.51.tail_ref.tails_ref, f32[8,5376]{1,0:T(8,128)} %maximum_maximum_fusion.taps_ref.tapss_ref, bf16[128,5376]{1,0:T(8,128)(2,1)} %xs_ref.7, ...), custom_call_target="tpu_custom_call" | custom-call | tf_op jit(solution)/shard_map/local/pallas_call | solution.py:249
  30.4 0.4 collective-permute-start
  30.7 0.6 add_add_fusion.1.half_ref
  31.3 7.9 %local.2 = (f32[16,16,2560]{2,1,0:T(8,128)}, f32[128,256]{1,0:T(8,128)}) custom-call(s32[3]{0:T(128)} %add_add_fusion.1.half_ref, bf16[128,5376]{1,0:T(8,128)(2,1)} %xs_ref.7, bf16[8,5376]{1,0:T(8,128)(2,1)} %get-tuple-element.51.tail_ref.tails_ref, f32[8,5376]{1,0:T(8,128)} %maximum_maximum_fusion.taps_ref.tapss_ref, bf16[128,5376]{1,0:T(8,128)(2,1)} %xs_ref.7, ...), custom_call_target="tpu_custom_call" | custom-call | tf_op jit(solution)/shard_map/local/pallas_call | solution.py:249
  39.2 0.0 collective-permute-done.other_ref.partner_ref
  39.2 0.0 copy-start
  39.2 1.4 copy-done
  40.6 6.6 %join.1 = f32[16,16,2560]{2,1,0:T(8,128)} custom-call(s32[3]{0:T(128)} %add_add_fusion.1.half_ref, f32[16,16,2560]{2,1,0:T(8,128)} %get-tuple-element.54.mine_ref, f32[16,16,2560]{2,1,0:T(8,128)} %copy-done, f32[32,128]{1,0:T(8,128)} %get-tuple-element.56.through_ref), custom_call_target="tpu_custom_call" | custom-call | tf_op jit(solution)/shard_map/join/pallas_call | solution.py:249
  47.3 4.9 %all-to-all-start = ((f32[16,16,2560]{2,1,0:T(8,128)}), f32[16,16,2560]{2,1,0:T(8,128)S(1)}, u32[]{:S(2)}, u32[]{:S(2)}) async-start(f32[16,16,2560]{2,1,0:T(8,128)} %join.1), calls=%async_computation | async-start | bytes 5242880 | tf_op jit(solution)/shard_map/all_to_all | solution.py:723
  52.2 15.0 %within.1 = (f32[128,5120]{1,0:T(8,128)}, f32[128,5120]{1,0:T(8,128)}, f32[128,128]{1,0:T(8,128)}) custom-call(s32[3]{0:T(128)} %add_add_fusion.1.half_ref, bf16[128,5376]{1,0:T(8,128)(2,1)} %xs_ref.7, bf16[8,5376]{1,0:T(8,128)(2,1)} %get-tuple-element.51.tail_ref.tails_ref, f32[8,5376]{1,0:T(8,128)} %maximum_maximum_fusion.taps_ref.tapss_ref, ...), custom_call_target="tpu_custom_call" | custom-call | tf_op jit(solution)/shard_map/within/pallas_call | solution.py:249
  67.2 25.7 %all-to-all-done.pair_ref = f32[16,16,2560]{2,1,0:T(8,128)S(1)} async-done(((f32[16,16,2560]{2,1,0:T(8,128)}), f32[16,16,2560]{2,1,0:T(8,128)S(1)}, u32[]{:S(2)}, u32[]{:S(2)}) %all-to-all-start) | async-done | bytes 2621472 | tf_op jit(solution)/shard_map/all_to_all | solution.py:723
  92.9 0.0 copy-start.2
  92.9 1.5 copy-done.2
  94.4 6.0 %carry.1 = f32[16,16,2560]{2,1,0:T(8,128)} custom-call(s32[3]{0:T(128)} %add_add_fusion.1.half_ref, f32[16,16,2560]{2,1,0:T(8,128)} %copy-done.2, f32[32,128]{1,0:T(8,128)} %get-tuple-element.56.through_ref), custom_call_target="tpu_custom_call" | custom-call | tf_op jit(solution)/shard_map/carry/pallas_call | solution.py:249
  100.4 3.9 %all-to-all-start.1 = ((f32[16,16,2560]{2,1,0:T(8,128)}), f32[16,16,2560]{2,1,0:T(8,128)S(1)}, u32[]{:S(2)}, u32[]{:S(2)}) async-start(f32[16,16,2560]{2,1,0:T(8,128)} %carry.1), calls=%async_computation.1 | async-start | bytes 5242880 | tf_op jit(solution)/shard_map/all_to_all | solution.py:723
  104.4 1.5 collective-permute-start.2
  105.9 35.5 %all-to-all-done.1.chip_ref = f32[16,16,2560]{2,1,0:T(8,128)S(1)} async-done(((f32[16,16,2560]{2,1,0:T(8,128)}), f32[16,16,2560]{2,1,0:T(8,128)S(1)}, u32[]{:S(2)}, u32[]{:S(2)}) %all-to-all-start.1) | async-done | bytes 2621472 | tf_op jit(solution)/shard_map/all_to_all | solution.py:723
  141.4 0.0 copy-start.1
  141.4 2.6 %collective-permute-start.1 = (f32[16,16,2560]{2,1,0:T(8,128)S(1)}, f32[16,16,2560]{2,1,0:T(8,128)}, u32[]{:S(2)}, u32[]{:S(2)}) collective-permute-start(f32[16,16,2560]{2,1,0:T(8,128)S(1)} %all-to-all-done.1.chip_ref), channel_id=1, source_target_pairs={{0,1},{1,0},{2,3},{3,2},{4,5},{5,4},{6,7},{7,6},{8,9},{9,8},{10,11... | collective-permute-start | bytes 7864328 | tf_op jit(solution)/shard_map/ppermute | solution.py:717
  144.0 0.0 copy-done.1
  144.0 14.1 %finish_first.1 = (bf16[128,5120]{1,0:T(8,128)(2,1)}, bf16[128,5120]{1,0:T(8,128)(2,1)}, f32[16,5120]{1,0:T(8,128)}, f32[8,5120]{1,0:T(8,128)}, f32[8,5120]{1,0:...) custom-call(s32[3]{0:T(128)} %add_add_fusion.1.half_ref, bf16[128,5376]{1,0:T(8,128)(2,1)} %xs_ref.7, ...), custom_call_target="tpu_custom_call" | custom-call | tf_op jit(solution)/shard_map/finish_first/pallas_call | solution.py:249
  158.1 0.0 collective-permute-done.2.partner_ref
  158.1 0.0 collective-permute-done.1.chip_ref
  158.1 14.7 %finish_second.1 = (bf16[128,5120]{1,0:T(8,128)(2,1)}, bf16[128,5120]{1,0:T(8,128)(2,1)}, f32[16,5120]{1,0:T(8,128)}, f32[8,5120]{1,0:T(8,128)}, f32[8,5120]{1,0...) custom-call(s32[3]{0:T(128)} %add_add_fusion.half_ref, ...), custom_call_target="tpu_custom_call", output_to_operand_aliasing={{0}: (26, {}), {1}: (27, {}), {2}: (28, {}), {3}: (29, {}),... | custom-call | tf_op jit(solution)/shard_map/finish_second/pallas_call | solution.py:249
  172.8 0.8 slice.20
  173.6 23.2 %totals.1 = (f32[4,5376]{1,0:T(4,128)}, f32[1,5376]{1,0:T(1,128)}, f32[8,128]{1,0:T(8,128)}, bf16[16,5376]{1,0:T(8,128)(2,1)}) custom-call(f32[8,5120]{1,0:T(8,128)} %get-tuple-element.83.taps_ref, f32[8,256]{1,0:T(8,128)} %get-tuple-element.84.small_ref, f32[8,128]{1,0:T(8,128)} %get-tuple-element.85.heads_ref, f32[8,5120]{1,0:T(8,128)} %get-tuple-element.86.borrowed_ref, ...), custom_call_target="tpu_custom_call" | custom-call | tf_op jit(solution)/shard_map/totals/pallas_call | solution.py:696
  196.8 0.0 copy-start.3
  196.9 1.3 slice_bitcast_fusion
  198.2 1.3 slice.19
  199.5 1.4 reduce
  200.9 2.1 %pad_maximum_fusion = bf16[128,5376]{1,0:T(8,128)(2,1)} fusion(bf16[16,5376]{1,0:T(8,128)(2,1)} %get-tuple-element.91, bf16[112,256]{1,0:T(8,128)(2,1)S(1)} %slice.20, bf16[112,5120]{1,0:T(8,128)(2,1)S(1)} %slice.19), kind=kLoop, calls=%fused_computation | loop fusion | flops 4128768 | bytes 2752512 | tf_op jit(solution)/shard_map/concatenate | solution.py:760
  203.0 0.0 copy-done.3
  203.0 0.6 copy.27
  (1 shorter events, 0.0 us)
Async XLA Ops:
  30.4 8.8 %collective-permute-start = (f32[16,16,2560]{2,1,0:T(8,128)}, f32[16,16,2560]{2,1,0:T(8,128)S(1)}, u32[]{:S(2)}, u32[]{:S(2)}) collective-permute-start(f32[16,16,2560]{2,1,0:T(8,128)} %get-tuple-element.55), channel_id=1, source_target_pairs={{0,1},{1,0},{2,3},{3,2},{4,5},{5,4},{6,7},{7,6},{8,9},{9,8},{10,11... | collective-permute-start | bytes 7864328 | tf_op jit(solution)/shard_map/ppermute | solution.py:717
  39.2 1.5 copy-start
  47.3 45.7 %all-to-all-start = ((f32[16,16,2560]{2,1,0:T(8,128)}), f32[16,16,2560]{2,1,0:T(8,128)S(1)}, u32[]{:S(2)}, u32[]{:S(2)}) async-start(f32[16,16,2560]{2,1,0:T(8,128)} %join.1), calls=%async_computation | async-start | bytes 5242880 | tf_op jit(solution)/shard_map/all_to_all | solution.py:723
  92.9 1.5 copy-start.2
  100.4 40.9 %all-to-all-start.1 = ((f32[16,16,2560]{2,1,0:T(8,128)}), f32[16,16,2560]{2,1,0:T(8,128)S(1)}, u32[]{:S(2)}, u32[]{:S(2)}) async-start(f32[16,16,2560]{2,1,0:T(8,128)} %carry.1), calls=%async_computation.1 | async-start | bytes 5242880 | tf_op jit(solution)/shard_map/all_to_all | solution.py:723
  104.4 53.7 %collective-permute-start.2 = (f32[16,16,2560]{2,1,0:T(8,128)}, f32[16,16,2560]{2,1,0:T(8,128)}, u32[]{:S(2)}, u32[]{:S(2)}) collective-permute-start(f32[16,16,2560]{2,1,0:T(8,128)} %get-tuple-element.54.mine_ref), channel_id=1, source_target_pairs={{0,1},{1,0},{2,3},{3,2},{4,5},{5,4},{6,7},{7,6},{8,9},{9,8},{10,11... | collective-permute-start | bytes 7864328 | tf_op jit(solution)/shard_map/ppermute | solution.py:717
  141.4 2.6 %copy-start.1 = (f32[16,16,2560]{2,1,0:T(8,128)}, f32[16,16,2560]{2,1,0:T(8,128)S(1)}, u32[]{:S(2)}) copy-start(f32[16,16,2560]{2,1,0:T(8,128)S(1)} %all-to-all-done.1.chip_ref) | copy-start | bytes 7864324
  141.4 16.7 %collective-permute-start.1 = (f32[16,16,2560]{2,1,0:T(8,128)S(1)}, f32[16,16,2560]{2,1,0:T(8,128)}, u32[]{:S(2)}, u32[]{:S(2)}) collective-permute-start(f32[16,16,2560]{2,1,0:T(8,128)S(1)} %all-to-all-done.1.chip_ref), channel_id=1, source_target_pairs={{0,1},{1,0},{2,3},{3,2},{4,5},{5,4},{6,7},{7,6},{8,9},{9,8},{10,11... | collective-permute-start | bytes 7864328 | tf_op jit(solution)/shard_map/ppermute | solution.py:717
  196.8 6.1 %copy-start.3 = (f32[4,5376]{1,0:T(4,128)S(1)}, f32[4,5376]{1,0:T(4,128)}, u32[]{:S(2)}) copy-start(f32[4,5376]{1,0:T(4,128)} %get-tuple-element.107) | copy-start | bytes 258052

commit v5 on v4

--- a/solution.py
+++ b/solution.py
@@ -90,56 +90,48 @@
     return 1.0 / (1.0 + jnp.exp(-v))
 
 
-def greet(axes):
-    barrier = pltpu.get_barrier_semaphore()
-    for axis, size in axes:
-        place = lax.axis_index(axis)
-
-        def signal(k, carry):
-            pl.semaphore_signal(
-                barrier, inc=1, device_id={axis: lax.rem(place + k, size)}, device_id_type=MESH
-            )
-            return carry
-
-        lax.fori_loop(1, size, signal, 0)
-    pl.semaphore_wait(barrier, sum(size - 1 for _, size in axes))
-
-
-def remote(source, target, send, receive, axis, peer):
-    return pltpu.make_async_remote_copy(
-        src_ref=source, dst_ref=target, send_sem=send, recv_sem=receive, device_id={axis: peer}, device_id_type=MESH
-    )
-
-
-def send_all(axis, size, source, target, send, receive):
-    place = lax.axis_index(axis)
-
-    def start(k, carry):
-        peer = lax.rem(place + k, size)
-        remote(source(peer), target.at[place], send.at[peer], receive.at[place], axis, peer).start()
-        return carry
-
-    lax.fori_loop(1, size, start, 0)
-
-
-def wait_all(axis, size, source, target, send, receive):
-    place = lax.axis_index(axis)
-
-    def wait(k, carry):
-        peer = lax.rem(place + k, size)
-        copy = remote(source(peer), target.at[peer], send.at[peer], receive.at[peer], axis, peer)
+def near(k):
+    place = lax.axis_index("seq")
+    slot = lax.rem(lax.rem(place, 8) + k, 8)
+    return (lax.axis_index("dp"), place - lax.rem(place, 8) + slot), slot
+
+
+def far(k):
+    place, group = lax.axis_index("seq"), lax.axis_index("dp")
+    runs = lax.axis_size("seq") // 8
+    slot = lax.rem(group * runs + place // 8 + k, lax.axis_size("dp") * runs)
+    return (slot // runs, lax.rem(slot, runs) * 8 + lax.rem(place, 8)), slot
+
+
+def send_all(peers, size, source, target, send, receive):
+    _, own = peers(0)
+    for k in range(1, size):
+        peer, slot = peers(k)
+        pltpu.make_async_remote_copy(
+            src_ref=source(slot), dst_ref=target.at[own], send_sem=send.at[slot], recv_sem=receive.at[own],
+            device_id=peer, device_id_type=MESH,
+        ).start()
+
+
+def wait_all(peers, size, source, target, send, receive):
+    for k in range(1, size):
+        peer, slot = peers(k)
+        copy = pltpu.make_async_remote_copy(
+            src_ref=source(slot), dst_ref=target.at[slot], send_sem=send.at[slot], recv_sem=receive.at[slot],
+            device_id=peer, device_id_type=MESH,
+        )
         copy.wait_send()
         copy.wait_recv()
-        return carry
-
-    lax.fori_loop(1, size, wait, 0)
-
-
-def head_kernel(shards, raw_in_ref, small_ref, row_ref, end_ref, run_ref, runT_ref, dt_ref, dtT_ref, both_ref, sig_ref,
-                sigsum_ref, through_ref, mask_ref, valid_ref, keep_ref, tail_ref, own_ref, raw, own, slots, tail_out, send,
-                receive, tail_send, tail_receive):
-    greet((("seq", shards),))
-    place = lax.axis_index("seq")
+
+
+def head_kernel(raw_in_ref, dt_bias_ref, a_log_ref, gain_ref, row_ref, weight_ref, bias_ref, end_ref, run_ref, runT_ref,
+                dt_ref, dtT_ref, both_ref, sig_ref, sigsum_ref, mask_ref, valid_ref, keep_ref, tail_ref, own_ref,
+                small_ref, taps_ref, raw):
+    taps_ref[:CONV, :] = weight_ref[...]
+    taps_ref[CONV:, :] = jnp.broadcast_to(bias_ref[...], (8 - CONV, CH))
+    small_ref[...] = jnp.zeros_like(small_ref)
+    for at, source in enumerate((dt_bias_ref, a_log_ref, gain_ref)):
+        small_ref[at : at + 1, :HEADS] = source[...]
     reset_row = row_ref[...].astype(F32)
     token, other = iota((ROWS, ROWS), 0), iota((ROWS, ROWS), 1)
     reset_col = jnp.sum(jnp.where(token == other, reset_row, 0.0), axis=1, keepdims=True)
@@ -159,12 +151,7 @@
         token == ROWS - 1, 1.0, jnp.where(token == ROWS - 2, one_on, jnp.where(token == ROWS - 3, one_on * two_on, 0.0))
     )[ROWS - 8 :]
     keep_ref[...] = keep
-    tail_out[...] = (end_ref[8:, :].astype(F32) * keep[:, 0:1]).astype(BF16)
-    onward = remote(tail_out, tail_ref, tail_send, tail_receive, "seq", lax.rem(place + 1, shards))
-
-    @pl.when(place < shards - 1)
-    def _():
-        onward.start()
+    tail_ref[...] = (end_ref[8:, :].astype(F32) * keep[:, 0:1]).astype(BF16)
 
     raw[...] = jnp.zeros_like(raw)
     raw[:HEADS, :] = raw_in_ref[...]
@@ -177,9 +164,7 @@
     count = segment_col[ROWS - 1 : ROWS]
     untouched = jnp.where(segment_col == 0.0, 1.0, 0.0)
     entry = jnp.exp(running) * untouched
-    own[...] = jnp.broadcast_to(entry[ROWS - 1 : ROWS], own.shape)
-    own_ref[...] = own[...]
-    send_all("seq", shards, lambda peer: own, slots, send, receive)
+    own_ref[...] = jnp.broadcast_to(entry[ROWS - 1 : ROWS], own_ref.shape)
     sig = sigmoid(biased)
     sig_ref[...] = sig
     sigsum_ref[...] = exact(lower, sig)
@@ -192,53 +177,33 @@
         first, second = halves(part)
         both_ref[at : at + ROWS, :LANES] = first
         both_ref[at : at + ROWS, LANES:] = second
-    slots[place] = own[...]
-    wait_all("seq", shards, lambda peer: own, slots, send, receive)
-    for shard in range(shards):
-        through_ref[shard : shard + 1, :] = slots[shard, 0:1, :]
-
-    @pl.when(place < shards - 1)
-    def _():
-        onward.wait_send()
-
-    @pl.when(place > 0)
-    def _():
-        onward.wait_recv()
-
-    @pl.when(place == 0)
-    def _():
-        tail_ref[...] = jnp.zeros_like(tail_ref)
-
-
-def head_stage(shards, raw, small, row, end):
+
+
+def head_stage(raw, dt_bias, a_log, gain, row, weight, bias, conv_input):
     square = jax.ShapeDtypeStruct((ROWS, LANES), F32)
+    eight = jax.ShapeDtypeStruct((8, LANES), F32)
     shapes = (
         square, square, square, square,
         jax.ShapeDtypeStruct((2 * ROWS, 2 * LANES), BF16),
         square, square,
-        jax.ShapeDtypeStruct((shards, LANES), F32),
         jax.ShapeDtypeStruct((2, ROWS, ROWS), F32),
         jax.ShapeDtypeStruct((ROWS, 8), F32),
-        jax.ShapeDtypeStruct((8, LANES), F32),
+        eight,
         jax.ShapeDtypeStruct((8, CH), BF16),
-        jax.ShapeDtypeStruct((8, LANES), F32),
-    )
-    in_vmem = pl.BlockSpec(memory_space=pltpu.VMEM)
+        eight, eight,
+        jax.ShapeDtypeStruct((8, CH), F32),
+    )
+    given = (raw, dt_bias, a_log, gain, row, weight, bias)
     return pl.pallas_call(
-        functools.partial(head_kernel, shards),
-        in_specs=[in_vmem] * 4,
-        out_specs=[in_vmem] * len(shapes),
+        head_kernel,
+        grid=(1,),
+        in_specs=[whole(part.shape) for part in given] + [pl.BlockSpec((16, CH), lambda *at: (ROWS // 16 - 1, 0))],
+        out_specs=[whole(part.shape) for part in shapes],
         out_shape=shapes,
-        scratch_shapes=[
-            pltpu.VMEM((ROWS, LANES), F32), pltpu.VMEM((8, LANES), F32), pltpu.VMEM((shards, 8, LANES), F32),
-            pltpu.VMEM((8, CH), BF16), pltpu.SemaphoreType.DMA((shards,)), pltpu.SemaphoreType.DMA((shards,)),
-            pltpu.SemaphoreType.DMA, pltpu.SemaphoreType.DMA,
-        ],
-        compiler_params=pltpu.CompilerParams(
-            vmem_limit_bytes=VMEM_BYTES, collective_id=0, has_side_effects=True
-        ),
+        scratch_shapes=[pltpu.VMEM((ROWS, LANES), F32)],
+        compiler_params=pltpu.CompilerParams(vmem_limit_bytes=VMEM_BYTES),
         name="heads",
-    )(raw, small, row, end)
+    )(*given, conv_input)
 
 
 def whole(shape):
@@ -384,61 +349,66 @@
     )
 
 
-def chip_decay(half_ref, through_ref, rows):
-    return spread_exact(through_ref[rows, :], head_columns(tile_at(pl.program_id(0), half_ref)))
-
-
-def own_pair(half_ref):
-    return pl.ds(pl.multiple_of(8 * (half_ref[1] // 4), 8), 8)
-
-
-def even_odd(half_ref, through_ref):
-    chips = chip_decay(half_ref, through_ref, own_pair(half_ref))
-    place = lax.rem(half_ref[1], 4)
-    row = iota(chips.shape, 0)
-    earlier = jnp.sum(jnp.where(row == 2 * place, chips, 0.0), axis=0, keepdims=True)
-    later = jnp.sum(jnp.where(row == 2 * place + 1, chips, 0.0), axis=0, keepdims=True)
-    return earlier[None], later[None]
-
-
-def join_kernel(group, half_ref, mine_ref, other_ref, through_ref, out_ref):
-    earlier, later = even_odd(half_ref, through_ref)
+def even_odd(half_ref, both):
     even = half_ref[2] == 0
-    mine, other = mine_ref[...], other_ref[...]
-    first, second = jnp.where(even, mine, other), jnp.where(even, other, mine)
-    out_ref[:, :group, :] = later * first[:, :group] + second[:, :group]
-    out_ref[:, group:, :] = first[:, group:] + earlier * second[:, group:]
-
-
-def join_stage(group, half, mine, other, through):
-    spec = pair_spec(mine.shape, True)
+    own, partner = both[0:1], both[8:9]
+    return jnp.where(even, own, partner)[None], jnp.where(even, partner, own)[None]
+
+
+def join_kernel(group, half_ref, mine_ref, other_ref, own_ref, partner_ref, out_ref, both):
+    @pl.when(pl.program_id(0) == 0)
+    def _():
+        rows = jnp.concatenate([own_ref[...], partner_ref[...]], axis=0)
+        for at in range(HALF_TILES):
+            one_hot = head_columns(HALF_TILES * half_ref[0] + at)
+            both[:, TILE * at : TILE * (at + 1)] = spread_exact(rows, one_hot)
+
+    even = half_ref[2] == 0
+    for at in range(HALF_TILES):
+        lanes = slice(TILE * at, TILE * (at + 1))
+        earlier, later = even_odd(half_ref, both[:, lanes])
+        mine, other = mine_ref[:, :, lanes], other_ref[:, :, lanes]
+        first, second = jnp.where(even, mine, other), jnp.where(even, other, mine)
+        out_ref[:, :group, lanes] = later * first[:, :group] + second[:, :group]
+        out_ref[:, group:, lanes] = first[:, group:] + earlier * second[:, group:]
+    decay = own_ref[0:1, :] * partner_ref[0:1, :]
+    out_ref[:, :, INNER // 2 :] = jnp.broadcast_to(decay[None], out_ref.shape[:2] + (LANES,))
+
+
+def join_stage(group, half, mine, other, own, partner):
+    chips, rows, width = mine.shape
+    step = chips // 4
+    spec = pl.BlockSpec((step, rows, width), lambda i, half: (i, 0, 0))
     return call(
-        functools.partial(join_kernel, group), "join", half, HALF_TILES,
-        [spec, spec, whole(through.shape)], spec, jax.ShapeDtypeStruct(mine.shape, F32), [], (mine, other, through),
-    )
-
-
-def carry_kernel(group, half_ref, pair_ref, through_ref, out_ref, decay):
+        functools.partial(join_kernel, group), "join", half, 4,
+        [spec, spec, whole((8, LANES)), whole((8, LANES))],
+        pl.BlockSpec((step, rows, width + LANES), lambda i, half: (i, 0, 0)),
+        jax.ShapeDtypeStruct((chips, rows, width + LANES), F32), [pltpu.VMEM((16, width), F32)],
+        (mine, other, own, partner),
+    )
+
+
+def carry_kernel(group, half_ref, pair_ref, rest_ref, out_ref, decay):
     chips = pair_ref.shape[0]
-    decay[...] = chip_decay(half_ref, through_ref, slice(None))
+    one_hot = head_columns(tile_at(pl.program_id(0), half_ref))
+    decay[...] = spread_exact(jnp.max(rest_ref[...], axis=1), one_hot)
     state = jnp.zeros((group, TILE), F32)
+    adjoint = jnp.zeros((group, TILE), F32)
     for chip in range(chips):
         out_ref[chip, :group, :] = state
-        state = decay[2 * chip : 2 * chip + 1, :] * decay[2 * chip + 1 : 2 * chip + 2, :] * state
-        state = state + pair_ref[chip, :group, :]
-    state = jnp.zeros((group, TILE), F32)
-    for chip in reversed(range(chips)):
-        out_ref[chip, group:, :] = state
-        state = decay[2 * chip : 2 * chip + 1, :] * decay[2 * chip + 1 : 2 * chip + 2, :] * state
-        state = state + pair_ref[chip, group:, :]
-
-
-def carry_stage(group, half, pairs, through):
-    spec = pair_spec(pairs.shape, True)
+        state = decay[chip : chip + 1, :] * state + pair_ref[chip, :group, :]
+        back = chips - 1 - chip
+        out_ref[back, group:, :] = adjoint
+        adjoint = decay[back : back + 1, :] * adjoint + pair_ref[back, group:, :]
+
+
+def carry_stage(group, half, pairs):
+    chips, rows, width = pairs.shape
+    shape = (chips, rows, width - LANES)
     return call(
         functools.partial(carry_kernel, group), "carry", half, HALF_TILES,
-        [spec, whole(through.shape)], spec, jax.ShapeDtypeStruct(pairs.shape, F32),
-        [pltpu.VMEM((through.shape[0], TILE), F32)], (pairs, through),
+        [pair_spec(shape, True), pl.BlockSpec((chips, rows, LANES), lambda *at: (0, 0, shape[2] // LANES))],
+        pair_spec(shape, True), jax.ShapeDtypeStruct(shape, F32), [pltpu.VMEM((chips, TILE), F32)], (pairs, pairs),
     )
 
 
@@ -457,13 +427,13 @@
 
 
 def finish_kernel(group, final, half_ref, x_ref, tail_ref, taps_ref, xs_ref, tails_ref, tapss_ref, valid_ref, cot_ref, both_ref,
-                  out_in_ref, grad_in_ref, chip_ref, partner_ref, bc_ref, small_ref, through_ref, *refs):
+                  out_in_ref, grad_in_ref, chip_ref, local_ref, bc_ref, small_ref, own_ref, partner_ref, *refs):
     if final:
-        score_grad_ref, run_ref, dt_ref, sig_ref, sigsum_ref, own_ref = refs[:6]
-        bc_before, head_before, token_before = refs[6:9]
-        out_ref, grad_ref, end_ref, borrowed_ref, taps_grad_ref = refs[14:19]
-        grads_ref, ends_ref, borroweds_ref, tapss_grad_ref, heads_ref = refs[19:24]
-        lhs_hi, lhs_lo, bc_grad, by_head, by_token = refs[24:]
+        score_grad_ref, run_ref, dt_ref, sig_ref, sigsum_ref = refs[:5]
+        bc_before, head_before, token_before = refs[5:8]
+        out_ref, grad_ref, end_ref, borrowed_ref, taps_grad_ref = refs[13:18]
+        grads_ref, ends_ref, borroweds_ref, tapss_grad_ref, heads_ref = refs[18:23]
+        lhs_hi, lhs_lo, bc_grad, by_head, by_token = refs[23:]
     else:
         out_ref, grad_ref, end_ref, borrowed_ref, taps_grad_ref, bc_grad, by_head, by_token, lhs_hi, lhs_lo = refs
     tile = pl.program_id(0)
@@ -492,21 +462,24 @@
     here = tile_at(tile, half_ref)
     weight = spread_heads(both_ref, here)
     leave, entry = weight[:ROWS], weight[ROWS:]
-    earlier, later = even_odd(half_ref, through_ref)
+    by_row = spread_exact(
+        jnp.concatenate([own_ref[...], partner_ref[...], small_ref[...]], axis=0), head_columns(here)
+    )
+    earlier, later = even_odd(half_ref, by_row)
     even = half_ref[2] == 0
     weight_state, weight_adjoint = jnp.where(even, 1.0, earlier), jnp.where(even, later, 1.0)
     with_state, with_adjoint = jnp.where(even, 0.0, 1.0), jnp.where(even, 1.0, 0.0)
     states = jnp.concatenate(
         [
-            weight_state * chip_ref[:, :group, :] + with_state * partner_ref[:, :group, :],
-            weight_adjoint * chip_ref[:, group:, :] + with_adjoint * partner_ref[:, group:, :],
+            weight_state * chip_ref[:, :group, :] + with_state * local_ref[:, :group, :],
+            weight_adjoint * chip_ref[:, group:, :] + with_adjoint * local_ref[:, group:, :],
         ],
         axis=1,
     ).reshape(2 * STATE, TILE)
     states_hi, states_lo = halves(states)
     read = mm(lhs_hi[...], states_hi) + mm(lhs_hi[...], states_lo) + mm(lhs_lo[...], states_hi)
     one_hot = head_columns(here)
-    gain = spread_exact(small_ref[...], one_hot)[2:3]
+    gain = by_row[18:19]
     through_state = out_in_ref[...] + entry * read[:ROWS]
     out_ref[...] = (through_state + gain * act).astype(BF16)
     act_grad_late = leave * read[ROWS:]
@@ -566,7 +539,7 @@
         heads_ref[...] = jnp.concatenate([bias_grad, alog_grad, by_head[2:3, :], jnp.zeros((5, LANES), F32)], axis=0)
 
 
-def finish_stage(group, half, operands, chip, partner, bc, small, through, last=None, before=None):
+def finish_stage(group, half, operands, chip, local, bc, small, own, partner, last=None, before=None):
     final = last is not None
     square = whole((ROWS, LANES))
     wide = (
@@ -592,14 +565,14 @@
         tile_spec(ROWS), tile_spec(8), tile_spec(8),
         small_spec(ROWS), small_spec(8), small_spec(8),
         whole((ROWS, 8)), tile_spec(ROWS), whole((2 * ROWS, 2 * LANES)),
-        tile_spec(ROWS), tile_spec(ROWS), pair_spec(chip.shape, True), pair_spec(partner.shape, True),
-        whole((ROWS, 2 * STATE)), whole((8, LANES)), whole(through.shape),
+        tile_spec(ROWS), tile_spec(ROWS), pair_spec(chip.shape, True), pair_spec(local.shape, True),
+        whole((ROWS, 2 * STATE)), whole((8, LANES)), whole((8, LANES)), whole((8, LANES)),
     ]
-    given = tuple(operands) + (chip, partner, bc, small, through)
+    given = tuple(operands) + (chip, local, bc, small, own, partner)
     lhs = [pltpu.VMEM((2 * ROWS, 2 * STATE), BF16)] * 2
     aliases = {}
     if final:
-        in_specs += [whole((ROWS, ROWS)), square, square, square, square, whole((8, LANES))]
+        in_specs += [whole((ROWS, ROWS)), square, square, square, square]
         in_specs += [whole(part.shape) for part in sums] + [pl.BlockSpec(memory_space=pl.ANY)] * len(wide)
         aliases = {1 + len(given) + len(last) + len(sums) + at: at for at in range(len(wide))}
         given += tuple(last) + tuple(before[len(wide):]) + tuple(before[: len(wide)])
@@ -613,50 +586,67 @@
     )
 
 
-def total_kernel(shards, groups, scale, taps_ref, small_ref, heads_ref, borrowed_ref, borroweds_ref, end_ref, ends_ref,
-                 keep_ref, weight_ref, bias_ref, heads_out_ref, last_ref,
-                 parts, slots, piece, dp_slots, result, got, got_small, send, receive, dp_send, dp_receive, back_send,
+def total_kernel(scale, taps_ref, small_ref, heads_ref, borrowed_ref, borroweds_ref, end_ref, ends_ref, keep_ref, grad_ref,
+                 grads_ref, weight_ref, bias_ref, heads_out_ref, whole_ref,
+                 parts, slots, piece, far_slots, result, got, got_small, send, receive, far_send, far_receive, back_send,
                  back_receive, rows_send, rows_receive):
-    greet((("seq", shards), ("dp", groups)))
+    shards, groups = lax.axis_size("seq"), lax.axis_size("dp")
+    others = groups * shards // 8
     place, group = lax.axis_index("seq"), lax.axis_index("dp")
-    before = lax.rem(place + shards - 1, shards)
-    returns = [
-        remote(borrowed_ref, got, rows_send.at[0], rows_receive.at[0], "seq", before),
-        remote(borroweds_ref, got_small, rows_send.at[1], rows_receive.at[1], "seq", before),
-    ]
+    before = (group, lax.rem(place + shards - 1, shards))
+    after = (group, lax.rem(place + 1, shards))
+    barrier = pltpu.get_barrier_semaphore()
+    for peers, size in ((near, 8), (far, others)):
+        for k in range(1, size):
+            pl.semaphore_signal(barrier, inc=1, device_id=peers(k)[0], device_id_type=MESH)
+    for peer in (before, after):
+        pl.semaphore_signal(barrier, inc=1, device_id=peer, device_id_type=MESH)
+    pl.semaphore_wait(barrier, 7 + others - 1 + 2)
+
+    depth = parts.shape[1]
     wide = CH // LANES
-    parts[...] = jnp.zeros_like(parts)
-    for at in range(wide + 1):
+    for at in range(8 * depth // 8):
         if at < INNER // LANES:
             block = taps_ref[:, LANES * at : LANES * (at + 1)]
         elif at < wide:
             block = small_ref[:, LANES * at - INNER : LANES * (at + 1) - INNER]
+        elif at == wide:
+            block = heads_ref[...]
         else:
-            block = heads_ref[...]
-        parts[at % shards, 8 * (at // shards) : 8 * (at // shards) + 8, :] = block
-    send_all("seq", shards, lambda peer: parts.at[peer], slots, send, receive)
+            block = jnp.zeros((8, LANES), F32)
+        parts[at % 8, 8 * (at // 8) : 8 * (at // 8) + 8, :] = block
+    send_all(near, 8, lambda slot: parts.at[slot], slots, send, receive)
+    returns = [
+        pltpu.make_async_remote_copy(
+            src_ref=source, dst_ref=target, send_sem=rows_send.at[at], recv_sem=rows_receive.at[at], device_id=before,
+            device_id_type=MESH,
+        )
+        for at, (source, target) in enumerate(((borrowed_ref, got), (borroweds_ref, got_small)))
+    ]
 
     @pl.when(place > 0)
     def _():
         for copy in returns:
             copy.start()
 
-    slots[place] = parts[place]
-    wait_all("seq", shards, lambda peer: parts.at[peer], slots, send, receive)
+    _, own = near(0)
+    _, far_own = far(0)
+    slots[own] = parts[own]
+    wait_all(near, 8, lambda slot: parts.at[slot], slots, send, receive)
     piece[...] = jnp.sum(slots[...], axis=0)
-    send_all("dp", groups, lambda peer: piece, dp_slots, dp_send, dp_receive)
-    dp_slots[group] = piece[...]
-    wait_all("dp", groups, lambda peer: piece, dp_slots, dp_send, dp_receive)
-    piece[...] = jnp.sum(dp_slots[...], axis=0) * scale
-    send_all("seq", shards, lambda peer: piece, result, back_send, back_receive)
-    result[place] = piece[...]
+    send_all(far, others, lambda slot: piece, far_slots, far_send, far_receive)
+    whole_ref[:, :INNER] = grad_ref[...]
+    whole_ref[:, INNER:] = grads_ref[...]
+    far_slots[far_own] = piece[...]
+    wait_all(far, others, lambda slot: piece, far_slots, far_send, far_receive)
+    piece[...] = jnp.sum(far_slots[...], axis=0) * scale
+    send_all(near, 8, lambda slot: piece, result, back_send, back_receive)
+    result[own] = piece[...]
 
     @pl.when(place > 0)
     def _():
         for copy in returns:
             copy.wait_send()
-
-    rows = 8 - CONV + 1
 
     @pl.when(place < shards - 1)
     def _():
@@ -664,18 +654,13 @@
             copy.wait_recv()
         keep = keep_ref[:, 0:1]
         for lanes, source, end in ((slice(0, INNER), got, end_ref), (slice(INNER, CH), got_small, ends_ref)):
-            last_ref[:8, lanes] = end[:8, :].astype(BF16)
-            late = iota(source.shape, 0) >= rows
-            last_ref[8:, lanes] = (end[8:, :] + jnp.where(late, source[...] * keep, 0.0)).astype(BF16)
-
-    @pl.when(place == shards - 1)
-    def _():
-        last_ref[:, :INNER] = end_ref[...].astype(BF16)
-        last_ref[:, INNER:] = ends_ref[...].astype(BF16)
-
-    wait_all("seq", shards, lambda peer: piece, result, back_send, back_receive)
+            late = iota(source.shape, 0) >= 8 - CONV + 1
+            rows = jnp.concatenate([end[:8, :], end[8:, :] + jnp.where(late, source[...] * keep, 0.0)], axis=0)
+            whole_ref[ROWS - 16 :, lanes] = rows.astype(BF16)
+
+    wait_all(near, 8, lambda slot: piece, result, back_send, back_receive)
     for at in range(wide + 1):
-        block = result[at % shards, 8 * (at // shards) : 8 * (at // shards) + 8, :]
+        block = result[at % 8, 8 * (at // 8) : 8 * (at // 8) + 8, :]
         if at < wide:
             weight_ref[:, LANES * at : LANES * (at + 1)] = block[:CONV]
             bias_ref[:, LANES * at : LANES * (at + 1)] = block[CONV : CONV + 1]
@@ -683,28 +668,27 @@
             heads_out_ref[...] = block
 
 
-def total_stage(shards, groups, scale, *operands):
-    depth = 8 * pl.cdiv(CH // LANES + 1, shards)
+def total_stage(others, scale, *operands):
+    depth = 8 * pl.cdiv(CH // LANES + 1, 8)
     in_vmem = pl.BlockSpec(memory_space=pltpu.VMEM)
     shapes = (
         jax.ShapeDtypeStruct((CONV, CH), F32),
         jax.ShapeDtypeStruct((1, CH), F32),
         jax.ShapeDtypeStruct((8, LANES), F32),
-        jax.ShapeDtypeStruct((16, CH), BF16),
+        jax.ShapeDtypeStruct((ROWS, CH), BF16),
     )
     dma = pltpu.SemaphoreType.DMA
     return pl.pallas_call(
-        functools.partial(total_kernel, shards, groups, scale),
+        functools.partial(total_kernel, scale),
         in_specs=[in_vmem] * len(operands),
         out_specs=[in_vmem] * len(shapes),
         out_shape=shapes,
         scratch_shapes=[
-            pltpu.VMEM((shards, depth, LANES), F32), pltpu.VMEM((shards, depth, LANES), F32),
-            pltpu.VMEM((depth, LANES), F32), pltpu.VMEM((groups, depth, LANES), F32),
-            pltpu.VMEM((shards, depth, LANES), F32),
+            pltpu.VMEM((8, depth, LANES), F32), pltpu.VMEM((8, depth, LANES), F32),
+            pltpu.VMEM((depth, LANES), F32), pltpu.VMEM((others, depth, LANES), F32),
+            pltpu.VMEM((8, depth, LANES), F32),
             pltpu.VMEM((8, INNER), F32), pltpu.VMEM((8, 2 * STATE), F32),
-            dma((shards,)), dma((shards,)), dma((groups,)), dma((groups,)), dma((shards,)), dma((shards,)),
-            dma((2,)), dma((2,)),
+            dma((8,)), dma((8,)), dma((others,)), dma((others,)), dma((8,)), dma((8,)), dma((2,)), dma((2,)),
         ],
         compiler_params=pltpu.CompilerParams(
             vmem_limit_bytes=VMEM_BYTES, collective_id=1, has_side_effects=True
@@ -729,38 +713,34 @@
     core = lax.rem(place, 2)
     half = jnp.stack([core, place // 2, core])
     other_half = jnp.stack([1 - core, place // 2, core])
-    taps = jnp.concatenate([conv_weight, conv_bias[None], jnp.zeros((3, CH), F32)], axis=0)
-    small = jnp.pad(jnp.stack([dt_bias, a_log, skip_gain]), ((0, 5), (0, LANES - HEADS)))
-
-    run, runT, dt, dtT, both, sig, sigsum, all_through, mask, valid, keep, tail, through = head_stage(
-        shards, dt_raw.T, small, doc_start[None], conv_input[ROWS - 16 :]
-    )
+    run, runT, dt, dtT, both, sig, sigsum, mask, valid, keep, tail, own, small, taps = head_stage(
+        dt_raw.T, dt_bias[None], a_log[None], skip_gain[None], doc_start[None], conv_weight, conv_bias[None], conv_input
+    )
+    tail = lax.ppermute(tail, "seq", [(i, i + 1) for i in range(shards - 1)])
+    partner = swap(own)
     theirs, bc = local_stage(group, other_half, conv_input, tail, taps, valid, cotangent, both)
     other = swap(theirs)
     mine, _ = local_stage(group, half, conv_input, tail, taps, valid, cotangent, both)
     other_second = swap(mine)
-    gathered = between_chips(join_stage(group, half, mine, other, all_through))
+    gathered = between_chips(join_stage(group, half, mine, other, own, partner))
     out_in, grad_in, score_grad = within_stage(
         half, conv_input, tail, taps, valid, cotangent, bc, run, runT, dt, dtT, mask
     )
     gathered, out_in, grad_in = lax.optimization_barrier((gathered, out_in, grad_in))
-    chip = between_chips(carry_stage(group, half, gathered, all_through))
+    chip = between_chips(carry_stage(group, half, gathered))
     chip_second = swap(chip)
     operands = (conv_input, tail, taps, conv_input, tail, taps, valid, cotangent, both, out_in, grad_in)
-    first = finish_stage(group, half, operands, chip, other, bc, small, all_through)
+    first = finish_stage(group, half, operands, chip, other, bc, small, own, partner)
     out, grad, end, borrowed, taps_grad, grads, ends, borroweds, tapss_grad, heads = finish_stage(
-        group, other_half, operands, chip_second, other_second, bc, small, all_through,
-        (score_grad, run, dt, sig, sigsum, through), first,
+        group, other_half, operands, chip_second, other_second, bc, small, own, partner,
+        (score_grad, run, dt, sig, sigsum), first,
     )
     groups = lax.axis_size("dp")
-    weight_grad, bias_grad, heads, last = total_stage(
-        shards, groups, float(groups * shards * ROWS) ** (-0.5), taps_grad, tapss_grad, heads, borrowed, borroweds,
-        end, ends, keep,
-    )
-    whole_grad = jnp.concatenate(
-        [jnp.concatenate([grad[: ROWS - 16], grads[: ROWS - 16]], axis=1), last], axis=0
-    )
-    return (out, whole_grad, weight_grad, bias_grad[0], heads[0, :HEADS], heads[1, :HEADS], heads[2, :HEADS])
+    weight_grad, bias_grad, heads, whole_grad = total_stage(
+        groups * shards // 8, float(groups * shards * ROWS) ** (-0.5), taps_grad, tapss_grad, heads, borrowed, borroweds,
+        end, ends, keep, grad, grads,
+    )
+    return (out, whole_grad, weight_grad, bias_grad.reshape(-1), heads[0, :HEADS], heads[1, :HEADS], heads[2, :HEADS])
 
 
 def solution(mesh):

time: 205 us -> 195 us (0.951)
  Pallas kernels: 111 us -> 97.5 us
  starting transfers between devices: 13.4 us -> 22.3 us
  other arithmetic: 7.67 us -> 2.54 us
    pallas_call x2, Pallas kernels: 39 us -> 26.5 us  [the longest x1 24.1 us: total_stage(): pl.pallas_call(functools.partial(total_kernel, scale), in_specs=[in_vmem]...]
    ppermute x0 -> x1, starting transfers between devices: none -> 4.59 us  [on_device(): tail = lax.ppermute(tail, 'seq', [(i, i + 1) for i in range(shards - 1)])]
    slice x3 -> x0, local copies, waits for them, and re-layouts: 3.76 us -> none  [the longest x1 1.6 us: on_device(): conv_input[ROWS - 16:]]
    concatenate x2 -> x0, other arithmetic: 3.74 us -> none  [the longest x1 2.09 us: on_device(): jnp.concatenate([jnp.concatenate([grad[:ROWS - 16], grads[:ROWS - 16]], a...]
    all_to_all x2, starting transfers between devices: 8.88 us -> 12.4 us  [between_chips(): lax.all_to_all(array, 'seq', 0, 0, axis_index_groups=groups, tiled=True)]
    unnamed x9 -> x16, local copies, waits for them, and re-layouts: 3.56 us -> 6.82 us
    ppermute x3 -> x4, starting transfers between devices: 4.47 us -> 5.37 us  [swap(): lax.ppermute(array, 'seq', [(i, i ^ 1) for i in range(lax.axis_size('seq'...]
  transfers between devices with their start and end apart: 5 -> 7, of which waited for: 2 -> 3; matrix products, arithmetic and copies ran while one was open for 0% -> 1% of each run, Pallas kernels for 18% -> 19%
where the time goes in v5:
time: 195 us; the launch traced here: 194 us
  Pallas kernels  97.5 us (50%)
  waiting for transfers between devices  61.8 us (32%)
  starting transfers between devices  22.3 us (11%)
  local copies, waits for them, and re-layouts  9.49 us (5%)
  other arithmetic  2.54 us (1%)
    pallas_call x7, Pallas kernels, call(): pl.pallas_call(kernel, grid_spec=pltpu.PrefetchScalarGridSpec(num_scalar_...  71.1 us
    all_to_all x2, waiting for transfers between devices, between_chips(): lax.all_to_all(array, 'seq', 0, 0, axis_index_groups=groups, tiled=True)  60.6 us
    pallas_call x1, Pallas kernels, total_stage(): pl.pallas_call(functools.partial(total_kernel, scale), in_specs=[in_vmem]...  24.1 us
    all_to_all x2, starting transfers between devices, between_chips(): lax.all_to_all(array, 'seq', 0, 0, axis_index_groups=groups, tiled=True)  12.4 us
    unnamed x16, local copies, waits for them, and re-layouts  6.82 us
    ppermute x4, starting transfers between devices, swap(): lax.ppermute(array, 'seq', [(i, i ^ 1) for i in range(lax.axis_size('seq'...  5.37 us
    ppermute x1, starting transfers between devices, on_device(): tail = lax.ppermute(tail, 'seq', [(i, i + 1) for i in range(shards - 1)])  4.59 us
  transfers between devices with their start and end apart: 7, of which 3 were waited for; matrix products, arithmetic and copies ran while one was open for 1% of the time, Pallas kernels for 19%

profile of v5, /device:TPU:1, one launch (start us, length us, event | category | flops | bytes accessed | tf_op | source)
XLA Modules:
  0.0 194.5 jit_solution(8521695206970112204)
XLA Ops:
  0.6 1.4 broadcast_in_dim.19.bias_ref
  2.0 2.4 %heads.1 = (f32[128,128]{1,0:T(8,128)}, f32[128,128]{1,0:T(8,128)}, f32[128,128]{1,0:T(8,128)}, f32[128,128]{1,0:T(8,128)}, bf16[256,256]{1,0:T(8,128)(2,1)}, /*...) custom-call(f32[80,128]{1,0:T(8,128)} %bitcast.14, ...), custom_call_target="tpu_custom_call" | custom-call | tf_op jit(solution)/shard_map/heads/pallas_call | solution.py:197
  4.4 0.0 copy-start.5
  4.4 4.6 %collective-permute-start = (bf16[8,5376]{1,0:T(8,128)(2,1)}, bf16[8,5376]{1,0:T(8,128)(2,1)S(1)}, u32[]{:S(2)}, u32[]{:S(2)}) collective-permute-start(bf16[8,5376]{1,0:T(8,128)(2,1)} %get-tuple-element.52), channel_id=1, source_target_pairs={{0,1},{1,2},{2,3},{3,4},{4,5},{5,6},{6,7},{7,8},{8,9},{9,10},{10,1... | collective-permute-start | bytes 258056 | tf_op jit(solution)/shard_map/ppermute | solution.py:719
  9.0 0.6 add_add_fusion.half_ref
  9.6 1.2 collective-permute-done.tail_ref.tails_ref
  10.8 0.0 copy-start.3
  10.8 0.6 copy-done.3
  11.5 7.9 %local.3 = (f32[16,16,2560]{2,1,0:T(8,128)}, f32[128,256]{1,0:T(8,128)}) custom-call(s32[3]{0:T(128)} %add_add_fusion.half_ref, bf16[128,5376]{1,0:T(8,128)(2,1)} %xs_ref.7, bf16[8,5376]{1,0:T(8,128)(2,1)} %copy-done.3, f32[8,5376]{1,0:T(8,128)} %get-tuple-element.53.taps_ref.tapss_ref, bf16[128,5376]{1,0:T(8,128)(2,1)} %xs_ref.7, ...), custom_call_target="tpu_custom_call" | custom-call | tf_op jit(solution)/shard_map/local/pallas_call | solution.py:214
  19.3 0.0 collective-permute-start.1
  19.3 0.0 copy-done.5
  19.3 0.5 collective-permute-start.2
  19.8 0.6 add_add_fusion.1.half_ref
  20.4 7.9 %local.2 = (f32[16,16,2560]{2,1,0:T(8,128)}, f32[128,256]{1,0:T(8,128)}) custom-call(s32[3]{0:T(128)} %add_add_fusion.1.half_ref, bf16[128,5376]{1,0:T(8,128)(2,1)} %xs_ref.7, bf16[8,5376]{1,0:T(8,128)(2,1)} %copy-done.3, f32[8,5376]{1,0:T(8,128)} %get-tuple-element.53.taps_ref.tapss_ref, bf16[128,5376]{1,0:T(8,128)(2,1)} %xs_ref.7, ...), custom_call_target="tpu_custom_call" | custom-call | tf_op jit(solution)/shard_map/local/pallas_call | solution.py:214
  28.3 0.0 collective-permute-done.2.partner_ref
  28.4 0.0 copy-start.6
  28.4 0.0 collective-permute-done.1.other_ref.local_ref
  28.4 0.0 copy-start.1
  28.4 0.6 copy-done.6
  28.9 0.9 copy-done.1
  29.9 5.7 %join.1 = f32[16,16,2688]{2,1,0:T(8,128)} custom-call(s32[3]{0:T(128)} %add_add_fusion.1.half_ref, f32[16,16,2560]{2,1,0:T(8,128)} %get-tuple-element.56.mine_ref, f32[16,16,2560]{2,1,0:T(8,128)} %copy-done.1, f32[8,128]{1,0:T(8,128)} %get-tuple-element.58.own_ref, f32[8,128]{1,0:T(8,128)} %copy-done.6), custom_call_target="tpu_custom_call" | custom-call | tf_op jit(solution)/shard_map/join/pallas_call | solution.py:214
  35.6 8.4 %all-to-all-start = ((f32[16,16,2688]{2,1,0:T(8,128)}), f32[16,16,2688]{2,1,0:T(8,128)S(1)}, u32[]{:S(2)}, u32[]{:S(2)}) async-start(f32[16,16,2688]{2,1,0:T(8,128)} %join.1), calls=%async_computation | async-start | bytes 5505024 | tf_op jit(solution)/shard_map/all_to_all | solution.py:707
  44.0 15.0 %within.1 = (f32[128,5120]{1,0:T(8,128)}, f32[128,5120]{1,0:T(8,128)}, f32[128,128]{1,0:T(8,128)}) custom-call(s32[3]{0:T(128)} %add_add_fusion.1.half_ref, bf16[128,5376]{1,0:T(8,128)(2,1)} %xs_ref.7, bf16[8,5376]{1,0:T(8,128)(2,1)} %copy-done.3, f32[8,5376]{1,0:T(8,128)} %get-tuple-element.53.taps_ref.tapss_ref, f32[128,8]{1,0:T(8,128)} %get-tuple-element.54.valid_ref, ...), custom_call_target="tpu_custom_call" | custom-call | tf_op jit(solution)/shard_map/within/pallas_call | solution.py:214
  59.0 26.6 %all-to-all-done.pair_ref.rest_ref = f32[16,16,2688]{2,1,0:T(8,128)S(1)} async-done(((f32[16,16,2688]{2,1,0:T(8,128)}), f32[16,16,2688]{2,1,0:T(8,128)S(1)}, u32[]{:S(2)}, u32[]{:S(2)}) %all-to-all-start) | async-done | bytes 2752544 | tf_op jit(solution)/shard_map/all_to_all | solution.py:707
  85.5 0.0 copy-start
  85.5 1.6 copy-done
  87.1 6.1 %carry.1 = f32[16,16,2560]{2,1,0:T(8,128)} custom-call(s32[3]{0:T(128)} %add_add_fusion.1.half_ref, f32[16,16,2688]{2,1,0:T(8,128)} %copy-done, f32[16,16,2688]{2,1,0:T(8,128)} %copy-done), custom_call_target="tpu_custom_call" | custom-call | tf_op jit(solution)/shard_map/carry/pallas_call | solution.py:214
  93.2 3.9 %all-to-all-start.1 = ((f32[16,16,2560]{2,1,0:T(8,128)}), f32[16,16,2560]{2,1,0:T(8,128)S(1)}, u32[]{:S(2)}, u32[]{:S(2)}) async-start(f32[16,16,2560]{2,1,0:T(8,128)} %carry.1), calls=%async_computation.1 | async-start | bytes 5242880 | tf_op jit(solution)/shard_map/all_to_all | solution.py:707
  97.1 1.9 collective-permute-start.4
  99.0 34.0 %all-to-all-done.1.chip_ref = f32[16,16,2560]{2,1,0:T(8,128)S(1)} async-done(((f32[16,16,2560]{2,1,0:T(8,128)}), f32[16,16,2560]{2,1,0:T(8,128)S(1)}, u32[]{:S(2)}, u32[]{:S(2)}) %all-to-all-start.1) | async-done | bytes 2621472 | tf_op jit(solution)/shard_map/all_to_all | solution.py:707
  133.0 0.0 copy-start.2
  133.0 3.0 %collective-permute-start.3 = (f32[16,16,2560]{2,1,0:T(8,128)S(1)}, f32[16,16,2560]{2,1,0:T(8,128)}, u32[]{:S(2)}, u32[]{:S(2)}) collective-permute-start(f32[16,16,2560]{2,1,0:T(8,128)S(1)} %all-to-all-done.1.chip_ref), channel_id=1, source_target_pairs={{0,1},{1,0},{2,3},{3,2},{4,5},{5,4},{6,7},{7,6},{8,9},{9,8},{10,11... | collective-permute-start | bytes 7864328 | tf_op jit(solution)/shard_map/ppermute | solution.py:701
  136.0 0.0 copy-done.2
  136.0 13.6 %finish_first.1 = (bf16[128,5120]{1,0:T(8,128)(2,1)}, bf16[128,5120]{1,0:T(8,128)(2,1)}, f32[16,5120]{1,0:T(8,128)}, f32[8,5120]{1,0:T(8,128)}, f32[8,5120]{1,0:...) custom-call(s32[3]{0:T(128)} %add_add_fusion.1.half_ref, bf16[128,5376]{1,0:T(8,128)(2,1)} %xs_ref.7, ...), custom_call_target="tpu_custom_call" | custom-call | tf_op jit(solution)/shard_map/finish_first/pallas_call | solution.py:214
  149.6 0.0 collective-permute-done.4.local_ref
  149.6 0.0 collective-permute-done.3.chip_ref
  149.6 14.9 %finish_second.1 = (bf16[128,5120]{1,0:T(8,128)(2,1)}, bf16[128,5120]{1,0:T(8,128)(2,1)}, f32[16,5120]{1,0:T(8,128)}, f32[8,5120]{1,0:T(8,128)}, f32[8,5120]{1,0...) custom-call(s32[3]{0:T(128)} %add_add_fusion.half_ref, ...), custom_call_target="tpu_custom_call", output_to_operand_aliasing={{0}: (26, {}), {1}: (27, {}), {2}: (28, {}), {3}: (29, {}),... | custom-call | tf_op jit(solution)/shard_map/finish_second/pallas_call | solution.py:214
  164.5 24.1 %totals.1 = (f32[4,5376]{1,0:T(4,128)}, f32[1,5376]{1,0:T(1,128)}, f32[8,128]{1,0:T(8,128)}, bf16[128,5376]{1,0:T(8,128)(2,1)}) custom-call(f32[8,5120]{1,0:T(8,128)} %get-tuple-element.83.taps_ref, f32[8,256]{1,0:T(8,128)} %get-tuple-element.84.small_ref, f32[8,128]{1,0:T(8,128)} %get-tuple-element.85.heads_ref, f32[8,5120]{1,0:T(8,128)} %get-tuple-element.86.borrowed_ref, ...), custom_call_target="tpu_custom_call" | custom-call | tf_op jit(solution)/shard_map/totals/pallas_call | solution.py:681
  188.6 0.0 copy-start.4
  188.6 1.3 slice_bitcast_fusion
  189.9 1.4 reduce
  191.3 2.5 %copy.28 = bf16[128,5376]{1,0:T(8,128)(2,1)} copy(bf16[128,5376]{1,0:T(8,128)(2,1)} %get-tuple-element.108) | data formatting | bytes 2752512
  193.8 0.0 copy-done.4
  193.8 0.6 copy.29
Async XLA Ops:
  4.4 14.9 %copy-start.5 = (f32[8,128]{1,0:T(8,128)S(1)}, f32[8,128]{1,0:T(8,128)}, u32[]{:S(2)}) copy-start(f32[8,128]{1,0:T(8,128)} %get-tuple-element.58.own_ref) | copy-start | bytes 12292
  4.4 6.4 %collective-permute-start = (bf16[8,5376]{1,0:T(8,128)(2,1)}, bf16[8,5376]{1,0:T(8,128)(2,1)S(1)}, u32[]{:S(2)}, u32[]{:S(2)}) collective-permute-start(bf16[8,5376]{1,0:T(8,128)(2,1)} %get-tuple-element.52), channel_id=1, source_target_pairs={{0,1},{1,2},{2,3},{3,4},{4,5},{5,6},{6,7},{7,8},{8,9},{9,10},{10,1... | collective-permute-start | bytes 258056 | tf_op jit(solution)/shard_map/ppermute | solution.py:719
  10.8 0.6 copy-start.3
  19.3 9.0 %collective-permute-start.1 = (f32[16,16,2560]{2,1,0:T(8,128)}, f32[16,16,2560]{2,1,0:T(8,128)S(1)}, u32[]{:S(2)}, u32[]{:S(2)}) collective-permute-start(f32[16,16,2560]{2,1,0:T(8,128)} %get-tuple-element.57), channel_id=1, source_target_pairs={{0,1},{1,0},{2,3},{3,2},{4,5},{5,4},{6,7},{7,6},{8,9},{9,8},{10,11... | collective-permute-start | bytes 7864328 | tf_op jit(solution)/shard_map/ppermute | solution.py:701
  19.3 9.0 %collective-permute-start.2 = (f32[8,128]{1,0:T(8,128)S(1)}, f32[8,128]{1,0:T(8,128)S(1)}, u32[]{:S(2)}, u32[]{:S(2)}) collective-permute-start(f32[8,128]{1,0:T(8,128)S(1)} %copy-done.5), channel_id=1, source_target_pairs={{0,1},{1,0},{2,3},{3,2},{4,5},{5,4},{6,7},{7,6},{8,9},{9,8},{10,11... | collective-permute-start | bytes 12296 | tf_op jit(solution)/shard_map/ppermute | solution.py:701
  28.4 0.6 copy-start.6
  28.4 1.5 copy-start.1
  35.6 50.0 %all-to-all-start = ((f32[16,16,2688]{2,1,0:T(8,128)}), f32[16,16,2688]{2,1,0:T(8,128)S(1)}, u32[]{:S(2)}, u32[]{:S(2)}) async-start(f32[16,16,2688]{2,1,0:T(8,128)} %join.1), calls=%async_computation | async-start | bytes 5505024 | tf_op jit(solution)/shard_map/all_to_all | solution.py:707
  85.5 1.6 copy-start
  93.2 39.8 %all-to-all-start.1 = ((f32[16,16,2560]{2,1,0:T(8,128)}), f32[16,16,2560]{2,1,0:T(8,128)S(1)}, u32[]{:S(2)}, u32[]{:S(2)}) async-start(f32[16,16,2560]{2,1,0:T(8,128)} %carry.1), calls=%async_computation.1 | async-start | bytes 5242880 | tf_op jit(solution)/shard_map/all_to_all | solution.py:707
  97.1 52.5 %collective-permute-start.4 = (f32[16,16,2560]{2,1,0:T(8,128)}, f32[16,16,2560]{2,1,0:T(8,128)}, u32[]{:S(2)}, u32[]{:S(2)}) collective-permute-start(f32[16,16,2560]{2,1,0:T(8,128)} %get-tuple-element.56.mine_ref), channel_id=1, source_target_pairs={{0,1},{1,0},{2,3},{3,2},{4,5},{5,4},{6,7},{7,6},{8,9},{9,8},{10,11... | collective-permute-start | bytes 7864328 | tf_op jit(solution)/shard_map/ppermute | solution.py:701
  133.0 3.0 %copy-start.2 = (f32[16,16,2560]{2,1,0:T(8,128)}, f32[16,16,2560]{2,1,0:T(8,128)S(1)}, u32[]{:S(2)}) copy-start(f32[16,16,2560]{2,1,0:T(8,128)S(1)} %all-to-all-done.1.chip_ref) | copy-start | bytes 7864324
  133.0 16.6 %collective-permute-start.3 = (f32[16,16,2560]{2,1,0:T(8,128)S(1)}, f32[16,16,2560]{2,1,0:T(8,128)}, u32[]{:S(2)}, u32[]{:S(2)}) collective-permute-start(f32[16,16,2560]{2,1,0:T(8,128)S(1)} %all-to-all-done.1.chip_ref), channel_id=1, source_target_pairs={{0,1},{1,0},{2,3},{3,2},{4,5},{5,4},{6,7},{7,6},{8,9},{9,8},{10,11... | collective-permute-start | bytes 7864328 | tf_op jit(solution)/shard_map/ppermute | solution.py:701
  188.6 5.2 %copy-start.4 = (f32[4,5376]{1,0:T(4,128)S(1)}, f32[4,5376]{1,0:T(4,128)}, u32[]{:S(2)}) copy-start(f32[4,5376]{1,0:T(4,128)} %get-tuple-element.109) | copy-start | bytes 258052

commit v6 on v5

--- a/solution.py
+++ b/solution.py
@@ -388,28 +388,70 @@
     )
 
 
-def carry_kernel(group, half_ref, pair_ref, rest_ref, out_ref, decay):
+ORDER = (10, 1, 4, 3, 12, 11, 9, 14, 6, 2, 8, 5, 15, 7, 13)
+
+
+def chip_after(k):
+    chip = lax.axis_index("seq") // 2
+    return lax.rem(chip // 4 + k // 4, 4) * 4 + lax.rem(lax.rem(chip, 4) + k % 4, 4)
+
+
+def carry_kernel(group, pair_ref, out_ref, ready, decay, send, receive):
     chips = pair_ref.shape[0]
-    one_hot = head_columns(tile_at(pl.program_id(0), half_ref))
-    decay[...] = spread_exact(jnp.max(rest_ref[...], axis=1), one_hot)
-    state = jnp.zeros((group, TILE), F32)
-    adjoint = jnp.zeros((group, TILE), F32)
-    for chip in range(chips):
-        out_ref[chip, :group, :] = state
-        state = decay[chip : chip + 1, :] * state + pair_ref[chip, :group, :]
-        back = chips - 1 - chip
-        out_ref[back, group:, :] = adjoint
-        adjoint = decay[back : back + 1, :] * adjoint + pair_ref[back, group:, :]
-
-
-def carry_stage(group, half, pairs):
+    chip, core = lax.axis_index("seq") // 2, lax.rem(lax.axis_index("seq"), 2)
+
+    def device(other):
+        return (lax.axis_index("dp"), 2 * other + core)
+
+    barrier = pltpu.get_barrier_semaphore()
+    for k in ORDER:
+        pl.semaphore_signal(barrier, inc=1, device_id=device(chip_after(k)), device_id_type=MESH)
+    by_head = jnp.max(pair_ref[:, :, INNER // 2 :], axis=1)
+    for at in range(HALF_TILES):
+        lanes = slice(TILE * at, TILE * (at + 1))
+        decay[:, lanes] = spread_exact(by_head, head_columns(HALF_TILES * core + at))
+        state = jnp.zeros((group, TILE), F32)
+        adjoint = jnp.zeros((group, TILE), F32)
+        for here in range(chips):
+            ready[here, :group, lanes] = state
+            state = decay[here : here + 1, lanes] * state + pair_ref[here, :group, lanes]
+            back = chips - 1 - here
+            ready[back, group:, lanes] = adjoint
+            adjoint = decay[back : back + 1, lanes] * adjoint + pair_ref[back, group:, lanes]
+    pl.semaphore_wait(barrier, len(ORDER))
+    for k in ORDER:
+        other = chip_after(k)
+        pltpu.make_async_remote_copy(
+            src_ref=ready.at[other], dst_ref=out_ref.at[chip], send_sem=send.at[other], recv_sem=receive.at[chip],
+            device_id=device(other), device_id_type=MESH,
+        ).start()
+    out_ref[chip] = ready[chip]
+    for k in ORDER:
+        other = chip_after(k)
+        copy = pltpu.make_async_remote_copy(
+            src_ref=ready.at[other], dst_ref=out_ref.at[other], send_sem=send.at[other], recv_sem=receive.at[other],
+            device_id=device(other), device_id_type=MESH,
+        )
+        copy.wait_send()
+        copy.wait_recv()
+
+
+def carry_stage(group, pairs):
     chips, rows, width = pairs.shape
     shape = (chips, rows, width - LANES)
-    return call(
-        functools.partial(carry_kernel, group), "carry", half, HALF_TILES,
-        [pair_spec(shape, True), pl.BlockSpec((chips, rows, LANES), lambda *at: (0, 0, shape[2] // LANES))],
-        pair_spec(shape, True), jax.ShapeDtypeStruct(shape, F32), [pltpu.VMEM((chips, TILE), F32)], (pairs, pairs),
-    )
+    in_vmem = pl.BlockSpec(memory_space=pltpu.VMEM)
+    return pl.pallas_call(
+        functools.partial(carry_kernel, group),
+        in_specs=[in_vmem],
+        out_specs=in_vmem,
+        out_shape=jax.ShapeDtypeStruct(shape, F32),
+        scratch_shapes=[
+            pltpu.VMEM(shape, F32), pltpu.VMEM((chips, shape[2]), F32),
+            pltpu.SemaphoreType.DMA((chips,)), pltpu.SemaphoreType.DMA((chips,)),
+        ],
+        compiler_params=pltpu.CompilerParams(vmem_limit_bytes=24 << 20, collective_id=2, has_side_effects=True),
+        name="carry",
+    )(pairs)
 
 
 def conv_backward(grad, shifted, taps, valid):
@@ -586,8 +628,8 @@
     )
 
 
-def total_kernel(scale, taps_ref, small_ref, heads_ref, borrowed_ref, borroweds_ref, end_ref, ends_ref, keep_ref, grad_ref,
-                 grads_ref, weight_ref, bias_ref, heads_out_ref, whole_ref,
+def total_kernel(scale, taps_ref, small_ref, heads_ref, borrowed_ref, borroweds_ref, end_ref, ends_ref, keep_ref,
+                 sums_ref, last_ref,
                  parts, slots, piece, far_slots, result, got, got_small, send, receive, far_send, far_receive, back_send,
                  back_receive, rows_send, rows_receive):
     shards, groups = lax.axis_size("seq"), lax.axis_size("dp")
@@ -635,8 +677,6 @@
     wait_all(near, 8, lambda slot: parts.at[slot], slots, send, receive)
     piece[...] = jnp.sum(slots[...], axis=0)
     send_all(far, others, lambda slot: piece, far_slots, far_send, far_receive)
-    whole_ref[:, :INNER] = grad_ref[...]
-    whole_ref[:, INNER:] = grads_ref[...]
     far_slots[far_own] = piece[...]
     wait_all(far, others, lambda slot: piece, far_slots, far_send, far_receive)
     piece[...] = jnp.sum(far_slots[...], axis=0) * scale
@@ -656,27 +696,66 @@
         for lanes, source, end in ((slice(0, INNER), got, end_ref), (slice(INNER, CH), got_small, ends_ref)):
             late = iota(source.shape, 0) >= 8 - CONV + 1
             rows = jnp.concatenate([end[:8, :], end[8:, :] + jnp.where(late, source[...] * keep, 0.0)], axis=0)
-            whole_ref[ROWS - 16 :, lanes] = rows.astype(BF16)
+            last_ref[:, lanes] = rows.astype(BF16)
+
+    @pl.when(place == shards - 1)
+    def _():
+        last_ref[:, :INNER] = end_ref[...].astype(BF16)
+        last_ref[:, INNER:] = ends_ref[...].astype(BF16)
 
     wait_all(near, 8, lambda slot: piece, result, back_send, back_receive)
     for at in range(wide + 1):
-        block = result[at % 8, 8 * (at // 8) : 8 * (at // 8) + 8, :]
-        if at < wide:
-            weight_ref[:, LANES * at : LANES * (at + 1)] = block[:CONV]
-            bias_ref[:, LANES * at : LANES * (at + 1)] = block[CONV : CONV + 1]
-        else:
-            heads_out_ref[...] = block
+        sums_ref[:, LANES * at : LANES * (at + 1)] = result[at % 8, 8 * (at // 8) : 8 * (at // 8) + 8, :]
+
+
+def layout_kernel(sums_ref, last_ref, grad_ref, grads_ref, weight_ref, bias_ref, dt_bias_ref, a_log_ref, gain_ref,
+                  whole_ref):
+    step = pl.program_id(0)
+
+    @pl.when(step == 0)
+    def _():
+        weight_ref[...] = sums_ref[:CONV, :CH]
+        bias_ref[...] = sums_ref[CONV : CONV + 1, :CH].reshape(CH)
+        for at, target in enumerate((dt_bias_ref, a_log_ref, gain_ref)):
+            target[...] = sums_ref[at : at + 1, CH : CH + HEADS].reshape(HEADS)
+
+    @pl.when(step < pl.num_programs(0) - 1)
+    def _():
+        whole_ref[:, :INNER] = grad_ref[...]
+        whole_ref[:, INNER:] = grads_ref[...]
+
+    @pl.when(step == pl.num_programs(0) - 1)
+    def _():
+        whole_ref[: whole_ref.shape[0] - 16, :INNER] = grad_ref[: whole_ref.shape[0] - 16, :]
+        whole_ref[: whole_ref.shape[0] - 16, INNER:] = grads_ref[: whole_ref.shape[0] - 16, :]
+        whole_ref[whole_ref.shape[0] - 16 :, :] = last_ref[...]
+
+
+def layout_stage(sums, last, grad, grads):
+    rows = 32
+    shapes = (
+        jax.ShapeDtypeStruct((CONV, CH), F32),
+        jax.ShapeDtypeStruct((CH,), F32),
+        jax.ShapeDtypeStruct((HEADS,), F32),
+        jax.ShapeDtypeStruct((HEADS,), F32),
+        jax.ShapeDtypeStruct((HEADS,), F32),
+        jax.ShapeDtypeStruct((ROWS, CH), BF16),
+    )
+    blocks = [pl.BlockSpec((rows, width), lambda i: (i, 0)) for width in (INNER, 2 * STATE, CH)]
+    return pl.pallas_call(
+        layout_kernel,
+        grid=(ROWS // rows,),
+        in_specs=[whole(sums.shape), whole(last.shape)] + blocks[:2],
+        out_specs=[whole(part.shape) for part in shapes[:5]] + blocks[2:],
+        out_shape=shapes,
+        name="layout",
+    )(sums, last, grad, grads)
 
 
 def total_stage(others, scale, *operands):
     depth = 8 * pl.cdiv(CH // LANES + 1, 8)
     in_vmem = pl.BlockSpec(memory_space=pltpu.VMEM)
-    shapes = (
-        jax.ShapeDtypeStruct((CONV, CH), F32),
-        jax.ShapeDtypeStruct((1, CH), F32),
-        jax.ShapeDtypeStruct((8, LANES), F32),
-        jax.ShapeDtypeStruct((ROWS, CH), BF16),
-    )
+    shapes = (jax.ShapeDtypeStruct((8, CH + LANES), F32), jax.ShapeDtypeStruct((16, CH), BF16))
     dma = pltpu.SemaphoreType.DMA
     return pl.pallas_call(
         functools.partial(total_kernel, scale),
@@ -727,7 +806,7 @@
         half, conv_input, tail, taps, valid, cotangent, bc, run, runT, dt, dtT, mask
     )
     gathered, out_in, grad_in = lax.optimization_barrier((gathered, out_in, grad_in))
-    chip = between_chips(carry_stage(group, half, gathered))
+    chip = carry_stage(group, gathered)
     chip_second = swap(chip)
     operands = (conv_input, tail, taps, conv_input, tail, taps, valid, cotangent, both, out_in, grad_in)
     first = finish_stage(group, half, operands, chip, other, bc, small, own, partner)
@@ -736,11 +815,12 @@
         (score_grad, run, dt, sig, sigsum), first,
     )
     groups = lax.axis_size("dp")
-    weight_grad, bias_grad, heads, whole_grad = total_stage(
+    sums, last = total_stage(
         groups * shards // 8, float(groups * shards * ROWS) ** (-0.5), taps_grad, tapss_grad, heads, borrowed, borroweds,
-        end, ends, keep, grad, grads,
-    )
-    return (out, whole_grad, weight_grad, bias_grad.reshape(-1), heads[0, :HEADS], heads[1, :HEADS], heads[2, :HEADS])
+        end, ends, keep,
+    )
+    weight_grad, bias_grad, dt_bias_grad, a_log_grad, gain_grad, whole_grad = layout_stage(sums, last, grad, grads)
+    return (out, whole_grad, weight_grad, bias_grad, dt_bias_grad, a_log_grad, gain_grad)
 
 
 def solution(mesh):

time: 195 us -> 179 us (0.918)
  waiting for transfers between devices: 61.8 us -> 27 us
  Pallas kernels: 97.5 us -> 129 us
  starting transfers between devices: 22.3 us -> 15.4 us
  local copies, waits for them, and re-layouts: 9.49 us -> 4.98 us
    pallas_call x0 -> x2, Pallas kernels: none -> 39.3 us  [the longest x1 35.6 us: carry_stage(): pl.pallas_call(functools.partial(carry_kernel, group), in_specs=[in_vmem]...]
    all_to_all x2 -> x1, waiting for transfers between devices: 60.6 us -> 25.8 us  [between_chips(): lax.all_to_all(array, 'seq', 0, 0, axis_index_groups=groups, tiled=True)]
    pallas_call x7 -> x6, Pallas kernels: 71.1 us -> 64.9 us  [call(): pl.pallas_call(kernel, grid_spec=pltpu.PrefetchScalarGridSpec(num_scalar_...]
    all_to_all x2 -> x1, starting transfers between devices: 12.4 us -> 8.45 us  [between_chips(): lax.all_to_all(array, 'seq', 0, 0, axis_index_groups=groups, tiled=True)]
    unnamed x16 -> x10, local copies, waits for them, and re-layouts: 6.82 us -> 3.62 us
    ppermute x4, starting transfers between devices: 5.37 us -> 2.39 us  [swap(): lax.ppermute(array, 'seq', [(i, i ^ 1) for i in range(lax.axis_size('seq'...]
  transfers between devices with their start and end apart: 7 -> 6, of which waited for: 3 -> 2; matrix products, arithmetic and copies ran while one was open for 1% -> 1% of each run, Pallas kernels for 19% -> 40%
where the time goes in v6:
time: 179 us; the launch traced here: 178 us
  Pallas kernels  129 us (72%)
  waiting for transfers between devices  27 us (15%)
  starting transfers between devices  15.4 us (9%)
  local copies, waits for them, and re-layouts  4.98 us (3%)
    pallas_call x6, Pallas kernels, call(): pl.pallas_call(kernel, grid_spec=pltpu.PrefetchScalarGridSpec(num_scalar_...  64.9 us
    pallas_call x1, Pallas kernels, carry_stage(): pl.pallas_call(functools.partial(carry_kernel, group), in_specs=[in_vmem]...  35.6 us
    all_to_all x1, waiting for transfers between devices, between_chips(): lax.all_to_all(array, 'seq', 0, 0, axis_index_groups=groups, tiled=True)  25.8 us
    pallas_call x1, Pallas kernels, total_stage(): pl.pallas_call(functools.partial(total_kernel, scale), in_specs=[in_vmem]...  22.4 us
    all_to_all x1, starting transfers between devices, between_chips(): lax.all_to_all(array, 'seq', 0, 0, axis_index_groups=groups, tiled=True)  8.45 us
    ppermute x1, starting transfers between devices, on_device(): tail = lax.ppermute(tail, 'seq', [(i, i + 1) for i in range(shards - 1)])  4.59 us
    pallas_call x1, Pallas kernels, layout_stage(): pl.pallas_call(layout_kernel, grid=(ROWS // rows,), in_specs=[whole(sums....  3.72 us
    unnamed x10, local copies, waits for them, and re-layouts  3.62 us
  transfers between devices with their start and end apart: 6, of which 2 were waited for; matrix products, arithmetic and copies ran while one was open for 1% of the time, Pallas kernels for 40%

profile of v6, /device:TPU:1, one launch (start us, length us, event | category | flops | bytes accessed | tf_op | source)
XLA Modules:
  0.0 178.4 jit_solution(4189996837201474652)
XLA Ops:
  0.6 1.4 broadcast_in_dim.19.bias_ref
  2.0 2.4 %heads.1 = (f32[128,128]{1,0:T(8,128)}, f32[128,128]{1,0:T(8,128)}, f32[128,128]{1,0:T(8,128)}, f32[128,128]{1,0:T(8,128)}, bf16[256,256]{1,0:T(8,128)(2,1)}, /*...) custom-call(f32[80,128]{1,0:T(8,128)} %bitcast.8, ...), custom_call_target="tpu_custom_call" | custom-call | tf_op jit(solution)/shard_map/heads/pallas_call | solution.py:197
  4.4 0.0 copy-start.3
  4.4 4.6 %collective-permute-start = (bf16[8,5376]{1,0:T(8,128)(2,1)}, bf16[8,5376]{1,0:T(8,128)(2,1)S(1)}, u32[]{:S(2)}, u32[]{:S(2)}) collective-permute-start(bf16[8,5376]{1,0:T(8,128)(2,1)} %get-tuple-element.56), channel_id=1, source_target_pairs={{0,1},{1,2},{2,3},{3,4},{4,5},{5,6},{6,7},{7,8},{8,9},{9,10},{10,1... | collective-permute-start | bytes 258056 | tf_op jit(solution)/shard_map/ppermute | solution.py:798
  9.0 0.7 add_add_fusion.half_ref
  9.7 1.2 collective-permute-done.tail_ref.tails_ref
  10.8 0.0 copy-start.1
  10.8 0.6 copy-done.1
  11.4 7.9 %local.3 = (f32[16,16,2560]{2,1,0:T(8,128)}, f32[128,256]{1,0:T(8,128)}) custom-call(s32[3]{0:T(128)} %add_add_fusion.half_ref, bf16[128,5376]{1,0:T(8,128)(2,1)} %xs_ref.7, bf16[8,5376]{1,0:T(8,128)(2,1)} %copy-done.1, f32[8,5376]{1,0:T(8,128)} %get-tuple-element.57.taps_ref.tapss_ref, bf16[128,5376]{1,0:T(8,128)(2,1)} %xs_ref.7, ...), custom_call_target="tpu_custom_call" | custom-call | tf_op jit(solution)/shard_map/local/pallas_call | solution.py:214
  19.4 0.0 collective-permute-start.1
  19.4 0.0 copy-done.3
  19.4 0.5 collective-permute-start.2
  19.9 0.6 add_add_fusion.1.half_ref
  20.5 7.9 %local.2 = (f32[16,16,2560]{2,1,0:T(8,128)}, f32[128,256]{1,0:T(8,128)}) custom-call(s32[3]{0:T(128)} %add_add_fusion.1.half_ref, bf16[128,5376]{1,0:T(8,128)(2,1)} %xs_ref.7, bf16[8,5376]{1,0:T(8,128)(2,1)} %copy-done.1, f32[8,5376]{1,0:T(8,128)} %get-tuple-element.57.taps_ref.tapss_ref, bf16[128,5376]{1,0:T(8,128)(2,1)} %xs_ref.7, ...), custom_call_target="tpu_custom_call" | custom-call | tf_op jit(solution)/shard_map/local/pallas_call | solution.py:214
  28.4 0.0 collective-permute-done.2.partner_ref
  28.4 0.0 copy-start.4
  28.4 0.0 collective-permute-done.1.other_ref.local_ref
  28.4 0.0 copy-start
  28.4 0.6 copy-done.4
  29.0 0.9 copy-done
  29.9 5.7 %join.1 = f32[16,16,2688]{2,1,0:T(8,128)} custom-call(s32[3]{0:T(128)} %add_add_fusion.1.half_ref, f32[16,16,2560]{2,1,0:T(8,128)} %get-tuple-element.60.mine_ref, f32[16,16,2560]{2,1,0:T(8,128)} %copy-done, f32[8,128]{1,0:T(8,128)} %get-tuple-element.62.own_ref, f32[8,128]{1,0:T(8,128)} %copy-done.4), custom_call_target="tpu_custom_call" | custom-call | tf_op jit(solution)/shard_map/join/pallas_call | solution.py:214
  35.6 8.4 %all-to-all-start = ((f32[16,16,2688]{2,1,0:T(8,128)}), f32[16,16,2688]{2,1,0:T(8,128)S(1)}, u32[]{:S(2)}, u32[]{:S(2)}) async-start(f32[16,16,2688]{2,1,0:T(8,128)} %join.1), calls=%async_computation | async-start | bytes 5505024 | tf_op jit(solution)/shard_map/all_to_all | solution.py:786
  44.1 0.8 collective-permute-start.4
  44.8 14.9 %within.1 = (f32[128,5120]{1,0:T(8,128)}, f32[128,5120]{1,0:T(8,128)}, f32[128,128]{1,0:T(8,128)}) custom-call(s32[3]{0:T(128)} %add_add_fusion.1.half_ref, bf16[128,5376]{1,0:T(8,128)(2,1)} %xs_ref.7, bf16[8,5376]{1,0:T(8,128)(2,1)} %copy-done.1, f32[8,5376]{1,0:T(8,128)} %get-tuple-element.57.taps_ref.tapss_ref, f32[128,8]{1,0:T(8,128)} %get-tuple-element.58.valid_ref, ...), custom_call_target="tpu_custom_call" | custom-call | tf_op jit(solution)/shard_map/within/pallas_call | solution.py:214
  59.8 25.8 %all-to-all-done.pair_ref = f32[16,16,2688]{2,1,0:T(8,128)S(1)} async-done(((f32[16,16,2688]{2,1,0:T(8,128)}), f32[16,16,2688]{2,1,0:T(8,128)S(1)}, u32[]{:S(2)}, u32[]{:S(2)}) %all-to-all-start) | async-done | bytes 2752544 | tf_op jit(solution)/shard_map/all_to_all | solution.py:786
  85.6 35.6 %carry.1.chip_ref = f32[16,16,2560]{2,1,0:T(8,128)} custom-call(f32[16,16,2688]{2,1,0:T(8,128)S(1)} %all-to-all-done.pair_ref), custom_call_target="tpu_custom_call" | custom-call | tf_op jit(solution)/shard_map/carry/pallas_call | solution.py:443
  121.2 1.1 collective-permute-start.3
  122.3 13.6 %finish_first.1 = (bf16[128,5120]{1,0:T(8,128)(2,1)}, bf16[128,5120]{1,0:T(8,128)(2,1)}, f32[16,5120]{1,0:T(8,128)}, f32[8,5120]{1,0:T(8,128)}, f32[8,5120]{1,0:...) custom-call(s32[3]{0:T(128)} %add_add_fusion.1.half_ref, bf16[128,5376]{1,0:T(8,128)(2,1)} %xs_ref.7, ...), custom_call_target="tpu_custom_call" | custom-call | tf_op jit(solution)/shard_map/finish_first/pallas_call | solution.py:214
  135.9 0.0 collective-permute-done.4.local_ref
  135.9 0.0 collective-permute-done.3.chip_ref
  135.9 0.0 copy-start.2
  135.9 1.5 copy-done.2
  137.4 14.9 %finish_second.1 = (bf16[128,5120]{1,0:T(8,128)(2,1)}, bf16[128,5120]{1,0:T(8,128)(2,1)}, f32[16,5120]{1,0:T(8,128)}, f32[8,5120]{1,0:T(8,128)}, f32[8,5120]{1,0...) custom-call(s32[3]{0:T(128)} %add_add_fusion.half_ref, ...), custom_call_target="tpu_custom_call", output_to_operand_aliasing={{0}: (26, {}), {1}: (27, {}), {2}: (28, {}), {3}: (29, {}),... | custom-call | tf_op jit(solution)/shard_map/finish_second/pallas_call | solution.py:214
  152.3 22.4 %totals.1 = (f32[8,5504]{1,0:T(8,128)}, bf16[16,5376]{1,0:T(8,128)(2,1)}) custom-call(f32[8,5120]{1,0:T(8,128)} %get-tuple-element.87.taps_ref, f32[8,256]{1,0:T(8,128)} %get-tuple-element.88.small_ref, f32[8,128]{1,0:T(8,128)} %get-tuple-element.89.heads_ref, f32[8,5120]{1,0:T(8,128)} %get-tuple-element.90.borrowed_ref, ...), custom_call_target="tpu_custom_call" | custom-call | tf_op jit(solution)/shard_map/totals/pallas_call | solution.py:760
  174.7 3.7 %layout.1 = (f32[4,5376]{1,0:T(4,128)}, f32[5376]{0:T(1024)}, f32[80]{0:T(128)}, f32[80]{0:T(128)}, f32[80]{0:T(128)}, /*index=5*/bf16[128,5376]{1,0:T(8,128)(2,1)}) custom-call(f32[8,5504]{1,0:T(8,128)} %get-tuple-element.95.sums_ref, bf16[16,5376]{1,0:T(8,128)(2,1)} %get-tuple-element.96.last_ref, bf16[128,5120]{1,0:T(8,128)(2,1)} %get-tuple-element.97.grad_ref, ...), custom_call_target="tpu_custom_call" | custom-call | tf_op jit(solution)/shard_map/layout/pallas_call | solution.py:745
Async XLA Ops:
  4.4 15.0 %copy-start.3 = (f32[8,128]{1,0:T(8,128)S(1)}, f32[8,128]{1,0:T(8,128)}, u32[]{:S(2)}) copy-start(f32[8,128]{1,0:T(8,128)} %get-tuple-element.62.own_ref) | copy-start | bytes 12292
  4.4 6.4 %collective-permute-start = (bf16[8,5376]{1,0:T(8,128)(2,1)}, bf16[8,5376]{1,0:T(8,128)(2,1)S(1)}, u32[]{:S(2)}, u32[]{:S(2)}) collective-permute-start(bf16[8,5376]{1,0:T(8,128)(2,1)} %get-tuple-element.56), channel_id=1, source_target_pairs={{0,1},{1,2},{2,3},{3,4},{4,5},{5,6},{6,7},{7,8},{8,9},{9,10},{10,1... | collective-permute-start | bytes 258056 | tf_op jit(solution)/shard_map/ppermute | solution.py:798
  10.8 0.6 copy-start.1
  19.4 9.0 %collective-permute-start.1 = (f32[16,16,2560]{2,1,0:T(8,128)}, f32[16,16,2560]{2,1,0:T(8,128)S(1)}, u32[]{:S(2)}, u32[]{:S(2)}) collective-permute-start(f32[16,16,2560]{2,1,0:T(8,128)} %get-tuple-element.61), channel_id=1, source_target_pairs={{0,1},{1,0},{2,3},{3,2},{4,5},{5,4},{6,7},{7,6},{8,9},{9,8},{10,11... | collective-permute-start | bytes 7864328 | tf_op jit(solution)/shard_map/ppermute | solution.py:780
  19.4 9.0 %collective-permute-start.2 = (f32[8,128]{1,0:T(8,128)S(1)}, f32[8,128]{1,0:T(8,128)S(1)}, u32[]{:S(2)}, u32[]{:S(2)}) collective-permute-start(f32[8,128]{1,0:T(8,128)S(1)} %copy-done.3), channel_id=1, source_target_pairs={{0,1},{1,0},{2,3},{3,2},{4,5},{5,4},{6,7},{7,6},{8,9},{9,8},{10,11... | collective-permute-start | bytes 12296 | tf_op jit(solution)/shard_map/ppermute | solution.py:780
  28.4 0.6 copy-start.4
  28.4 1.5 copy-start
  35.6 50.0 %all-to-all-start = ((f32[16,16,2688]{2,1,0:T(8,128)}), f32[16,16,2688]{2,1,0:T(8,128)S(1)}, u32[]{:S(2)}, u32[]{:S(2)}) async-start(f32[16,16,2688]{2,1,0:T(8,128)} %join.1), calls=%async_computation | async-start | bytes 5505024 | tf_op jit(solution)/shard_map/all_to_all | solution.py:786
  44.1 91.9 %collective-permute-start.4 = (f32[16,16,2560]{2,1,0:T(8,128)}, f32[16,16,2560]{2,1,0:T(8,128)}, u32[]{:S(2)}, u32[]{:S(2)}) collective-permute-start(f32[16,16,2560]{2,1,0:T(8,128)} %get-tuple-element.60.mine_ref), channel_id=1, source_target_pairs={{0,1},{1,0},{2,3},{3,2},{4,5},{5,4},{6,7},{7,6},{8,9},{9,8},{10,11... | collective-permute-start | bytes 7864328 | tf_op jit(solution)/shard_map/ppermute | solution.py:780
  121.2 14.8 %collective-permute-start.3 = (f32[16,16,2560]{2,1,0:T(8,128)}, f32[16,16,2560]{2,1,0:T(8,128)S(1)}, u32[]{:S(2)}, u32[]{:S(2)}) collective-permute-start(f32[16,16,2560]{2,1,0:T(8,128)} %carry.1.chip_ref), channel_id=1, source_target_pairs={{0,1},{1,0},{2,3},{3,2},{4,5},{5,4},{6,7},{7,6},{8,9},{9,8},{10,11... | collective-permute-start | bytes 7864328 | tf_op jit(solution)/shard_map/ppermute | solution.py:780
  135.9 1.5 copy-start.2

commit v7 on v6

--- a/solution.py
+++ b/solution.py
@@ -23,7 +23,8 @@
 BF16 = jnp.bfloat16
 EXACT = lax.Precision.HIGHEST
 HALF_TILES = TILES // 2
-VMEM_BYTES = 60 << 20
+VMEM_BYTES = 20 << 20
+CARRY_BYTES = 28 << 20
 MESH = pl.DeviceIdType.MESH
 
 
@@ -241,151 +242,81 @@
     return pl.BlockSpec(shape[:2] + (TILE,), lambda i, half: (0, 0, jnp.maximum(i - HALF_TILES, 0)))
 
 
-def local_kernel(group, half_ref, x_ref, tail_ref, taps_ref, xs_ref, tails_ref, tapss_ref, valid_ref, cot_ref,
-                 both_ref, pair_ref, bc_ref, lhs_hi, lhs_lo):
-    valid = valid_ref[...]
-
-    @pl.when(pl.program_id(0) == 0)
-    def _():
-        total, _ = convolve(tails_ref[...].astype(F32), xs_ref[...].astype(F32), tapss_ref[...], valid)
-        small = total * sigmoid(total)
-        bc_ref[...] = small
-        for at, late in ((0, False), (STATE, True)):
-            pick = interleave(group, late).astype(BF16)
-            first, second = halves(small[:, at : at + STATE])
-            lhs_hi[:, at : at + ROWS] = mm_nt(pick, first).astype(BF16)
-            lhs_lo[:, at : at + ROWS] = mm_nt(pick, second).astype(BF16)
-
-    total, _ = convolve(tail_ref[...].astype(F32), x_ref[...].astype(F32), taps_ref[...], valid)
+def local_start(group, xs, tails, tapss, valid, bc_ref, lhs_hi, lhs_lo):
+    total, _ = convolve(tails.astype(F32), xs.astype(F32), tapss, valid)
+    small = total * sigmoid(total)
+    bc_ref[...] = small
+    for at, late in ((0, False), (STATE, True)):
+        pick = interleave(group, late).astype(BF16)
+        first, second = halves(small[:, at : at + STATE])
+        lhs_hi[:, at : at + ROWS] = mm_nt(pick, first).astype(BF16)
+        lhs_lo[:, at : at + ROWS] = mm_nt(pick, second).astype(BF16)
+
+
+def local_tile(tile, x_ref, tail_ref, taps_ref, valid_ref, cot_ref, both_ref, lhs_hi, lhs_lo):
+    columns = pl.ds(pl.multiple_of(TILE * tile, TILE), TILE)
+    total, _ = convolve(
+        tail_ref[:, columns].astype(F32), x_ref[:, columns].astype(F32), taps_ref[:, columns], valid_ref[...]
+    )
     act = total * sigmoid(total)
-    weight = spread_heads(both_ref, tile_at(pl.program_id(0), half_ref))
-    first, second = halves(weight * jnp.concatenate([act, cot_ref[...].astype(F32)], axis=0))
-    result = mm(lhs_hi[...], first) + mm(lhs_hi[...], second) + mm(lhs_lo[...], first)
-    pair_ref[...] = result.reshape(pair_ref.shape)
-
-
-def local_stage(group, half, conv_input, tail, taps, valid, cotangent, both):
-    shape = (STATE // group, 2 * group, INNER // 2)
-    return call(
-        functools.partial(local_kernel, group), "local", half, HALF_TILES,
-        [
-            tile_spec(ROWS), tile_spec(8), tile_spec(8),
-            small_spec(ROWS), small_spec(8), small_spec(8),
-            whole((ROWS, 8)), tile_spec(ROWS), whole((2 * ROWS, 2 * LANES)),
-        ],
-        [pair_spec(shape, True), whole((ROWS, 2 * STATE))],
-        (jax.ShapeDtypeStruct(shape, F32), jax.ShapeDtypeStruct((ROWS, 2 * STATE), F32)),
-        [pltpu.VMEM((2 * STATE, 2 * ROWS), BF16)] * 2,
-        (conv_input, tail, taps, conv_input, tail, taps, valid, cotangent, both),
-    )
-
-
-def within_kernel(half_ref, x_ref, tail_ref, taps_ref, valid_ref, cot_ref, bc_ref, run_ref, runT_ref, dt_ref, dtT_ref,
-                  mask_ref, out_ref, grad_ref, score_grad_ref, score, scoreT):
-    tile = pl.program_id(0)
-
-    @pl.when(tile == 0)
-    def _():
-        keys, reads = bc_ref[:, :STATE], bc_ref[:, STATE:]
-        keys_hi, keys_lo = halves(keys)
-        reads_hi, reads_lo = halves(reads)
-        score[...] = mask_ref[0] * (mm_nt(reads_hi, keys_hi) + mm_nt(reads_hi, keys_lo) + mm_nt(reads_lo, keys_hi))
-        scoreT[...] = mask_ref[1] * (mm_nt(keys_hi, reads_hi) + mm_nt(keys_hi, reads_lo) + mm_nt(keys_lo, reads_hi))
-        score_grad_ref[...] = jnp.zeros_like(score_grad_ref)
-
-    total, _ = convolve(tail_ref[...].astype(F32), x_ref[...].astype(F32), taps_ref[...], valid_ref[...])
+    weight = spread_heads(both_ref, tile)
+    first, second = halves(weight * jnp.concatenate([act, cot_ref[:, columns].astype(F32)], axis=0))
+    return mm(lhs_hi[...], first) + mm(lhs_hi[...], second) + mm(lhs_lo[...], first)
+
+
+def within_start(bc_ref, mask_ref, score_grad_ref, score, scoreT):
+    keys, reads = bc_ref[:, :STATE], bc_ref[:, STATE:]
+    keys_hi, keys_lo = halves(keys)
+    reads_hi, reads_lo = halves(reads)
+    score[...] = mask_ref[0] * (mm_nt(reads_hi, keys_hi) + mm_nt(reads_hi, keys_lo) + mm_nt(reads_lo, keys_hi))
+    scoreT[...] = mask_ref[1] * (mm_nt(keys_hi, reads_hi) + mm_nt(keys_hi, reads_lo) + mm_nt(keys_lo, reads_hi))
+    score_grad_ref[...] = jnp.zeros_like(score_grad_ref)
+
+
+def within_tile(tile, x_ref, tail_ref, taps_ref, valid_ref, cot_ref, runT_ref, dtT_ref, out_ref, grad_ref,
+                score_grad_ref, score, scoreT):
+    at = pl.multiple_of(TILE * tile, TILE)
+    columns = pl.ds(at, TILE)
+    total, _ = convolve(
+        tail_ref[:, columns].astype(F32), x_ref[:, columns].astype(F32), taps_ref[:, columns], valid_ref[...]
+    )
     act = total * sigmoid(total)
-    turn = lax.rem(LANES - TILE_HEADS * tile_at(tile, half_ref), LANES)
-    run = pltpu.roll(run_ref[...], turn, 1)
-    dt = pltpu.roll(dt_ref[...], turn, 1)
+    rows = pl.ds(pl.multiple_of(TILE_HEADS * tile, TILE_HEADS), TILE_HEADS)
+    run_rows, dt_rows = runT_ref[rows, :], dtT_ref[rows, :]
+    run, dt = run_rows.T, dt_rows.T
     left = iota((ROWS, LANES), 1) < HEAD_DIM
     left = jnp.where(left, 1.0, 0.0).astype(BF16)
     right = 1.0 - left
     score_grad = score_grad_ref[...]
     for pair in range(TILE_HEADS // 2):
         lanes = slice(LANES * pair, LANES * (pair + 1))
+        here = pl.ds(at + LANES * pair, LANES)
         spread, weights, weightsT = [], [], []
         for head in (2 * pair, 2 * pair + 1):
-            run_col, run_row = run[:, head : head + 1], runT_ref[head : head + 1, :]
-            difference = run_col - run_row
-            step = jnp.exp(jnp.minimum(difference, 0.0)) * dtT_ref[head : head + 1, :]
+            difference = run[:, head : head + 1] - run_rows[head : head + 1, :]
+            step = jnp.exp(jnp.minimum(difference, 0.0)) * dt_rows[head : head + 1, :]
             spread.append(step)
             weights.append(step * score[...])
             weightsT.append(jnp.exp(jnp.minimum(-difference, 0.0)) * dt[:, head : head + 1] * scoreT[...])
         x_hi, x_lo = halves(act[:, lanes])
-        upstream = cot_ref[:, lanes]
+        upstream = cot_ref[:, here]
         x_hi2 = jnp.concatenate([x_hi * left, x_hi * right], axis=0)
         x_lo2 = jnp.concatenate([x_lo * left, x_lo * right], axis=0)
         upstream2 = jnp.concatenate([upstream * left, upstream * right], axis=0)
         w_hi, w_lo = halves(jnp.concatenate(weights, axis=1))
         wide = mm(w_hi, jnp.concatenate([x_hi2, x_lo2], axis=1))
-        out_ref[:, lanes] = wide[:, :LANES] + wide[:, LANES:] + mm(w_lo, x_hi2)
+        out_ref[:, here] = wide[:, :LANES] + wide[:, LANES:] + mm(w_lo, x_hi2)
         wt_hi, wt_lo = halves(jnp.concatenate(weightsT, axis=1))
-        grad_ref[:, lanes] = mm(wt_hi, upstream2) + mm(wt_lo, upstream2)
+        grad_ref[:, here] = mm(wt_hi, upstream2) + mm(wt_lo, upstream2)
         inner = mm_nt(upstream2, jnp.concatenate([x_hi, x_lo], axis=0))
         inner = inner[:, :ROWS] + inner[:, ROWS:]
         score_grad = score_grad + inner[:ROWS] * spread[0] + inner[ROWS:] * spread[1]
     score_grad_ref[...] = score_grad
 
-    @pl.when(tile == TILES - 1)
-    def _():
-        score_grad_ref[...] = score_grad_ref[...] * mask_ref[0]
-
-
-def within_stage(half, conv_input, tail, taps, valid, cotangent, bc, run, runT, dt, dtT, mask):
-    square = whole((ROWS, LANES))
-    rows = pl.BlockSpec((TILE_HEADS, LANES), lambda i, half: (tile_at(i, half), 0))
-    wide = jax.ShapeDtypeStruct((ROWS, INNER), F32)
-    return call(
-        within_kernel, "within", half, TILES,
-        [
-            tile_spec(ROWS), tile_spec(8), tile_spec(8), whole((ROWS, 8)), tile_spec(ROWS),
-            whole((ROWS, 2 * STATE)), square, rows, square, rows, whole((2, ROWS, ROWS)),
-        ],
-        [tile_spec(ROWS), tile_spec(ROWS), whole((ROWS, ROWS))],
-        (wide, wide, jax.ShapeDtypeStruct((ROWS, ROWS), F32)),
-        [pltpu.VMEM((ROWS, ROWS), F32)] * 2,
-        (conv_input, tail, taps, valid, cotangent, bc, run, runT, dt, dtT, mask),
-    )
-
-
-def even_odd(half_ref, both):
-    even = half_ref[2] == 0
+
+def even_odd(even, both):
     own, partner = both[0:1], both[8:9]
     return jnp.where(even, own, partner)[None], jnp.where(even, partner, own)[None]
-
-
-def join_kernel(group, half_ref, mine_ref, other_ref, own_ref, partner_ref, out_ref, both):
-    @pl.when(pl.program_id(0) == 0)
-    def _():
-        rows = jnp.concatenate([own_ref[...], partner_ref[...]], axis=0)
-        for at in range(HALF_TILES):
-            one_hot = head_columns(HALF_TILES * half_ref[0] + at)
-            both[:, TILE * at : TILE * (at + 1)] = spread_exact(rows, one_hot)
-
-    even = half_ref[2] == 0
-    for at in range(HALF_TILES):
-        lanes = slice(TILE * at, TILE * (at + 1))
-        earlier, later = even_odd(half_ref, both[:, lanes])
-        mine, other = mine_ref[:, :, lanes], other_ref[:, :, lanes]
-        first, second = jnp.where(even, mine, other), jnp.where(even, other, mine)
-        out_ref[:, :group, lanes] = later * first[:, :group] + second[:, :group]
-        out_ref[:, group:, lanes] = first[:, group:] + earlier * second[:, group:]
-    decay = own_ref[0:1, :] * partner_ref[0:1, :]
-    out_ref[:, :, INNER // 2 :] = jnp.broadcast_to(decay[None], out_ref.shape[:2] + (LANES,))
-
-
-def join_stage(group, half, mine, other, own, partner):
-    chips, rows, width = mine.shape
-    step = chips // 4
-    spec = pl.BlockSpec((step, rows, width), lambda i, half: (i, 0, 0))
-    return call(
-        functools.partial(join_kernel, group), "join", half, 4,
-        [spec, spec, whole((8, LANES)), whole((8, LANES))],
-        pl.BlockSpec((step, rows, width + LANES), lambda i, half: (i, 0, 0)),
-        jax.ShapeDtypeStruct((chips, rows, width + LANES), F32), [pltpu.VMEM((16, width), F32)],
-        (mine, other, own, partner),
-    )
 
 
 ORDER = (10, 1, 4, 3, 12, 11, 9, 14, 6, 2, 8, 5, 15, 7, 13)
@@ -396,17 +327,98 @@
     return lax.rem(chip // 4 + k // 4, 4) * 4 + lax.rem(lax.rem(chip, 4) + k % 4, 4)
 
 
-def carry_kernel(group, pair_ref, out_ref, ready, decay, send, receive):
-    chips = pair_ref.shape[0]
-    chip, core = lax.axis_index("seq") // 2, lax.rem(lax.axis_index("seq"), 2)
-
-    def device(other):
-        return (lax.axis_index("dp"), 2 * other + core)
-
+def same_core(chip):
+    return (lax.axis_index("dp"), 2 * chip + lax.rem(lax.axis_index("seq"), 2))
+
+
+def chip_copy(source, target, k, slot, send, receive):
+    other = chip_after(k)
+    slot = other if slot is None else slot
+    return pltpu.make_async_remote_copy(
+        src_ref=source.at[other], dst_ref=target.at[slot], send_sem=send.at[other], recv_sem=receive.at[slot],
+        device_id=same_core(other), device_id_type=MESH,
+    )
+
+
+def pair_copy(source, target, send, receive):
+    place = lax.axis_index("seq")
+    return pltpu.make_async_remote_copy(
+        src_ref=source, dst_ref=target, send_sem=send, recv_sem=receive,
+        device_id=(lax.axis_index("dp"), place + 1 - 2 * lax.rem(place, 2)), device_id_type=MESH,
+    )
+
+
+def carry_kernel(group, x_ref, tail_ref, taps_ref, valid_ref, cot_ref, both_ref, own_ref, runT_ref, dtT_ref, mask_ref,
+                 chips_ref, others_ref, out_ref, grad_ref, score_grad_ref, bc_ref, partner_ref,
+                 mine_ref, theirs_ref, joined, gathered, ready, decay, score, scoreT, lhs_hi, lhs_lo, send, receive,
+                 back_send, back_receive, on_send, on_receive, pair_send, pair_receive):
+    chips = mine_ref.shape[0]
+    place = lax.axis_index("seq")
+    chip, core = place // 2, lax.rem(place, 2)
+    even = core == 0
     barrier = pltpu.get_barrier_semaphore()
+    pl.semaphore_signal(
+        barrier, inc=1, device_id=(lax.axis_index("dp"), place + 1 - 2 * core), device_id_type=MESH
+    )
     for k in ORDER:
-        pl.semaphore_signal(barrier, inc=1, device_id=device(chip_after(k)), device_id_type=MESH)
-    by_head = jnp.max(pair_ref[:, :, INNER // 2 :], axis=1)
+        pl.semaphore_signal(barrier, inc=1, device_id=same_core(chip_after(k)), device_id_type=MESH)
+    local_start(
+        group, x_ref[:, INNER:], tail_ref[:, INNER:], taps_ref[:, INNER:], valid_ref[...], bc_ref, lhs_hi, lhs_lo
+    )
+
+    def local_half(half, target):
+        def tile_step(at, carry):
+            result = local_tile(
+                HALF_TILES * half + at, x_ref, tail_ref, taps_ref, valid_ref, cot_ref, both_ref, lhs_hi, lhs_lo
+            )
+            target[:, :, pl.ds(pl.multiple_of(TILE * at, TILE), TILE)] = result.reshape(chips, 2 * group, TILE)
+            return carry
+
+        lax.fori_loop(0, HALF_TILES, tile_step, 0)
+
+    local_half(1 - core, theirs_ref)
+    pl.semaphore_wait(barrier, len(ORDER) + 1)
+    swaps = [
+        pair_copy(theirs_ref, others_ref.at[0], pair_send.at[0], pair_receive.at[0]),
+        pair_copy(own_ref, partner_ref, pair_send.at[1], pair_receive.at[1]),
+        pair_copy(mine_ref, others_ref.at[1], pair_send.at[2], pair_receive.at[2]),
+    ]
+    swaps[0].start()
+    swaps[1].start()
+    local_half(core, mine_ref)
+    swaps[2].start()
+    swaps[0].wait_recv()
+    swaps[1].wait_recv()
+    rows = jnp.concatenate([own_ref[...], partner_ref[...]], axis=0)
+    for at in range(HALF_TILES):
+        lanes = slice(TILE * at, TILE * (at + 1))
+        earlier, later = even_odd(even, spread_exact(rows, head_columns(HALF_TILES * core + at)))
+        mine, other = mine_ref[:, :, lanes], others_ref[0, :, :, lanes]
+        first, second = jnp.where(even, mine, other), jnp.where(even, other, mine)
+        joined[:, :group, lanes] = later * first[:, :group] + second[:, :group]
+        joined[:, group:, lanes] = first[:, group:] + earlier * second[:, group:]
+    joined[:, :, INNER // 2 :] = jnp.broadcast_to(
+        (own_ref[0:1, :] * partner_ref[0:1, :])[None], joined.shape[:2] + (LANES,)
+    )
+    for k in ORDER:
+        chip_copy(joined, gathered, k, chip, send, receive).start()
+    gathered[chip] = joined[chip]
+
+    within_start(bc_ref, mask_ref, score_grad_ref, score, scoreT)
+
+    def step(tile, carry):
+        within_tile(tile, x_ref, tail_ref, taps_ref, valid_ref, cot_ref, runT_ref, dtT_ref, out_ref, grad_ref,
+                    score_grad_ref, score, scoreT)
+        return carry
+
+    lax.fori_loop(0, TILES, step, 0)
+    score_grad_ref[...] = score_grad_ref[...] * mask_ref[0]
+
+    for k in ORDER:
+        copy = chip_copy(joined, gathered, k, None, send, receive)
+        copy.wait_send()
+        copy.wait_recv()
+    by_head = jnp.max(gathered[:, :, INNER // 2 :], axis=1)
     for at in range(HALF_TILES):
         lanes = slice(TILE * at, TILE * (at + 1))
         decay[:, lanes] = spread_exact(by_head, head_columns(HALF_TILES * core + at))
@@ -414,44 +426,62 @@
         adjoint = jnp.zeros((group, TILE), F32)
         for here in range(chips):
             ready[here, :group, lanes] = state
-            state = decay[here : here + 1, lanes] * state + pair_ref[here, :group, lanes]
+            state = decay[here : here + 1, lanes] * state + gathered[here, :group, lanes]
             back = chips - 1 - here
             ready[back, group:, lanes] = adjoint
-            adjoint = decay[back : back + 1, lanes] * adjoint + pair_ref[back, group:, lanes]
-    pl.semaphore_wait(barrier, len(ORDER))
+            adjoint = decay[back : back + 1, lanes] * adjoint + gathered[back, group:, lanes]
+    own_half = chips_ref.at[0]
     for k in ORDER:
-        other = chip_after(k)
-        pltpu.make_async_remote_copy(
-            src_ref=ready.at[other], dst_ref=out_ref.at[chip], send_sem=send.at[other], recv_sem=receive.at[chip],
-            device_id=device(other), device_id_type=MESH,
-        ).start()
-    out_ref[chip] = ready[chip]
+        chip_copy(ready, own_half, k, chip, back_send, back_receive).start()
+    chips_ref[0, chip] = ready[chip]
+
+    def onward(slot):
+        return pair_copy(chips_ref.at[0, slot], chips_ref.at[1, slot], on_send.at[slot], on_receive.at[slot])
+
+    onward(chip).start()
     for k in ORDER:
-        other = chip_after(k)
-        copy = pltpu.make_async_remote_copy(
-            src_ref=ready.at[other], dst_ref=out_ref.at[other], send_sem=send.at[other], recv_sem=receive.at[other],
-            device_id=device(other), device_id_type=MESH,
-        )
+        chip_copy(ready, own_half, k, None, back_send, back_receive).wait_recv()
+        onward(chip_after(k)).start()
+    for k in ORDER:
+        chip_copy(ready, own_half, k, None, back_send, back_receive).wait_send()
+    for slot in range(chips):
+        copy = onward(slot)
         copy.wait_send()
         copy.wait_recv()
-
-
-def carry_stage(group, pairs):
-    chips, rows, width = pairs.shape
-    shape = (chips, rows, width - LANES)
+    for copy in swaps:
+        copy.wait_send()
+    swaps[2].wait_recv()
+
+
+def carry_stage(group, *operands):
+    chips, rows, width = STATE // group, 2 * group, INNER // 2
+    wide = jax.ShapeDtypeStruct((ROWS, INNER), F32)
+    both = jax.ShapeDtypeStruct((2, chips, rows, width), F32)
     in_vmem = pl.BlockSpec(memory_space=pltpu.VMEM)
+    dma = pltpu.SemaphoreType.DMA((chips,))
+    three = pltpu.SemaphoreType.DMA((3,))
+    half = pltpu.VMEM((chips, rows, width), F32)
+    more = pltpu.VMEM((chips, rows, width + LANES), F32)
+    square = pltpu.VMEM((ROWS, ROWS), F32)
+    lhs = pltpu.VMEM((2 * STATE, 2 * ROWS), BF16)
+    shapes = (
+        both, both, wide, wide,
+        jax.ShapeDtypeStruct((ROWS, ROWS), F32),
+        jax.ShapeDtypeStruct((ROWS, 2 * STATE), F32),
+        jax.ShapeDtypeStruct((8, LANES), F32),
+    )
     return pl.pallas_call(
         functools.partial(carry_kernel, group),
-        in_specs=[in_vmem],
-        out_specs=in_vmem,
-        out_shape=jax.ShapeDtypeStruct(shape, F32),
+        in_specs=[in_vmem] * len(operands),
+        out_specs=[in_vmem] * len(shapes),
+        out_shape=shapes,
         scratch_shapes=[
-            pltpu.VMEM(shape, F32), pltpu.VMEM((chips, shape[2]), F32),
-            pltpu.SemaphoreType.DMA((chips,)), pltpu.SemaphoreType.DMA((chips,)),
+            half, half, more, more, half, pltpu.VMEM((chips, width), F32), square, square, lhs, lhs,
+            dma, dma, dma, dma, dma, dma, three, three,
         ],
-        compiler_params=pltpu.CompilerParams(vmem_limit_bytes=24 << 20, collective_id=2, has_side_effects=True),
+        compiler_params=pltpu.CompilerParams(vmem_limit_bytes=CARRY_BYTES, collective_id=2, has_side_effects=True),
         name="carry",
-    )(pairs)
+    )(*operands)
 
 
 def conv_backward(grad, shifted, taps, valid):
@@ -468,16 +498,12 @@
     return total, jnp.concatenate(parts, axis=0)
 
 
-def finish_kernel(group, final, half_ref, x_ref, tail_ref, taps_ref, xs_ref, tails_ref, tapss_ref, valid_ref, cot_ref, both_ref,
-                  out_in_ref, grad_in_ref, chip_ref, local_ref, bc_ref, small_ref, own_ref, partner_ref, *refs):
-    if final:
-        score_grad_ref, run_ref, dt_ref, sig_ref, sigsum_ref = refs[:5]
-        bc_before, head_before, token_before = refs[5:8]
-        out_ref, grad_ref, end_ref, borrowed_ref, taps_grad_ref = refs[13:18]
-        grads_ref, ends_ref, borroweds_ref, tapss_grad_ref, heads_ref = refs[18:23]
-        lhs_hi, lhs_lo, bc_grad, by_head, by_token = refs[23:]
-    else:
-        out_ref, grad_ref, end_ref, borrowed_ref, taps_grad_ref, bc_grad, by_head, by_token, lhs_hi, lhs_lo = refs
+def finish_kernel(group, half_ref, x_ref, tail_ref, taps_ref, xs_ref, tails_ref, tapss_ref, valid_ref, cot_ref, both_ref,
+                  out_in_ref, grad_in_ref, chip_ref, local_ref, bc_ref, small_ref, own_ref, partner_ref, score_grad_ref,
+                  run_ref, dt_ref, sig_ref, sigsum_ref,
+                  out_ref, grad_ref, end_ref, borrowed_ref, taps_grad_ref, grads_ref, ends_ref, borroweds_ref,
+                  tapss_grad_ref, heads_ref,
+                  lhs_hi, lhs_lo, bc_grad, by_head, by_token):
     tile = pl.program_id(0)
     valid = valid_ref[...]
 
@@ -488,14 +514,9 @@
             first, second = halves(bc_ref[:, source : source + STATE])
             lhs_hi[at : at + ROWS, :] = mm_nt(first, pick).astype(BF16)
             lhs_lo[at : at + ROWS, :] = mm_nt(second, pick).astype(BF16)
-        if final:
-            bc_grad[...] = bc_before[...]
-            by_head[...] = head_before[...]
-            by_token[...] = token_before[...]
-        else:
-            bc_grad[...] = jnp.zeros_like(bc_grad)
-            by_head[...] = jnp.zeros_like(by_head)
-            by_token[...] = jnp.zeros_like(by_token)
+        bc_grad[...] = jnp.zeros_like(bc_grad)
+        by_head[...] = jnp.zeros_like(by_head)
+        by_token[...] = jnp.zeros_like(by_token)
 
     total, shifted = convolve(tail_ref[...].astype(F32), x_ref[...].astype(F32), taps_ref[...], valid)
     gate = sigmoid(total)
@@ -507,8 +528,8 @@
     by_row = spread_exact(
         jnp.concatenate([own_ref[...], partner_ref[...], small_ref[...]], axis=0), head_columns(here)
     )
-    earlier, later = even_odd(half_ref, by_row)
     even = half_ref[2] == 0
+    earlier, later = even_odd(even, by_row)
     weight_state, weight_adjoint = jnp.where(even, 1.0, earlier), jnp.where(even, later, 1.0)
     with_state, with_adjoint = jnp.where(even, 0.0, 1.0), jnp.where(even, 1.0, 0.0)
     states = jnp.concatenate(
@@ -554,10 +575,7 @@
     grad_ref[...] = full[8:].astype(BF16)
     end_ref[...] = full[ROWS - 8 :]
 
-    if not final:
-        return
-
-    @pl.when(tile == HALF_TILES - 1)
+    @pl.when(tile == TILES - 1)
     def _():
         score_grad = score_grad_ref[...]
         keys, reads = bc_ref[:, :STATE], bc_ref[:, STATE:]
@@ -581,50 +599,40 @@
         heads_ref[...] = jnp.concatenate([bias_grad, alog_grad, by_head[2:3, :], jnp.zeros((5, LANES), F32)], axis=0)
 
 
-def finish_stage(group, half, operands, chip, local, bc, small, own, partner, last=None, before=None):
-    final = last is not None
+def finish_stage(group, half, *operands):
     square = whole((ROWS, LANES))
-    wide = (
+    eight = whole((8, LANES))
+    shapes = (
         jax.ShapeDtypeStruct((ROWS, INNER), BF16),
         jax.ShapeDtypeStruct((ROWS, INNER), BF16),
         jax.ShapeDtypeStruct((16, INNER), F32),
         jax.ShapeDtypeStruct((8, INNER), F32),
         jax.ShapeDtypeStruct((8, INNER), F32),
-    )
-    sums = (
-        jax.ShapeDtypeStruct((2 * ROWS, 2 * STATE), F32),
-        jax.ShapeDtypeStruct((8, LANES), F32),
-        jax.ShapeDtypeStruct((2 * ROWS, LANES), F32),
-    )
-    ends = (
         jax.ShapeDtypeStruct((ROWS, 2 * STATE), BF16),
         jax.ShapeDtypeStruct((16, 2 * STATE), F32),
         jax.ShapeDtypeStruct((8, 2 * STATE), F32),
         jax.ShapeDtypeStruct((8, 2 * STATE), F32),
         jax.ShapeDtypeStruct((8, LANES), F32),
     )
-    in_specs = [
-        tile_spec(ROWS), tile_spec(8), tile_spec(8),
-        small_spec(ROWS), small_spec(8), small_spec(8),
-        whole((ROWS, 8)), tile_spec(ROWS), whole((2 * ROWS, 2 * LANES)),
-        tile_spec(ROWS), tile_spec(ROWS), pair_spec(chip.shape, True), pair_spec(local.shape, True),
-        whole((ROWS, 2 * STATE)), whole((8, LANES)), whole((8, LANES)), whole((8, LANES)),
-    ]
-    given = tuple(operands) + (chip, local, bc, small, own, partner)
-    lhs = [pltpu.VMEM((2 * ROWS, 2 * STATE), BF16)] * 2
-    aliases = {}
-    if final:
-        in_specs += [whole((ROWS, ROWS)), square, square, square, square]
-        in_specs += [whole(part.shape) for part in sums] + [pl.BlockSpec(memory_space=pl.ANY)] * len(wide)
-        aliases = {1 + len(given) + len(last) + len(sums) + at: at for at in range(len(wide))}
-        given += tuple(last) + tuple(before[len(wide):]) + tuple(before[: len(wide)])
-        rest, scratch = ends, lhs + [pltpu.VMEM(part.shape, F32) for part in sums]
-    else:
-        rest, scratch = sums, lhs
+    states = pl.BlockSpec(
+        (None, STATE // group, 2 * group, TILE), lambda i, half: (i // HALF_TILES, 0, 0, lax.rem(i, HALF_TILES))
+    )
     return call(
-        functools.partial(finish_kernel, group, final), "finish_second" if final else "finish_first", half, HALF_TILES,
-        in_specs, [tile_spec(part.shape[0]) for part in wide] + [whole(part.shape) for part in rest], wide + rest,
-        scratch, given, aliases,
+        functools.partial(finish_kernel, group), "finish", half, TILES,
+        [
+            tile_spec(ROWS), tile_spec(8), tile_spec(8),
+            small_spec(ROWS), small_spec(8), small_spec(8),
+            whole((ROWS, 8)), tile_spec(ROWS), whole((2 * ROWS, 2 * LANES)),
+            tile_spec(ROWS), tile_spec(ROWS), states, states,
+            whole((ROWS, 2 * STATE)), eight, eight, eight, whole((ROWS, ROWS)), square, square, square, square,
+        ],
+        [tile_spec(part.shape[0]) for part in shapes[:5]] + [whole(part.shape) for part in shapes[5:]],
+        shapes,
+        [
+            pltpu.VMEM((2 * ROWS, 2 * STATE), BF16), pltpu.VMEM((2 * ROWS, 2 * STATE), BF16),
+            pltpu.VMEM((2 * ROWS, 2 * STATE), F32), pltpu.VMEM((8, LANES), F32), pltpu.VMEM((2 * ROWS, LANES), F32),
+        ],
+        operands,
     )
 
 
@@ -776,43 +784,21 @@
     )(*operands)
 
 
-def swap(array):
-    return lax.ppermute(array, "seq", [(i, i ^ 1) for i in range(lax.axis_size("seq"))])
-
-
-def between_chips(array):
-    size = lax.axis_size("seq")
-    groups = [list(range(0, size, 2)), list(range(1, size, 2))]
-    return lax.all_to_all(array, "seq", 0, 0, axis_index_groups=groups, tiled=True)
-
-
 def on_device(conv_input, doc_start, conv_weight, conv_bias, dt_raw, dt_bias, a_log, skip_gain, cotangent):
     shards, place = lax.axis_size("seq"), lax.axis_index("seq")
     group = 2 * STATE // shards
     core = lax.rem(place, 2)
     half = jnp.stack([core, place // 2, core])
-    other_half = jnp.stack([1 - core, place // 2, core])
     run, runT, dt, dtT, both, sig, sigsum, mask, valid, keep, tail, own, small, taps = head_stage(
         dt_raw.T, dt_bias[None], a_log[None], skip_gain[None], doc_start[None], conv_weight, conv_bias[None], conv_input
     )
     tail = lax.ppermute(tail, "seq", [(i, i + 1) for i in range(shards - 1)])
-    partner = swap(own)
-    theirs, bc = local_stage(group, other_half, conv_input, tail, taps, valid, cotangent, both)
-    other = swap(theirs)
-    mine, _ = local_stage(group, half, conv_input, tail, taps, valid, cotangent, both)
-    other_second = swap(mine)
-    gathered = between_chips(join_stage(group, half, mine, other, own, partner))
-    out_in, grad_in, score_grad = within_stage(
-        half, conv_input, tail, taps, valid, cotangent, bc, run, runT, dt, dtT, mask
-    )
-    gathered, out_in, grad_in = lax.optimization_barrier((gathered, out_in, grad_in))
-    chip = carry_stage(group, gathered)
-    chip_second = swap(chip)
-    operands = (conv_input, tail, taps, conv_input, tail, taps, valid, cotangent, both, out_in, grad_in)
-    first = finish_stage(group, half, operands, chip, other, bc, small, own, partner)
+    chips, others, out_in, grad_in, score_grad, bc, partner = carry_stage(
+        group, conv_input, tail, taps, valid, cotangent, both, own, runT, dtT, mask
+    )
     out, grad, end, borrowed, taps_grad, grads, ends, borroweds, tapss_grad, heads = finish_stage(
-        group, other_half, operands, chip_second, other_second, bc, small, own, partner,
-        (score_grad, run, dt, sig, sigsum), first,
+        group, half, conv_input, tail, taps, conv_input, tail, taps, valid, cotangent, both, out_in, grad_in, chips,
+        others, bc, small, own, partner, score_grad, run, dt, sig, sigsum,
     )
     groups = lax.axis_size("dp")
     sums, last = total_stage(

time: 179 us -> 161 us (0.90)
  waiting for transfers between devices: 27 us -> 1.41 us
  Pallas kernels: 129 us -> 143 us
  starting transfers between devices: 15.4 us -> 4.59 us
  local copies, waits for them, and re-layouts: 4.98 us -> 10.1 us
    pallas_call x1, Pallas kernels: 35.6 us -> 89.7 us  [carry_stage(): pl.pallas_call(functools.partial(carry_kernel, group), in_specs=[in_vmem]...]
    pallas_call x6 -> x1, Pallas kernels: 64.9 us -> 24.4 us  [call(): pl.pallas_call(kernel, grid_spec=pltpu.PrefetchScalarGridSpec(num_scalar_...]
    all_to_all x1 -> x0, waiting for transfers between devices: 25.8 us -> none  [between_chips(): lax.all_to_all(array, 'seq', 0, 0, axis_index_groups=groups, tiled=True)]
    all_to_all x1 -> x0, starting transfers between devices: 8.45 us -> none  [between_chips(): lax.all_to_all(array, 'seq', 0, 0, axis_index_groups=groups, tiled=True)]
    unnamed x10 -> x28, local copies, waits for them, and re-layouts: 3.62 us -> 9.37 us
    pallas_call x1, Pallas kernels: 22.4 us -> 24.9 us  [total_stage(): pl.pallas_call(functools.partial(total_kernel, scale), in_specs=[in_vmem]...]
    ppermute x4 -> x0, starting transfers between devices: 2.39 us -> none  [swap(): lax.ppermute(array, 'seq', [(i, i ^ 1) for i in range(lax.axis_size('seq'...]
    pallas_call x1, Pallas kernels: 2.39 us -> 0.48 us  [head_stage(): pl.pallas_call(head_kernel, grid=(1,), in_specs=[whole(part.shape) for pa...]
  transfers between devices with their start and end apart: 6 -> 1, of which waited for: 2 -> 1; matrix products, arithmetic and copies ran while one was open for 1% -> 0% of each run, Pallas kernels for 40% -> 0%
where the time goes in v7:
time: 161 us; the launch traced here: 160 us
  Pallas kernels  143 us (89%)
  local copies, waits for them, and re-layouts  10.1 us (6%)
  starting transfers between devices  4.59 us (3%)
    pallas_call x1, Pallas kernels, carry_stage(): pl.pallas_call(functools.partial(carry_kernel, group), in_specs=[in_vmem]...  89.7 us
    pallas_call x1, Pallas kernels, total_stage(): pl.pallas_call(functools.partial(total_kernel, scale), in_specs=[in_vmem]...  24.9 us
    pallas_call x1, Pallas kernels, call(): pl.pallas_call(kernel, grid_spec=pltpu.PrefetchScalarGridSpec(num_scalar_...  24.4 us
    unnamed x28, local copies, waits for them, and re-layouts  9.37 us
    ppermute x1, starting transfers between devices, on_device(): tail = lax.ppermute(tail, 'seq', [(i, i + 1) for i in range(shards - 1)])  4.59 us
    pallas_call x1, Pallas kernels, layout_stage(): pl.pallas_call(layout_kernel, grid=(ROWS // rows,), in_specs=[whole(sums....  3.71 us
  transfers between devices with their start and end apart: 1, of which 1 were waited for; matrix products, arithmetic and copies ran while one was open for 0% of the time, Pallas kernels for 0%

profile of v7, /device:TPU:1, one launch (start us, length us, event | category | flops | bytes accessed | tf_op | source)
XLA Modules:
  0.0 160.2 jit_solution(1180044016036654739)
XLA Ops:
  0.6 0.8 broadcast_in_dim.19.bias_ref
  1.4 0.0 copy-start
  1.4 1.3 copy-done
  2.7 0.0 copy-start.7
  2.7 0.9 copy-done.7
  3.6 0.0 copy-start.9
  3.6 0.8 copy-done.9
  4.4 0.0 copy-start.10
  4.4 0.7 copy-done.10
  5.1 0.0 copy-start.11
  5.1 0.7 copy-done.11
  5.7 0.0 copy-start.12
  5.7 0.7 copy-done.12
  6.4 0.0 copy-start.13
  6.4 0.7 copy-done.13
  7.0 0.0 copy-start.1
  7.0 0.5 heads.1
  7.5 4.6 %collective-permute-start = (bf16[8,5376]{1,0:T(8,128)(2,1)S(1)}, bf16[8,5376]{1,0:T(8,128)(2,1)S(1)}, u32[]{:S(2)}, u32[]{:S(2)}) collective-permute-start(bf16[8,5376]{1,0:T(8,128)(2,1)S(1)} %get-tuple-element.46), channel_id=1, source_target_pairs={{0,1},{1,2},{2,3},{3,4},{4,5},{5,6},{6,7},{7,8},{8,9},{9,10},{10,1... | collective-permute-start | bytes 258056 | tf_op jit(solution)/shard_map/ppermute | solution.py:795
  12.1 0.1 pad_add_fusion.half_ref
  12.2 1.4 collective-permute-done.tail_ref.tails_ref
  13.6 0.0 copy-done.1
  13.6 0.0 copy-start.2
  13.6 1.3 copy-done.2
  14.9 0.0 copy-start.3
  14.9 89.7 %carry.1 = (f32[2,16,16,2560]{3,2,1,0:T(8,128)S(1)}, f32[2,16,16,2560]{3,2,1,0:T(8,128)S(1)}, f32[128,5120]{1,0:T(8,128)S(1)}, f32[128,5120]{1,0:T(8,128)S(1)}, ...) custom-call(bf16[128,5376]{1,0:T(8,128)(2,1)S(1)} %copy-done.1, ...), custom_call_target="tpu_custom_call" | custom-call | tf_op jit(solution)/shard_map/carry/pallas_call | solution.py:473
  104.7 0.0 copy-done.3
  104.7 24.4 %finish.1 = (bf16[128,5120]{1,0:T(8,128)(2,1)}, bf16[128,5120]{1,0:T(8,128)(2,1)S(1)}, f32[16,5120]{1,0:T(8,128)S(1)}, f32[8,5120]{1,0:T(8,128)S(1)}, f32[8,5120...) custom-call(s32[3]{0:T(128)S(1)} %pad_add_fusion.half_ref, ...), custom_call_target="tpu_custom_call" | custom-call | tf_op jit(solution)/shard_map/finish/pallas_call | solution.py:215
  129.1 0.0 copy-start.4
  129.1 1.1 copy-done.4
  130.2 0.0 copy-start.8
  130.2 24.9 %totals.1 = (f32[8,5504]{1,0:T(8,128)S(1)}, bf16[16,5376]{1,0:T(8,128)(2,1)S(1)}) custom-call(f32[8,5120]{1,0:T(8,128)S(1)} %get-tuple-element.67.taps_ref, f32[8,256]{1,0:T(8,128)S(1)} %get-tuple-element.68.small_ref, f32[8,128]{1,0:T(8,128)S(1)} %get-tuple-element.69.heads_ref, f32[8,5120]{1,0:T(8,128)S(1)} %get-tuple-element.70.borrowed_ref, ...), custom_call_target="tpu_custom_call" | custom-call | tf_op jit(solution)/shard_map/totals/pallas_call | solution.py:768
  155.1 0.0 copy-start.5
  155.2 0.7 copy-done.5
  155.8 0.0 copy-start.6
  155.8 0.7 copy-done.6
  156.5 0.0 copy-done.8
  156.5 3.7 %layout.1 = (f32[4,5376]{1,0:T(4,128)}, f32[5376]{0:T(1024)}, f32[80]{0:T(128)}, f32[80]{0:T(128)}, f32[80]{0:T(128)}, /*index=5*/bf16[128,5376]{1,0:T(8,128)(2,1)}) custom-call(f32[8,5504]{1,0:T(8,128)} %copy-done.5, bf16[16,5376]{1,0:T(8,128)(2,1)} %copy-done.6, bf16[128,5120]{1,0:T(8,128)(2,1)} %copy-done.4, bf16[128,256]{1,0:T(8,128)(2,1)} %copy-done.8), custom_call_target="tpu_custom_call" | custom-call | tf_op jit(solution)/shard_map/layout/pallas_call | solution.py:753
Async XLA Ops:
  1.4 1.3 copy-start
  2.7 0.9 copy-start.7
  3.6 0.8 copy-start.9
  4.4 0.7 copy-start.10
  5.1 0.7 copy-start.11
  5.7 0.7 copy-start.12
  6.4 0.7 copy-start.13
  7.0 6.6 %copy-start.1 = (bf16[128,5376]{1,0:T(8,128)(2,1)S(1)}, bf16[128,5376]{1,0:T(8,128)(2,1)}, u32[]{:S(2)}) copy-start(bf16[128,5376]{1,0:T(8,128)(2,1)} %xs_ref.1) | copy-start | bytes 4128772
  7.5 6.1 %collective-permute-start = (bf16[8,5376]{1,0:T(8,128)(2,1)S(1)}, bf16[8,5376]{1,0:T(8,128)(2,1)S(1)}, u32[]{:S(2)}, u32[]{:S(2)}) collective-permute-start(bf16[8,5376]{1,0:T(8,128)(2,1)S(1)} %get-tuple-element.46), channel_id=1, source_target_pairs={{0,1},{1,2},{2,3},{3,4},{4,5},{5,6},{6,7},{7,8},{8,9},{9,10},{10,1... | collective-permute-start | bytes 258056 | tf_op jit(solution)/shard_map/ppermute | solution.py:795
  13.6 1.3 copy-start.2
  14.9 89.7 %copy-start.3 = (bf16[128,5120]{1,0:T(8,128)(2,1)S(1)}, bf16[128,5120]{1,0:T(8,128)(2,1)}, u32[]{:S(2)}) copy-start(bf16[128,5120]{1,0:T(8,128)(2,1)} %cot_ref.3) | copy-start | bytes 3932164
  129.1 1.1 copy-start.4
  130.2 26.3 %copy-start.8 = (bf16[128,256]{1,0:T(8,128)(2,1)}, bf16[128,256]{1,0:T(8,128)(2,1)S(1)}, u32[]{:S(2)}) copy-start(bf16[128,256]{1,0:T(8,128)(2,1)S(1)} %get-tuple-element.78.grads_ref) | copy-start | bytes 196612
  155.1 0.7 copy-start.5
  155.8 0.7 copy-start.6

commit v8 on v7

--- a/solution.py
+++ b/solution.py
@@ -335,9 +335,12 @@
     other = chip_after(k)
     slot = other if slot is None else slot
     return pltpu.make_async_remote_copy(
-        src_ref=source.at[other], dst_ref=target.at[slot], send_sem=send.at[other], recv_sem=receive.at[slot],
+        src_ref=source(other), dst_ref=target(slot), send_sem=send.at[other], recv_sem=receive.at[slot],
         device_id=same_core(other), device_id_type=MESH,
     )
+
+
+PIECES = ((0, 2), (2, 5))
 
 
 def pair_copy(source, target, send, receive):
@@ -366,7 +369,7 @@
         group, x_ref[:, INNER:], tail_ref[:, INNER:], taps_ref[:, INNER:], valid_ref[...], bc_ref, lhs_hi, lhs_lo
     )
 
-    def local_half(half, target):
+    def local_piece(half, piece, target):
         def tile_step(at, carry):
             result = local_tile(
                 HALF_TILES * half + at, x_ref, tail_ref, taps_ref, valid_ref, cot_ref, both_ref, lhs_hi, lhs_lo
@@ -374,34 +377,70 @@
             target[:, :, pl.ds(pl.multiple_of(TILE * at, TILE), TILE)] = result.reshape(chips, 2 * group, TILE)
             return carry
 
-        lax.fori_loop(0, HALF_TILES, tile_step, 0)
-
-    local_half(1 - core, theirs_ref)
-    pl.semaphore_wait(barrier, len(ORDER) + 1)
-    swaps = [
-        pair_copy(theirs_ref, others_ref.at[0], pair_send.at[0], pair_receive.at[0]),
-        pair_copy(own_ref, partner_ref, pair_send.at[1], pair_receive.at[1]),
-        pair_copy(mine_ref, others_ref.at[1], pair_send.at[2], pair_receive.at[2]),
-    ]
-    swaps[0].start()
-    swaps[1].start()
-    local_half(core, mine_ref)
-    swaps[2].start()
-    swaps[0].wait_recv()
-    swaps[1].wait_recv()
-    rows = jnp.concatenate([own_ref[...], partner_ref[...]], axis=0)
-    for at in range(HALF_TILES):
-        lanes = slice(TILE * at, TILE * (at + 1))
-        earlier, later = even_odd(even, spread_exact(rows, head_columns(HALF_TILES * core + at)))
-        mine, other = mine_ref[:, :, lanes], others_ref[0, :, :, lanes]
-        first, second = jnp.where(even, mine, other), jnp.where(even, other, mine)
-        joined[:, :group, lanes] = later * first[:, :group] + second[:, :group]
-        joined[:, group:, lanes] = first[:, group:] + earlier * second[:, group:]
-    joined[:, :, INNER // 2 :] = jnp.broadcast_to(
-        (own_ref[0:1, :] * partner_ref[0:1, :])[None], joined.shape[:2] + (LANES,)
-    )
-    for k in ORDER:
-        chip_copy(joined, gathered, k, chip, send, receive).start()
+        lax.fori_loop(*PIECES[piece], tile_step, 0)
+
+    def lanes_of(piece):
+        first, last = PIECES[piece]
+        return slice(TILE * first, TILE * last)
+
+    def sent_lanes(piece):
+        first, last = PIECES[piece]
+        return slice(0 if piece == 0 else LANES + TILE * first, LANES + TILE * last)
+
+    def swap(piece, source, at):
+        lanes, slot = lanes_of(piece), 2 * piece + at
+        return pair_copy(
+            source.at[:, :, lanes], others_ref.at[at, :, :, lanes], pair_send.at[slot], pair_receive.at[slot]
+        )
+
+    def out_copy(piece, k, slot):
+        lanes = sent_lanes(piece)
+        return chip_copy(
+            lambda at: joined.at[at, :, lanes], lambda at: gathered.at[at, :, lanes], k, slot, send.at[piece],
+            receive.at[piece],
+        )
+
+    def back_copy(piece, k, slot):
+        lanes = lanes_of(piece)
+        return chip_copy(
+            lambda at: ready.at[at, :, lanes], lambda at: chips_ref.at[0, at, :, lanes], k, slot, back_send.at[piece],
+            back_receive.at[piece],
+        )
+
+    def onward(piece, slot):
+        lanes = lanes_of(piece)
+        return pair_copy(
+            chips_ref.at[0, slot, :, lanes], chips_ref.at[1, slot, :, lanes], on_send.at[piece, slot],
+            on_receive.at[piece, slot],
+        )
+
+    pieces = range(len(PIECES))
+    own_decay = pair_copy(own_ref, partner_ref, pair_send.at[2 * len(PIECES)], pair_receive.at[2 * len(PIECES)])
+    for piece in pieces:
+        local_piece(1 - core, piece, theirs_ref)
+        if piece == 0:
+            pl.semaphore_wait(barrier, len(ORDER) + 1)
+            own_decay.start()
+        swap(piece, theirs_ref, 0).start()
+        local_piece(core, piece, mine_ref)
+        swap(piece, mine_ref, 1).start()
+        if piece == 0:
+            own_decay.wait_recv()
+            joined[:, :, :LANES] = jnp.broadcast_to(
+                (own_ref[0:1, :] * partner_ref[0:1, :])[None], joined.shape[:2] + (LANES,)
+            )
+        swap(piece, theirs_ref, 0).wait_recv()
+        rows = jnp.concatenate([own_ref[...], partner_ref[...]], axis=0)
+        for at in range(*PIECES[piece]):
+            lanes = slice(TILE * at, TILE * (at + 1))
+            target = slice(LANES + TILE * at, LANES + TILE * (at + 1))
+            earlier, later = even_odd(even, spread_exact(rows, head_columns(HALF_TILES * core + at)))
+            mine, other = mine_ref[:, :, lanes], others_ref[0, :, :, lanes]
+            first, second = jnp.where(even, mine, other), jnp.where(even, other, mine)
+            joined[:, :group, target] = later * first[:, :group] + second[:, :group]
+            joined[:, group:, target] = first[:, group:] + earlier * second[:, group:]
+        for k in ORDER:
+            out_copy(piece, k, chip).start()
     gathered[chip] = joined[chip]
 
     within_start(bc_ref, mask_ref, score_grad_ref, score, scoreT)
@@ -414,43 +453,43 @@
     lax.fori_loop(0, TILES, step, 0)
     score_grad_ref[...] = score_grad_ref[...] * mask_ref[0]
 
-    for k in ORDER:
-        copy = chip_copy(joined, gathered, k, None, send, receive)
-        copy.wait_send()
-        copy.wait_recv()
-    by_head = jnp.max(gathered[:, :, INNER // 2 :], axis=1)
-    for at in range(HALF_TILES):
-        lanes = slice(TILE * at, TILE * (at + 1))
-        decay[:, lanes] = spread_exact(by_head, head_columns(HALF_TILES * core + at))
-        state = jnp.zeros((group, TILE), F32)
-        adjoint = jnp.zeros((group, TILE), F32)
-        for here in range(chips):
-            ready[here, :group, lanes] = state
-            state = decay[here : here + 1, lanes] * state + gathered[here, :group, lanes]
-            back = chips - 1 - here
-            ready[back, group:, lanes] = adjoint
-            adjoint = decay[back : back + 1, lanes] * adjoint + gathered[back, group:, lanes]
-    own_half = chips_ref.at[0]
-    for k in ORDER:
-        chip_copy(ready, own_half, k, chip, back_send, back_receive).start()
-    chips_ref[0, chip] = ready[chip]
-
-    def onward(slot):
-        return pair_copy(chips_ref.at[0, slot], chips_ref.at[1, slot], on_send.at[slot], on_receive.at[slot])
-
-    onward(chip).start()
-    for k in ORDER:
-        chip_copy(ready, own_half, k, None, back_send, back_receive).wait_recv()
-        onward(chip_after(k)).start()
-    for k in ORDER:
-        chip_copy(ready, own_half, k, None, back_send, back_receive).wait_send()
-    for slot in range(chips):
-        copy = onward(slot)
-        copy.wait_send()
-        copy.wait_recv()
-    for copy in swaps:
-        copy.wait_send()
-    swaps[2].wait_recv()
+    for piece in pieces:
+        for k in ORDER:
+            out_copy(piece, k, None).wait_recv()
+        by_head = jnp.max(gathered[:, :, :LANES], axis=1)
+        for at in range(*PIECES[piece]):
+            lanes = slice(TILE * at, TILE * (at + 1))
+            source = slice(LANES + TILE * at, LANES + TILE * (at + 1))
+            decay[:, lanes] = spread_exact(by_head, head_columns(HALF_TILES * core + at))
+            state = jnp.zeros((group, TILE), F32)
+            adjoint = jnp.zeros((group, TILE), F32)
+            for here in range(chips):
+                ready[here, :group, lanes] = state
+                state = decay[here : here + 1, lanes] * state + gathered[here, :group, source]
+                back = chips - 1 - here
+                ready[back, group:, lanes] = adjoint
+                adjoint = decay[back : back + 1, lanes] * adjoint + gathered[back, group:, source]
+        for k in ORDER:
+            back_copy(piece, k, chip).start()
+        lanes = lanes_of(piece)
+        chips_ref[0, chip, :, lanes] = ready[chip, :, lanes]
+        onward(piece, chip).start()
+    for piece in pieces:
+        for k in ORDER:
+            back_copy(piece, k, None).wait_recv()
+            onward(piece, chip_after(k)).start()
+    for piece in pieces:
+        for k in ORDER:
+            out_copy(piece, k, None).wait_send()
+            back_copy(piece, k, None).wait_send()
+        for slot in range(chips):
+            copy = onward(piece, slot)
+            copy.wait_send()
+            copy.wait_recv()
+        swap(piece, theirs_ref, 0).wait_send()
+        swap(piece, mine_ref, 1).wait_send()
+        swap(piece, mine_ref, 1).wait_recv()
+    own_decay.wait_send()
 
 
 def carry_stage(group, *operands):
@@ -458,8 +497,8 @@
     wide = jax.ShapeDtypeStruct((ROWS, INNER), F32)
     both = jax.ShapeDtypeStruct((2, chips, rows, width), F32)
     in_vmem = pl.BlockSpec(memory_space=pltpu.VMEM)
-    dma = pltpu.SemaphoreType.DMA((chips,))
-    three = pltpu.SemaphoreType.DMA((3,))
+    dma = pltpu.SemaphoreType.DMA((len(PIECES), chips))
+    three = pltpu.SemaphoreType.DMA((2 * len(PIECES) + 1,))
     half = pltpu.VMEM((chips, rows, width), F32)
     more = pltpu.VMEM((chips, rows, width + LANES), F32)
     square = pltpu.VMEM((ROWS, ROWS), F32)
@@ -564,9 +603,9 @@
         ],
         axis=0,
     )
-    by_head[...] += lax.dot_general(
-        sums, one_hot.astype(F32), (((1,), (1,)), ((), ())), precision=EXACT, preferred_element_type=F32
-    )
+    first = sums.astype(BF16)
+    second, third = halves(sums - first.astype(F32))
+    by_head[...] += mm_nt(first, one_hot) + mm_nt(second, one_hot) + mm_nt(third, one_hot)
 
     act_grad = act_grad + gain * upstream
     conv_grad = act_grad * (gate + act * (1.0 - gate))

time: 161 us -> 146 us (0.907)
  Pallas kernels: 143 us -> 129 us
    pallas_call x1, Pallas kernels: 89.7 us -> 80.1 us  [carry_stage(): pl.pallas_call(functools.partial(carry_kernel, group), in_specs=[in_vmem]...]
    pallas_call x1, Pallas kernels: 24.9 us -> 21.3 us  [total_stage(): pl.pallas_call(functools.partial(total_kernel, scale), in_specs=[in_vmem]...]
where the time goes in v8:
time: 146 us
  Pallas kernels  129 us (88%)
  local copies, waits for them, and re-layouts  10.1 us (7%)
  starting transfers between devices  4.59 us (3%)
    pallas_call x1, Pallas kernels, carry_stage(): pl.pallas_call(functools.partial(carry_kernel, group), in_specs=[in_vmem]...  80.1 us
    pallas_call x1, Pallas kernels, call(): pl.pallas_call(kernel, grid_spec=pltpu.PrefetchScalarGridSpec(num_scalar_...  23.3 us
    pallas_call x1, Pallas kernels, total_stage(): pl.pallas_call(functools.partial(total_kernel, scale), in_specs=[in_vmem]...  21.3 us
    unnamed x28, local copies, waits for them, and re-layouts  9.37 us
    ppermute x1, starting transfers between devices, on_device(): tail = lax.ppermute(tail, 'seq', [(i, i + 1) for i in range(shards - 1)])  4.59 us
    pallas_call x1, Pallas kernels, layout_stage(): pl.pallas_call(layout_kernel, grid=(ROWS // rows,), in_specs=[whole(sums....  3.71 us
  transfers between devices with their start and end apart: 1, of which 1 were waited for; matrix products, arithmetic and copies ran while one was open for 0% of the time, Pallas kernels for 0%

profile of v8, /device:TPU:1, one launch (start us, length us, event | category | flops | bytes accessed | tf_op | source)
XLA Modules:
  0.0 145.8 jit_solution(5152755961912445196)
XLA Ops:
  0.6 0.8 broadcast_in_dim.19.bias_ref
  1.4 0.0 copy-start
  1.4 1.3 copy-done
  2.7 0.0 copy-start.7
  2.7 0.9 copy-done.7
  3.6 0.0 copy-start.9
  3.6 0.8 copy-done.9
  4.4 0.0 copy-start.10
  4.4 0.7 copy-done.10
  5.1 0.0 copy-start.11
  5.1 0.7 copy-done.11
  5.7 0.0 copy-start.12
  5.7 0.7 copy-done.12
  6.4 0.0 copy-start.13
  6.4 0.7 copy-done.13
  7.0 0.0 copy-start.1
  7.0 0.5 heads.1
  7.5 4.6 %collective-permute-start = (bf16[8,5376]{1,0:T(8,128)(2,1)S(1)}, bf16[8,5376]{1,0:T(8,128)(2,1)S(1)}, u32[]{:S(2)}, u32[]{:S(2)}) collective-permute-start(bf16[8,5376]{1,0:T(8,128)(2,1)S(1)} %get-tuple-element.46), channel_id=1, source_target_pairs={{0,1},{1,2},{2,3},{3,4},{4,5},{5,6},{6,7},{7,8},{8,9},{9,10},{10,1... | collective-permute-start | bytes 258056 | tf_op jit(solution)/shard_map/ppermute | solution.py:834
  12.1 0.1 pad_add_fusion.half_ref
  12.2 1.4 collective-permute-done.tail_ref.tails_ref
  13.6 0.0 copy-done.1
  13.6 0.0 copy-start.2
  13.6 1.3 copy-done.2
  14.9 0.0 copy-start.3
  14.9 80.1 %carry.1 = (f32[2,16,16,2560]{3,2,1,0:T(8,128)S(1)}, f32[2,16,16,2560]{3,2,1,0:T(8,128)S(1)}, f32[128,5120]{1,0:T(8,128)S(1)}, f32[128,5120]{1,0:T(8,128)S(1)}, ...) custom-call(bf16[128,5376]{1,0:T(8,128)(2,1)S(1)} %copy-done.1, ...), custom_call_target="tpu_custom_call" | custom-call | tf_op jit(solution)/shard_map/carry/pallas_call | solution.py:512
  95.0 0.0 copy-done.3
  95.0 23.3 %finish.1 = (bf16[128,5120]{1,0:T(8,128)(2,1)}, bf16[128,5120]{1,0:T(8,128)(2,1)S(1)}, f32[16,5120]{1,0:T(8,128)S(1)}, f32[8,5120]{1,0:T(8,128)S(1)}, f32[8,5120...) custom-call(s32[3]{0:T(128)S(1)} %pad_add_fusion.half_ref, ...), custom_call_target="tpu_custom_call" | custom-call | tf_op jit(solution)/shard_map/finish/pallas_call | solution.py:215
  118.4 0.0 copy-start.4
  118.4 1.1 copy-done.4
  119.5 0.0 copy-start.8
  119.5 21.3 %totals.1 = (f32[8,5504]{1,0:T(8,128)S(1)}, bf16[16,5376]{1,0:T(8,128)(2,1)S(1)}) custom-call(f32[8,5120]{1,0:T(8,128)S(1)} %get-tuple-element.67.taps_ref, f32[8,256]{1,0:T(8,128)S(1)} %get-tuple-element.68.small_ref, f32[8,128]{1,0:T(8,128)S(1)} %get-tuple-element.69.heads_ref, f32[8,5120]{1,0:T(8,128)S(1)} %get-tuple-element.70.borrowed_ref, ...), custom_call_target="tpu_custom_call" | custom-call | tf_op jit(solution)/shard_map/totals/pallas_call | solution.py:807
  140.8 0.0 copy-start.5
  140.8 0.7 copy-done.5
  141.5 0.0 copy-start.6
  141.5 0.7 copy-done.6
  142.1 0.0 copy-done.8
  142.1 3.7 %layout.1 = (f32[4,5376]{1,0:T(4,128)}, f32[5376]{0:T(1024)}, f32[80]{0:T(128)}, f32[80]{0:T(128)}, f32[80]{0:T(128)}, /*index=5*/bf16[128,5376]{1,0:T(8,128)(2,1)}) custom-call(f32[8,5504]{1,0:T(8,128)} %copy-done.5, bf16[16,5376]{1,0:T(8,128)(2,1)} %copy-done.6, bf16[128,5120]{1,0:T(8,128)(2,1)} %copy-done.4, bf16[128,256]{1,0:T(8,128)(2,1)} %copy-done.8), custom_call_target="tpu_custom_call" | custom-call | tf_op jit(solution)/shard_map/layout/pallas_call | solution.py:792
Async XLA Ops:
  1.4 1.3 copy-start
  2.7 0.9 copy-start.7
  3.6 0.8 copy-start.9
  4.4 0.7 copy-start.10
  5.1 0.7 copy-start.11
  5.7 0.7 copy-start.12
  6.4 0.7 copy-start.13
  7.0 6.6 %copy-start.1 = (bf16[128,5376]{1,0:T(8,128)(2,1)S(1)}, bf16[128,5376]{1,0:T(8,128)(2,1)}, u32[]{:S(2)}) copy-start(bf16[128,5376]{1,0:T(8,128)(2,1)} %xs_ref.1) | copy-start | bytes 4128772
  7.5 6.1 %collective-permute-start = (bf16[8,5376]{1,0:T(8,128)(2,1)S(1)}, bf16[8,5376]{1,0:T(8,128)(2,1)S(1)}, u32[]{:S(2)}, u32[]{:S(2)}) collective-permute-start(bf16[8,5376]{1,0:T(8,128)(2,1)S(1)} %get-tuple-element.46), channel_id=1, source_target_pairs={{0,1},{1,2},{2,3},{3,4},{4,5},{5,6},{6,7},{7,8},{8,9},{9,10},{10,1... | collective-permute-start | bytes 258056 | tf_op jit(solution)/shard_map/ppermute | solution.py:834
  13.6 1.3 copy-start.2
  14.9 80.1 %copy-start.3 = (bf16[128,5120]{1,0:T(8,128)(2,1)S(1)}, bf16[128,5120]{1,0:T(8,128)(2,1)}, u32[]{:S(2)}) copy-start(bf16[128,5120]{1,0:T(8,128)(2,1)} %cot_ref.3) | copy-start | bytes 3932164
  118.4 1.1 copy-start.4
  119.5 22.7 %copy-start.8 = (bf16[128,256]{1,0:T(8,128)(2,1)}, bf16[128,256]{1,0:T(8,128)(2,1)S(1)}, u32[]{:S(2)}) copy-start(bf16[128,256]{1,0:T(8,128)(2,1)S(1)} %get-tuple-element.78.grads_ref) | copy-start | bytes 196612
  140.8 0.7 copy-start.5
  141.5 0.7 copy-start.6

commit v9 on v8

--- a/solution.py
+++ b/solution.py
@@ -340,7 +340,7 @@
     )
 
 
-PIECES = ((0, 2), (2, 5))
+PIECES = ((0, 1), (1, 3), (3, 5))
 
 
 def pair_copy(source, target, send, receive):

time: 146 us -> 141 us (0.966)
  Pallas kernels: 129 us -> 124 us
    pallas_call x1, Pallas kernels: 80.1 us -> 75.3 us  [carry_stage(): pl.pallas_call(functools.partial(carry_kernel, group), in_specs=[in_vmem]...]
where the time goes in v9:
time: 141 us
  Pallas kernels  124 us (88%)
  local copies, waits for them, and re-layouts  10.1 us (7%)
  starting transfers between devices  4.59 us (3%)
  waiting for transfers between devices  1.41 us (1%)
    pallas_call x1, Pallas kernels, carry_stage(): pl.pallas_call(functools.partial(carry_kernel, group), in_specs=[in_vmem]...  75.3 us
    pallas_call x1, Pallas kernels, call(): pl.pallas_call(kernel, grid_spec=pltpu.PrefetchScalarGridSpec(num_scalar_...  23.3 us
    pallas_call x1, Pallas kernels, total_stage(): pl.pallas_call(functools.partial(total_kernel, scale), in_specs=[in_vmem]...  21 us
    unnamed x28, local copies, waits for them, and re-layouts  9.37 us
    ppermute x1, starting transfers between devices, on_device(): tail = lax.ppermute(tail, 'seq', [(i, i + 1) for i in range(shards - 1)])  4.59 us
    pallas_call x1, Pallas kernels, layout_stage(): pl.pallas_call(layout_kernel, grid=(ROWS // rows,), in_specs=[whole(sums....  3.71 us
  transfers between devices with their start and end apart: 1, of which 1 were waited for; matrix products, arithmetic and copies ran while one was open for 0% of the time, Pallas kernels for 0%

profile of v9, /device:TPU:1, one launch (start us, length us, event | category | flops | bytes accessed | tf_op | source)
XLA Modules:
  0.0 140.7 jit_solution(13331799975045297936)
XLA Ops:
  0.6 0.8 broadcast_in_dim.19.bias_ref
  1.4 0.0 copy-start
  1.4 1.3 copy-done
  2.7 0.0 copy-start.7
  2.7 0.9 copy-done.7
  3.6 0.0 copy-start.9
  3.6 0.8 copy-done.9
  4.4 0.0 copy-start.10
  4.4 0.7 copy-done.10
  5.1 0.0 copy-start.11
  5.1 0.7 copy-done.11
  5.7 0.0 copy-start.12
  5.7 0.7 copy-done.12
  6.4 0.0 copy-start.13
  6.4 0.7 copy-done.13
  7.0 0.0 copy-start.1
  7.0 0.5 heads.1
  7.5 4.6 %collective-permute-start = (bf16[8,5376]{1,0:T(8,128)(2,1)S(1)}, bf16[8,5376]{1,0:T(8,128)(2,1)S(1)}, u32[]{:S(2)}, u32[]{:S(2)}) collective-permute-start(bf16[8,5376]{1,0:T(8,128)(2,1)S(1)} %get-tuple-element.46), channel_id=1, source_target_pairs={{0,1},{1,2},{2,3},{3,4},{4,5},{5,6},{6,7},{7,8},{8,9},{9,10},{10,1... | collective-permute-start | bytes 258056 | tf_op jit(solution)/shard_map/ppermute | solution.py:834
  12.1 0.1 pad_add_fusion.half_ref
  12.2 1.4 %collective-permute-done.tail_ref.tails_ref = bf16[8,5376]{1,0:T(8,128)(2,1)S(1)} collective-permute-done((bf16[8,5376]{1,0:T(8,128)(2,1)S(1)}, bf16[8,5376]{1,0:T(8,128)(2,1)S(1)}, u32[]{:S(2)}, u32[]{:S(2)}) %collective-permute-start) | collective-permute-done | bytes 86048 | tf_op jit(solution)/shard_map/ppermute | solution.py:834
  13.6 0.0 copy-done.1
  13.6 0.0 copy-start.2
  13.6 1.3 copy-done.2
  14.9 0.0 copy-start.3
  14.9 75.3 %carry.1 = (f32[2,16,16,2560]{3,2,1,0:T(8,128)S(1)}, f32[2,16,16,2560]{3,2,1,0:T(8,128)S(1)}, f32[128,5120]{1,0:T(8,128)S(1)}, f32[128,5120]{1,0:T(8,128)S(1)}, ...) custom-call(bf16[128,5376]{1,0:T(8,128)(2,1)S(1)} %copy-done.1, ...), custom_call_target="tpu_custom_call" | custom-call | tf_op jit(solution)/shard_map/carry/pallas_call | solution.py:512
  90.2 0.0 copy-done.3
  90.2 23.3 %finish.1 = (bf16[128,5120]{1,0:T(8,128)(2,1)}, bf16[128,5120]{1,0:T(8,128)(2,1)S(1)}, f32[16,5120]{1,0:T(8,128)S(1)}, f32[8,5120]{1,0:T(8,128)S(1)}, f32[8,5120...) custom-call(s32[3]{0:T(128)S(1)} %pad_add_fusion.half_ref, ...), custom_call_target="tpu_custom_call" | custom-call | tf_op jit(solution)/shard_map/finish/pallas_call | solution.py:215
  113.6 0.0 copy-start.4
  113.6 1.1 copy-done.4
  114.6 0.0 copy-start.8
  114.6 21.0 %totals.1 = (f32[8,5504]{1,0:T(8,128)S(1)}, bf16[16,5376]{1,0:T(8,128)(2,1)S(1)}) custom-call(f32[8,5120]{1,0:T(8,128)S(1)} %get-tuple-element.67.taps_ref, f32[8,256]{1,0:T(8,128)S(1)} %get-tuple-element.68.small_ref, f32[8,128]{1,0:T(8,128)S(1)} %get-tuple-element.69.heads_ref, f32[8,5120]{1,0:T(8,128)S(1)} %get-tuple-element.70.borrowed_ref, ...), custom_call_target="tpu_custom_call" | custom-call | tf_op jit(solution)/shard_map/totals/pallas_call | solution.py:807
  135.6 0.0 copy-start.5
  135.6 0.7 copy-done.5
  136.3 0.0 copy-start.6
  136.3 0.7 copy-done.6
  137.0 0.0 copy-done.8
  137.0 3.7 %layout.1 = (f32[4,5376]{1,0:T(4,128)}, f32[5376]{0:T(1024)}, f32[80]{0:T(128)}, f32[80]{0:T(128)}, f32[80]{0:T(128)}, /*index=5*/bf16[128,5376]{1,0:T(8,128)(2,1)}) custom-call(f32[8,5504]{1,0:T(8,128)} %copy-done.5, bf16[16,5376]{1,0:T(8,128)(2,1)} %copy-done.6, bf16[128,5120]{1,0:T(8,128)(2,1)} %copy-done.4, bf16[128,256]{1,0:T(8,128)(2,1)} %copy-done.8), custom_call_target="tpu_custom_call" | custom-call | tf_op jit(solution)/shard_map/layout/pallas_call | solution.py:792
Async XLA Ops:
  1.4 1.3 copy-start
  2.7 0.9 copy-start.7
  3.6 0.8 copy-start.9
  4.4 0.7 copy-start.10
  5.1 0.7 copy-start.11
  5.7 0.7 copy-start.12
  6.4 0.7 copy-start.13
  7.0 6.6 %copy-start.1 = (bf16[128,5376]{1,0:T(8,128)(2,1)S(1)}, bf16[128,5376]{1,0:T(8,128)(2,1)}, u32[]{:S(2)}) copy-start(bf16[128,5376]{1,0:T(8,128)(2,1)} %xs_ref.1) | copy-start | bytes 4128772
  7.5 6.1 %collective-permute-start = (bf16[8,5376]{1,0:T(8,128)(2,1)S(1)}, bf16[8,5376]{1,0:T(8,128)(2,1)S(1)}, u32[]{:S(2)}, u32[]{:S(2)}) collective-permute-start(bf16[8,5376]{1,0:T(8,128)(2,1)S(1)} %get-tuple-element.46), channel_id=1, source_target_pairs={{0,1},{1,2},{2,3},{3,4},{4,5},{5,6},{6,7},{7,8},{8,9},{9,10},{10,1... | collective-permute-start | bytes 258056 | tf_op jit(solution)/shard_map/ppermute | solution.py:834
  13.6 1.3 copy-start.2
  14.9 75.3 %copy-start.3 = (bf16[128,5120]{1,0:T(8,128)(2,1)S(1)}, bf16[128,5120]{1,0:T(8,128)(2,1)}, u32[]{:S(2)}) copy-start(bf16[128,5120]{1,0:T(8,128)(2,1)} %cot_ref.3) | copy-start | bytes 3932164
  113.6 1.1 copy-start.4
  114.6 22.3 %copy-start.8 = (bf16[128,256]{1,0:T(8,128)(2,1)}, bf16[128,256]{1,0:T(8,128)(2,1)S(1)}, u32[]{:S(2)}) copy-start(bf16[128,256]{1,0:T(8,128)(2,1)S(1)} %get-tuple-element.78.grads_ref) | copy-start | bytes 196612
  135.6 0.7 copy-start.5
  136.3 0.7 copy-start.6

commit v10 on v9

--- a/solution.py
+++ b/solution.py
@@ -125,14 +125,13 @@
         copy.wait_recv()
 
 
-def head_kernel(raw_in_ref, dt_bias_ref, a_log_ref, gain_ref, row_ref, weight_ref, bias_ref, end_ref, run_ref, runT_ref,
+def head_kernel(raw_in_ref, heads_in_ref, row_ref, weight_ref, bias_ref, end_ref, run_ref, runT_ref,
                 dt_ref, dtT_ref, both_ref, sig_ref, sigsum_ref, mask_ref, valid_ref, keep_ref, tail_ref, own_ref,
                 small_ref, taps_ref, raw):
     taps_ref[:CONV, :] = weight_ref[...]
     taps_ref[CONV:, :] = jnp.broadcast_to(bias_ref[...], (8 - CONV, CH))
     small_ref[...] = jnp.zeros_like(small_ref)
-    for at, source in enumerate((dt_bias_ref, a_log_ref, gain_ref)):
-        small_ref[at : at + 1, :HEADS] = source[...]
+    small_ref[:3, :HEADS] = heads_in_ref[...]
     reset_row = row_ref[...].astype(F32)
     token, other = iota((ROWS, ROWS), 0), iota((ROWS, ROWS), 1)
     reset_col = jnp.sum(jnp.where(token == other, reset_row, 0.0), axis=1, keepdims=True)
@@ -180,7 +179,7 @@
         both_ref[at : at + ROWS, LANES:] = second
 
 
-def head_stage(raw, dt_bias, a_log, gain, row, weight, bias, conv_input):
+def head_stage(raw, heads_in, row, weight, bias, conv_input):
     square = jax.ShapeDtypeStruct((ROWS, LANES), F32)
     eight = jax.ShapeDtypeStruct((8, LANES), F32)
     shapes = (
@@ -194,7 +193,7 @@
         eight, eight,
         jax.ShapeDtypeStruct((8, CH), F32),
     )
-    given = (raw, dt_bias, a_log, gain, row, weight, bias)
+    given = (raw, heads_in, row, weight, bias)
     return pl.pallas_call(
         head_kernel,
         grid=(1,),
@@ -829,7 +828,7 @@
     core = lax.rem(place, 2)
     half = jnp.stack([core, place // 2, core])
     run, runT, dt, dtT, both, sig, sigsum, mask, valid, keep, tail, own, small, taps = head_stage(
-        dt_raw.T, dt_bias[None], a_log[None], skip_gain[None], doc_start[None], conv_weight, conv_bias[None], conv_input
+        dt_raw.T, jnp.stack([dt_bias, a_log, skip_gain]), doc_start[None], conv_weight, conv_bias[None], conv_input
     )
     tail = lax.ppermute(tail, "seq", [(i, i + 1) for i in range(shards - 1)])
     chips, others, out_in, grad_in, score_grad, bc, partner = carry_stage(

time: 141 us -> 140 us (level)
  local copies, waits for them, and re-layouts: 10.1 us -> 8.12 us
    unnamed x28 -> x22, local copies, waits for them, and re-layouts: 9.37 us -> 7.37 us
where the time goes in v10:
time: 140 us; the launch traced here: 139 us
  Pallas kernels  124 us (89%)
  local copies, waits for them, and re-layouts  8.12 us (6%)
  starting transfers between devices  4.6 us (3%)
  waiting for transfers between devices  1.41 us (1%)
    pallas_call x1, Pallas kernels, carry_stage(): pl.pallas_call(functools.partial(carry_kernel, group), in_specs=[in_vmem]...  75.3 us
    pallas_call x1, Pallas kernels, call(): pl.pallas_call(kernel, grid_spec=pltpu.PrefetchScalarGridSpec(num_scalar_...  23.3 us
    pallas_call x1, Pallas kernels, total_stage(): pl.pallas_call(functools.partial(total_kernel, scale), in_specs=[in_vmem]...  20.8 us
    unnamed x22, local copies, waits for them, and re-layouts  7.37 us
    ppermute x1, starting transfers between devices, on_device(): tail = lax.ppermute(tail, 'seq', [(i, i + 1) for i in range(shards - 1)])  4.6 us
    pallas_call x1, Pallas kernels, layout_stage(): pl.pallas_call(layout_kernel, grid=(ROWS // rows,), in_specs=[whole(sums....  3.71 us
  transfers between devices with their start and end apart: 1, of which 1 were waited for; matrix products, arithmetic and copies ran while one was open for 0% of the time, Pallas kernels for 0%

profile of v10, /device:TPU:1, one launch (start us, length us, event | category | flops | bytes accessed | tf_op | source)
XLA Modules:
  0.0 139.2 jit_solution(6538043437103241520)
XLA Ops:
  0.6 0.8 broadcast_in_dim.7.bias_ref
  1.4 0.7 pad_maximum_fusion.heads_in_ref
  2.1 0.0 copy-start
  2.1 1.3 copy-done
  3.4 0.0 copy-start.7
  3.4 0.9 copy-done.7
  4.3 0.0 copy-start.9
  4.3 0.8 copy-done.9
  5.1 0.0 copy-start.10
  5.1 0.7 copy-done.10
  5.8 0.0 copy-start.1
  5.8 0.5 heads.1
  6.2 4.6 %collective-permute-start = (bf16[8,5376]{1,0:T(8,128)(2,1)S(1)}, bf16[8,5376]{1,0:T(8,128)(2,1)S(1)}, u32[]{:S(2)}, u32[]{:S(2)}) collective-permute-start(bf16[8,5376]{1,0:T(8,128)(2,1)S(1)} %get-tuple-element.46), channel_id=1, source_target_pairs={{0,1},{1,2},{2,3},{3,4},{4,5},{5,6},{6,7},{7,8},{8,9},{9,10},{10,1... | collective-permute-start | bytes 258056 | tf_op jit(solution)/shard_map/ppermute | solution.py:833
  10.8 0.1 pad_add_fusion.half_ref
  10.9 1.4 %collective-permute-done.tail_ref.tails_ref = bf16[8,5376]{1,0:T(8,128)(2,1)S(1)} collective-permute-done((bf16[8,5376]{1,0:T(8,128)(2,1)S(1)}, bf16[8,5376]{1,0:T(8,128)(2,1)S(1)}, u32[]{:S(2)}, u32[]{:S(2)}) %collective-permute-start) | collective-permute-done | bytes 86048 | tf_op jit(solution)/shard_map/ppermute | solution.py:833
  12.3 0.0 copy-done.1
  12.3 0.0 copy-start.2
  12.3 1.3 copy-done.2
  13.7 0.0 copy-start.3
  13.7 75.3 %carry.1 = (f32[2,16,16,2560]{3,2,1,0:T(8,128)S(1)}, f32[2,16,16,2560]{3,2,1,0:T(8,128)S(1)}, f32[128,5120]{1,0:T(8,128)S(1)}, f32[128,5120]{1,0:T(8,128)S(1)}, ...) custom-call(bf16[128,5376]{1,0:T(8,128)(2,1)S(1)} %copy-done.1, ...), custom_call_target="tpu_custom_call" | custom-call | tf_op jit(solution)/shard_map/carry/pallas_call | solution.py:511
  89.0 0.0 copy-done.3
  89.0 23.3 %finish.1 = (bf16[128,5120]{1,0:T(8,128)(2,1)}, bf16[128,5120]{1,0:T(8,128)(2,1)S(1)}, f32[16,5120]{1,0:T(8,128)S(1)}, f32[8,5120]{1,0:T(8,128)S(1)}, f32[8,5120...) custom-call(s32[3]{0:T(128)S(1)} %pad_add_fusion.half_ref, ...), custom_call_target="tpu_custom_call" | custom-call | tf_op jit(solution)/shard_map/finish/pallas_call | solution.py:214
  112.3 0.0 copy-start.4
  112.3 1.1 copy-done.4
  113.4 0.0 copy-start.8
  113.4 20.8 %totals.1 = (f32[8,5504]{1,0:T(8,128)S(1)}, bf16[16,5376]{1,0:T(8,128)(2,1)S(1)}) custom-call(f32[8,5120]{1,0:T(8,128)S(1)} %get-tuple-element.67.taps_ref, f32[8,256]{1,0:T(8,128)S(1)} %get-tuple-element.68.small_ref, f32[8,128]{1,0:T(8,128)S(1)} %get-tuple-element.69.heads_ref, f32[8,5120]{1,0:T(8,128)S(1)} %get-tuple-element.70.borrowed_ref, ...), custom_call_target="tpu_custom_call" | custom-call | tf_op jit(solution)/shard_map/totals/pallas_call | solution.py:806
  134.2 0.0 copy-start.5
  134.2 0.7 copy-done.5
  134.8 0.0 copy-start.6
  134.8 0.7 copy-done.6
  135.5 0.0 copy-done.8
  135.5 3.7 %layout.1 = (f32[4,5376]{1,0:T(4,128)}, f32[5376]{0:T(1024)}, f32[80]{0:T(128)}, f32[80]{0:T(128)}, f32[80]{0:T(128)}, /*index=5*/bf16[128,5376]{1,0:T(8,128)(2,1)}) custom-call(f32[8,5504]{1,0:T(8,128)} %copy-done.5, bf16[16,5376]{1,0:T(8,128)(2,1)} %copy-done.6, bf16[128,5120]{1,0:T(8,128)(2,1)} %copy-done.4, bf16[128,256]{1,0:T(8,128)(2,1)} %copy-done.8), custom_call_target="tpu_custom_call" | custom-call | tf_op jit(solution)/shard_map/layout/pallas_call | solution.py:791
Async XLA Ops:
  2.1 1.3 copy-start
  3.4 0.9 copy-start.7
  4.3 0.8 copy-start.9
  5.1 0.7 copy-start.10
  5.8 6.6 %copy-start.1 = (bf16[128,5376]{1,0:T(8,128)(2,1)S(1)}, bf16[128,5376]{1,0:T(8,128)(2,1)}, u32[]{:S(2)}) copy-start(bf16[128,5376]{1,0:T(8,128)(2,1)} %xs_ref.1) | copy-start | bytes 4128772
  6.2 6.1 %collective-permute-start = (bf16[8,5376]{1,0:T(8,128)(2,1)S(1)}, bf16[8,5376]{1,0:T(8,128)(2,1)S(1)}, u32[]{:S(2)}, u32[]{:S(2)}) collective-permute-start(bf16[8,5376]{1,0:T(8,128)(2,1)S(1)} %get-tuple-element.46), channel_id=1, source_target_pairs={{0,1},{1,2},{2,3},{3,4},{4,5},{5,6},{6,7},{7,8},{8,9},{9,10},{10,1... | collective-permute-start | bytes 258056 | tf_op jit(solution)/shard_map/ppermute | solution.py:833
  12.3 1.3 copy-start.2
  13.7 75.3 %copy-start.3 = (bf16[128,5120]{1,0:T(8,128)(2,1)S(1)}, bf16[128,5120]{1,0:T(8,128)(2,1)}, u32[]{:S(2)}) copy-start(bf16[128,5120]{1,0:T(8,128)(2,1)} %cot_ref.3) | copy-start | bytes 3932164
  112.3 1.1 copy-start.4
  113.4 22.1 %copy-start.8 = (bf16[128,256]{1,0:T(8,128)(2,1)}, bf16[128,256]{1,0:T(8,128)(2,1)S(1)}, u32[]{:S(2)}) copy-start(bf16[128,256]{1,0:T(8,128)(2,1)S(1)} %get-tuple-element.78.grads_ref) | copy-start | bytes 196612
  134.2 0.7 copy-start.5
  134.8 0.7 copy-start.6
